TPU v7x, 32 devices: a whole 2x2x4 slice. The times are simulated.
32 devices in a mesh: dp: 2 (over x), uly: 4 (over z), blk: 4 (over y, core).
Axes of the slice: x: 2, y: 2, z: 4, core: 2. Of those that a mesh axis runs over, the one named last changes fastest.
Arguments:
- inputs: float32 [1, 4096, 768], P(None, ('dp', 'uly', 'blk')), may hold values from -6 to 6
- cotangent: float32 [1, 4096, 768], P(None, ('dp', 'uly', 'blk')), may hold values from -6 to 6
- qkv_weight: bfloat16 [768, 2304], P(('dp', 'blk')), may hold values from -0.21875 to 0.21875
- query_bias: bfloat16 [768], P(('dp', 'blk')), may hold values from -4 to 4
- value_bias: bfloat16 [768], P(('dp', 'blk')), may hold values from -0.75 to 0.75
- out_weight: bfloat16 [768, 768], P(('dp', 'blk')), may hold values from -3 to 3
- out_bias: bfloat16 [768], P(('dp', 'blk')), may hold values from -4 to 4
- norm1_gain: bfloat16 [768], P(('dp', 'blk')), may hold values from 0.099609375 to 1.8984375
- norm1_bias: bfloat16 [768], P(('dp', 'blk')), may hold values from -4 to 4
- norm2_gain: bfloat16 [768], P(('dp', 'blk')), may hold values from 0.099609375 to 1.8984375
- norm2_bias: bfloat16 [768], P(('dp', 'blk')), may hold values from -4 to 4
- up_weight: bfloat16 [768, 3072], P(('dp', 'blk')), may hold values from -0.21875 to 0.21875
- up_bias: bfloat16 [3072], P(('dp', 'blk')), may hold values from -4 to 4
- down_weight: bfloat16 [3072, 768], P(None, ('dp', 'blk')), may hold values from -0.109375 to 0.109375
- down_bias: bfloat16 [768], P(('dp', 'blk')), may hold values from -4 to 4
- doc_lengths: int32 [1, 2, 8], P(None, 'dp'), may hold values from 1 to 1024, 2048 in all within a row
- pad_mask: int32 [1, 4096], P(None, 'dp'), may hold values 0 or 1
Outputs:
- output: float32 [1, 4096, 768], P(None, ('dp', 'uly', 'blk'))
- grad_inputs: float32 [1, 4096, 768], P(None, ('dp', 'uly', 'blk'))
- grad_qkv_weight: float32 [768, 2304], P(('dp', 'blk'))
- grad_query_bias: float32 [768], P(('dp', 'blk'))
- grad_value_bias: float32 [768], P(('dp', 'blk'))
- grad_out_weight: float32 [768, 768], P(('dp', 'blk'))
- grad_out_bias: float32 [768], P(('dp', 'blk'))
- grad_norm1_gain: float32 [768], P(('dp', 'blk'))
- grad_norm1_bias: float32 [768], P(('dp', 'blk'))
- grad_norm2_gain: float32 [768], P(('dp', 'blk'))
- grad_norm2_bias: float32 [768], P(('dp', 'blk'))
- grad_up_weight: float32 [768, 3072], P(('dp', 'blk'))
- grad_up_bias: float32 [3072], P(('dp', 'blk'))
- grad_down_weight: float32 [3072, 768], P(None, ('dp', 'blk'))
- grad_down_bias: float32 [768], P(('dp', 'blk'))
Inputs may be any that keep to these rules, and one draw needn't show every extreme that they name: `doc_lengths`: the 8 lengths of a sequence sum to 2048; the longest document of every sequence has 1024 rows.
All inputs are finite; a program needn't handle non-finite values. No bound on the sum of `pad_mask` on one device may be relied on, other than what follows from the above.
Results may differ from a plain program's by a relative error of at most 0.025.
Values may be sent and summed in bfloat16 or wider, within the bound.
No kernel may reach another device: no remote copies, remote signals or barrier semaphores. Data moves between devices by JAX's collectives and lax.ppermute only.
A program may use at most 192 MiB of HBM per device.

v0:
```python
import functools

import jax
import jax.numpy as jnp
from jax import lax
from jax.experimental import pallas as pl
from jax.experimental.pallas import tpu as pltpu
from jax.sharding import PartitionSpec as P

HEADS = 12
HEAD_DIM = 64
FF = 3072
F32 = jnp.float32
BF16 = jnp.bfloat16
NEG = -1e30
VMEM_LIMIT = 60 * 1024 * 1024

ROWS = 128
ULY = 4
BLK = 4
GROUP = ROWS * ULY
KEYS = GROUP * BLK
WIDTH = HEADS * HEAD_DIM
HW = WIDTH // ULY
LOCAL_HEADS = HEADS // ULY
OWNERS = 8
OWN = WIDTH // OWNERS
PANEL = OWN + 16
QUART = FF // BLK
COST = 1


def swap(array, axis, by):
    peers = lax.axis_size(axis)
    return lax.ppermute(array, axis, [(i, i ^ by) for i in range(peers)])


def vm():
    return pl.BlockSpec(memory_space=pltpu.VMEM)


def anyspace():
    return pl.BlockSpec(memory_space=pl.ANY)


def smem():
    return pl.BlockSpec(memory_space=pltpu.SMEM)


def call(kernel, outs, args, scratch=(), flops=0, in_any=()):
    specs = [smem()] + [anyspace() if i in in_any else vm() for i in range(1, len(args))]
    nbytes = sum(a.size * a.dtype.itemsize for a in args) + sum(
        o.size * o.dtype.itemsize for o in outs
    )
    return pl.pallas_call(
        kernel,
        out_shape=outs,
        in_specs=specs,
        out_specs=[vm() for _ in outs],
        scratch_shapes=list(scratch),
        cost_estimate=pl.CostEstimate(
            flops=flops // COST, bytes_accessed=nbytes // COST, transcendentals=0
        ),
        compiler_params=pltpu.CompilerParams(vmem_limit_bytes=VMEM_LIMIT),
    )(*args)


def sds(shape, dtype):
    return jax.ShapeDtypeStruct(shape, dtype)


def nn(a, b):
    return lax.dot_general(a, b, (((1,), (0,)), ((), ())), preferred_element_type=F32)


def nt(a, b):
    return lax.dot_general(a, b, (((1,), (1,)), ((), ())), preferred_element_type=F32)


def tn(a, b):
    return lax.dot_general(a, b, (((0,), (0,)), ((), ())), preferred_element_type=F32)


def rows_at(index, size):
    return pl.ds(pl.multiple_of(index * size, 32), size)


def vec(vv_ref, row, lane):
    return jnp.concatenate(
        [vv_ref[o].astype(F32)[row : row + 1, lane : lane + OWN] for o in range(OWNERS)], axis=1
    )


def norm_stats(v):
    mean = jnp.mean(v, axis=-1, keepdims=True)
    cen = v - mean
    var = jnp.mean(cen * cen, axis=-1, keepdims=True)
    r = lax.rsqrt(var + 1e-12)
    return cen * r, r


def norm_kernel(tab, x_ref, n_ref):
    n_ref[...] = norm_stats(x_ref[...])[0].astype(BF16)


def prep_kernel(tab, x_ref, w_ref, rows_ref, n_ref, panel_ref):
    z = tab[1]
    panel_ref[OWN:, :] = rows_ref[...]
    for k in range(ULY):

        @pl.when(z == k)
        def _():
            parts = [w_ref[:, p * WIDTH + k * HW : p * WIDTH + (k + 1) * HW] for p in range(3)]
            panel_ref[:OWN, :] = jnp.concatenate(parts, axis=1)

    n_ref[...] = norm_stats(x_ref[...])[0].astype(BF16)


def quarter(index):
    return pl.ds(pl.multiple_of(index * QUART, 128), QUART)


def ffn_prep_kernel(tab, u_ref, d_ref, a_ref, b_ref, turned):
    b = tab[3]
    for q in range(BLK):
        part = d_ref[q * QUART : (q + 1) * QUART, :]
        turned[q] = part.astype(F32).T.astype(BF16)
    for s in range(BLK):
        q = jnp.bitwise_xor(b, s)
        ref = (a_ref, b_ref)[s // 2]
        ref[s % 2, 0] = u_ref[:, quarter(q)]
        ref[s % 2, 1] = turned[q]


def qkv_kernel(owner_bits, tab, n0, n1, n2, n3, *rest):
    arrays = rest[: len(owner_bits)]
    q_ref, kv_ref, h_ref, w_ref, vv_ref = rest[len(owner_bits) :]
    me, z = tab[0], tab[1]
    for ref, bits in zip(arrays, owner_bits):
        for i, bit in enumerate(bits):
            o = jnp.bitwise_xor(me, bit)
            w_ref[rows_at(o, OWN), :] = ref[i, :OWN, :]
            vv_ref[o] = ref[i, OWN:PANEL, :]
    gain = vec(vv_ref, 0, 0)
    shift = vec(vv_ref, 0, OWN)
    lo = vv_ref[2 * z].astype(F32)
    hi = vv_ref[2 * z + 1].astype(F32)
    zero = jnp.zeros((1, HW), F32)
    bias = jnp.concatenate(
        [
            lo[0:1, 2 * OWN : 3 * OWN],
            hi[0:1, 2 * OWN : 3 * OWN],
            zero,
            lo[0:1, 3 * OWN : 4 * OWN],
            hi[0:1, 3 * OWN : 4 * OWN],
        ],
        axis=1,
    )
    for i, ref in enumerate((n0, n1, n2, n3)):
        rows = slice(i * ROWS, (i + 1) * ROWS)
        h = (ref[...].astype(F32) * gain + shift).astype(BF16)
        h_ref[rows, :] = h
        proj = (nn(h, w_ref[...]) + bias).astype(BF16)
        q_ref[rows, :] = proj[:, :HW] * jnp.asarray(HEAD_DIM ** (-0.5), BF16)
        kv_ref[rows, :] = proj[:, HW:]


def placed(piece, upper):
    zero = jnp.zeros_like(piece)
    return jnp.concatenate([zero, piece] if upper else [piece, zero], axis=1)


def head_cols(h):
    return slice(h * HEAD_DIM, (h + 1) * HEAD_DIM)


def window(index):
    lane = index * HEAD_DIM
    start = lane // 128 * 128
    return slice(start, start + 128), (lane % 128) >= 64


def attend_kernel(tab, q_ref, k0, k1, k2, k3, qc_ref, kc_ref, o0, o1, o2, o3, all_ref, lse_ref):
    kvs = (k0, k1, k2, k3)
    outs = (o0, o1, o2, o3)

    lane = lax.broadcasted_iota(jnp.int32, (ROWS, 128), 1)

    def step(i, carry):
        rows = rows_at(i, ROWS)
        code1 = qc_ref[rows, 0:1]
        code2 = qc_ref[rows, 1:2]
        masks = []
        for j in range(BLK):
            kc = kc_ref[0:1, j * GROUP : (j + 1) * GROUP]
            masks.append((kc == code1) | (kc == code2))
        heads = []
        lse = jnp.zeros((ROWS, 128), F32)
        for h in range(LOCAL_HEADS):
            kwin, kup = window(h)
            vwin, vup = window(LOCAL_HEADS + h)
            qp = placed(q_ref[rows, head_cols(h)], kup)
            scores = [
                jnp.where(masks[j], nt(qp, kvs[j][:, kwin]), NEG) for j in range(BLK)
            ]
            top = functools.reduce(jnp.maximum, [jnp.max(s, axis=1, keepdims=True) for s in scores])
            total = jnp.zeros((ROWS, 1), F32)
            acc = jnp.zeros((ROWS, 128), F32)
            for j in range(BLK):
                e = jnp.exp(scores[j] - top)
                total = total + jnp.sum(e, axis=1, keepdims=True)
                acc = acc + nn(e.astype(BF16), kvs[j][:, vwin])
            acc = acc[:, 64:] if vup else acc[:, :64]
            heads.append((acc / total).astype(BF16))
            lse = jnp.where(lane == h, top + jnp.log(total), lse)
        all_ref[rows, :] = jnp.concatenate(heads, axis=1)
        lse_ref[rows, :] = lse
        return carry

    lax.fori_loop(0, ULY, step, 0)
    for i in range(ULY):
        outs[i][...] = all_ref[i * ROWS : (i + 1) * ROWS, :]


def mix_kernel(owner_bits, tab, a0, a1, a2, a3, x_ref, vv_ref, *rest):
    arrays = rest[: len(owner_bits)]
    resid_ref, h_ref, ow_ref = rest[len(owner_bits) :]
    me, z = tab[0], tab[1]
    for ref, bits in zip(arrays, owner_bits):
        for i, bit in enumerate(bits):
            ow_ref[rows_at(jnp.bitwise_xor(me, bit), OWN), :] = ref[i]
    acc = x_ref[...] + vec(vv_ref, 0, 4 * OWN)
    for j, ref in enumerate((a0, a1, a2, a3)):
        acc = acc + nn(ref[...], ow_ref[rows_at(jnp.bitwise_xor(z, j), HW), :])
    resid_ref[...] = acc
    n, _ = norm_stats(acc)
    h_ref[...] = (n * vec(vv_ref, 0, 5 * OWN) + vec(vv_ref, 1, 0)).astype(BF16)


CHUNK = 256


def ffn_kernel(plan, tab, h0, h1, h2, h3, c0, c1, c2, c3, vv_ref, *rest):
    count = 1 + max(index for index, _, _ in plan)
    parts = rest[:count]
    act_ref, dhid_ref, yo_ref, y1, y2, y3, go_ref, g1, g2, g3 = rest[count : count + 10]
    u_ref, d_ref, hall, call_ref, bias_ref, yacc, gacc, sems = rest[count + 10 :]
    me, b = tab[0], tab[3]
    copies = []
    for index, slot, bit in plan:
        rows = rows_at(jnp.bitwise_xor(me, bit), OWN)
        for k, target in enumerate((u_ref, d_ref)):
            copy = pltpu.make_async_copy(
                parts[index].at[slot, k], target.at[rows, :], sems.at[len(copies)]
            )
            copy.start()
            copies.append(copy)
    for i, (h_ref, c_ref) in enumerate(((h0, c0), (h1, c1), (h2, c2), (h3, c3))):
        rows = slice(i * ROWS, (i + 1) * ROWS)
        hall[rows, :] = h_ref[...]
        call_ref[rows, :] = c_ref[...]
    for k in range(2):
        bias_ref[:, k * 384 : (k + 1) * 384] = vv_ref[2 * b + k].astype(F32)[1:2, 192:576]
    yacc[...] = jnp.zeros_like(yacc)
    gacc[...] = jnp.zeros_like(gacc)
    for copy in copies:
        copy.wait()

    def step(k, carry):
        cols = pl.ds(pl.multiple_of(k * CHUNK, CHUNK), CHUNK)
        hid = nn(hall[...], u_ref[:, cols]) + bias_ref[:, cols]
        dact = nn(call_ref[...], d_ref[:, cols])
        cdf = 0.5 * (1.0 + lax.erf(hid * 0.7071067811865476))
        act = (hid * cdf).astype(BF16)
        pdf = jnp.exp(-0.5 * hid * hid) * 0.3989422804014327
        dhid = (dact * (cdf + hid * pdf)).astype(BF16)
        act_ref[:, cols] = act
        dhid_ref[:, cols] = dhid
        yacc[...] += nt(act, d_ref[:, cols])
        gacc[...] += nt(dhid, u_ref[:, cols])
        return carry

    lax.fori_loop(0, QUART // CHUNK, step, 0)
    yo_ref[...] = yacc[:ROWS, :]
    go_ref[...] = gacc[:ROWS, :]
    for i, (y_ref, g_ref) in enumerate(((y1, g1), (y2, g2), (y3, g3)), 1):
        rows = slice(i * ROWS, (i + 1) * ROWS)
        y_ref[...] = yacc[rows, :].astype(BF16)
        g_ref[...] = gacc[rows, :].astype(BF16)


def ffn_grad_kernel(tab, r0, r1, r2, r3, right_ref, keep, send, left):
    me = tab[0]
    for i, ref in enumerate((r0, r1, r2, r3)):
        left[:, i * ROWS : (i + 1) * ROWS] = ref[...].T
    for ref, base in ((send, 4), (keep, 0)):
        for s in range(BLK):
            o = jnp.bitwise_xor(me, base + s)
            ref[s] = nn(left[rows_at(o, OWN), :], right_ref[...]).astype(BF16)


def back_mix_kernel(
    tab, resid_ref, cot_ref, go_ref, g1, g2, g3, ow_ref, vv_ref, dres_ref, dmix_ref, d0, d1, d2, d3, vs_ref
):
    z = tab[1]
    grad = go_ref[...] + g1[...].astype(F32) + g2[...].astype(F32) + g3[...].astype(F32)
    n, r = norm_stats(resid_ref[...])
    dn = grad * vec(vv_ref, 0, 5 * OWN)
    dres = cot_ref[...] + r * (
        dn
        - jnp.mean(dn, axis=-1, keepdims=True)
        - n * jnp.mean(dn * n, axis=-1, keepdims=True)
    )
    dres_ref[...] = dres
    dmix = dres.astype(BF16)
    dmix_ref[...] = dmix
    for j, ref in enumerate((d0, d1, d2, d3)):
        ref[...] = nt(dmix, ow_ref[rows_at(jnp.bitwise_xor(z, j), HW), :]).astype(BF16)
    vs_ref[0:1, :] = jnp.sum(dmix.astype(F32), axis=0, keepdims=True)
    vs_ref[1:2, :] = jnp.sum(grad * n, axis=0, keepdims=True)
    vs_ref[2:3, :] = jnp.sum(grad, axis=0, keepdims=True)
    vs_ref[3:8, :] = jnp.zeros((5, WIDTH), F32)


def out_grad_kernel(tab, a0, a1, a2, a3, dmix_ref, vs_ref, dhid_ref, c_ref, keep, send, left, vrow):
    me, z, b = tab[0], tab[1], tab[3]
    for j, ref in enumerate((a0, a1, a2, a3)):
        left[rows_at(jnp.bitwise_xor(z, j), HW), :] = ref[...].astype(F32).T.astype(BF16)
    vs = vs_ref[...]
    usum = jnp.sum(dhid_ref[...].astype(F32), axis=0, keepdims=True)
    csum = jnp.sum(c_ref[...].astype(F32), axis=0, keepdims=True)
    for o in range(OWNERS):
        part = usum[:, (o % 2) * 384 : (o % 2 + 1) * 384]
        row = jnp.concatenate(
            [vs[k : k + 1, o * OWN : (o + 1) * OWN] for k in range(3)]
            + [jnp.where(b == o // 2, part, 0.0), csum[:, o * OWN : (o + 1) * OWN]],
            axis=1,
        )
        vrow[o] = jnp.broadcast_to(row, (16, WIDTH)).astype(BF16)
    for ref, base in ((send, 1), (keep, 0)):
        for s in range(4):
            o = jnp.bitwise_xor(me, base + (s // 2) * 2 + (s % 2) * 4)
            ref[s, :OWN, :] = nn(left[rows_at(o, OWN), :], dmix_ref[...]).astype(BF16)
            ref[s, OWN:, :] = vrow[o]


def back_attend_kernel(
    tab,
    q_ref,
    k0,
    k1,
    k2,
    k3,
    g0,
    g1,
    g2,
    g3,
    all_ref,
    lse_ref,
    qr_ref,
    kcol_ref,
    dq_ref,
    keep,
    send,
    acc,
    gall,
):
    kvs = (k0, k1, k2, k3)
    acc[...] = jnp.zeros_like(acc)
    for i, g_ref in enumerate((g0, g1, g2, g3)):
        gall[i * ROWS : (i + 1) * ROWS, :] = g_ref[...]
    lane = lax.broadcasted_iota(jnp.int32, (ROWS, 128), 1)

    def step(i, carry):
        rows = rows_at(i, ROWS)
        prod = gall[rows, :].astype(F32) * all_ref[rows, :].astype(F32)
        stat = jnp.zeros((ROWS, 128), F32)
        for h in range(LOCAL_HEADS):
            stat = jnp.where(
                lane == h, jnp.sum(prod[:, head_cols(h)], axis=1, keepdims=True), stat
            )
        rowdot = stat.T
        lse = lse_ref[rows, :].T
        code1 = qr_ref[0:1, rows]
        code2 = qr_ref[1:2, rows]
        dq = [jnp.zeros((ROWS, 128), F32) for _ in range(LOCAL_HEADS)]
        for j in range(BLK):
            kc = kcol_ref[j * GROUP : (j + 1) * GROUP, :]
            mask = (kc == code1) | (kc == code2)
            for h in range(LOCAL_HEADS):
                kwin, kup = window(h)
                vwin, vup = window(LOCAL_HEADS + h)
                qp = placed(q_ref[rows, head_cols(h)], kup)
                gp = placed(gall[rows, head_cols(h)], vup)
                kk = kvs[j][:, kwin]
                scores = nt(kk, qp)
                p = jnp.where(mask, jnp.exp(scores - lse[h : h + 1, :]), 0.0)
                dp = nt(kvs[j][:, vwin], gp)
                ds = (p * (dp - rowdot[h : h + 1, :])).astype(BF16)
                acc[j, :, vwin] += nn(p.astype(BF16), gp)
                acc[j, :, kwin] += nn(ds, qp)
                dq[h] = dq[h] + tn(ds, kk)
        parts = []
        for h in range(LOCAL_HEADS):
            _, kup = window(h)
            parts.append(dq[h][:, 64:] if kup else dq[h][:, :64])
        dq_ref[rows, :] = (jnp.concatenate(parts, axis=1) * HEAD_DIM ** (-0.5)).astype(BF16)
        return carry

    lax.fori_loop(0, ULY, step, 0)
    keep[0] = acc[0].astype(BF16)
    keep[1] = acc[2].astype(BF16)
    send[0] = acc[1].astype(BF16)
    send[1] = acc[3].astype(BF16)


def back_proj_kernel(
    tab, dq_ref, keep, recv, w_ref, n0, n1, n2, n3, dproj_ref, h0, h1, h2, h3, vs_ref
):
    dproj_ref[:, :HW] = dq_ref[...]
    dproj_ref[:, HW:] = (keep[...].astype(F32) + recv[...].astype(F32)).astype(BF16)
    gain = jnp.zeros((1, WIDTH), F32)
    shift = jnp.zeros((1, WIDTH), F32)
    for i, (n_ref, out) in enumerate(((n0, h0), (n1, h1), (n2, h2), (n3, h3))):
        rows = slice(i * ROWS, (i + 1) * ROWS)
        grad = nt(dproj_ref[rows, :], w_ref[...])
        out[...] = grad.astype(out.dtype)
        gain = gain + jnp.sum(grad * n_ref[...].astype(F32), axis=0, keepdims=True)
        shift = shift + jnp.sum(grad, axis=0, keepdims=True)
    vs_ref[0:1, :] = gain
    vs_ref[1:2, :] = shift
    cols = jnp.sum(dproj_ref[...].astype(F32), axis=0, keepdims=True)
    vs_ref[2:3, :] = jnp.concatenate([cols, jnp.zeros((1, WIDTH - 3 * HW), F32)], axis=1)
    vs_ref[3:8, :] = jnp.zeros((5, WIDTH), F32)


def qkv_grad_kernel(tab, h_ref, dproj_ref, vs_ref, keep, send, left, vrow):
    me, z = tab[0], tab[1]
    vs = vs_ref[...]
    for o in range(OWNERS):
        row = [vs[k : k + 1, o * OWN : (o + 1) * OWN] for k in range(2)]
        for lane in (0, 2 * HW):
            lane = lane + (o % 2) * OWN
            row.append(jnp.where(z == o // 2, vs[2:3, lane : lane + OWN], 0.0))
        row.append(jnp.zeros((1, 3 * HW - 4 * OWN), F32))
        vrow[o] = jnp.broadcast_to(jnp.concatenate(row, axis=1), (16, 3 * HW)).astype(BF16)
    for i in range(ULY):
        rows = slice(i * ROWS, (i + 1) * ROWS)
        left[:, rows] = h_ref[rows, :].T
    for ref, base in ((keep, 0), (send, 1)):
        for s in range(4):
            o = jnp.bitwise_xor(me, base + (s // 2) * 2 + (s % 2) * 4)
            ref[s, :OWN, :] = nn(left[rows_at(o, OWN), :], dproj_ref[...]).astype(BF16)
            ref[s, OWN:, :] = vrow[o]


def back_norm_kernel(tab, x_ref, dres_ref, h0, h1, h2, h3, vv_ref, out_ref):
    grad = h0[...] + h1[...].astype(F32) + h2[...].astype(F32) + h3[...].astype(F32)
    n, r = norm_stats(x_ref[...])
    dn = grad * vec(vv_ref, 0, 0)
    out_ref[...] = dres_ref[...] + r * (
        dn
        - jnp.mean(dn, axis=-1, keepdims=True)
        - n * jnp.mean(dn * n, axis=-1, keepdims=True)
    )


def output_kernel(tab, resid_ref, yo_ref, y1, y2, y3, vv_ref, out_ref):
    got = y1[...].astype(F32) + y2[...].astype(F32) + y3[...].astype(F32)
    out_ref[...] = resid_ref[...] + yo_ref[...] + got + vec(vv_ref, 1, OWN)


def low_sum(a, b):
    return (a.astype(F32) + b.astype(F32)).astype(BF16)


def split_kernel(bit, tab, a_ref, ac_ref, by_ref, byc_ref, keep, send):
    for value, low_out, high_out in ((0, keep, send), (1, send, keep)):

        @pl.when(tab[bit] == value)
        def _():
            low_out[0] = a_ref[0]
            low_out[1] = ac_ref[1]
            high_out[0] = by_ref[0]
            high_out[1] = byc_ref[1]


def merge_kernel(bit, tab, a_ref, b_ref, keep, send):
    for value, low_out, high_out in ((0, keep, send), (1, send, keep)):

        @pl.when(tab[bit] == value)
        def _():
            low_out[...] = low_sum(a_ref[0], b_ref[0])
            high_out[...] = low_sum(a_ref[1], b_ref[1])


def up_final_kernel(tab, p0, p1, p2, p3, out_ref):
    b, odd, high = tab[3], tab[4], tab[5]
    for flip, ref in ((0, p0), (2, p1), (1, p2), (3, p3)):
        q = jnp.bitwise_xor(jnp.bitwise_xor(b, 2 * odd + high), flip)
        out_ref[:, quarter(q)] = ref[...].astype(F32)


def down_final_kernel(tab, p0, p1, p2, p3, out_ref):
    b, odd, high = tab[3], tab[4], tab[5]
    for flip, ref in ((0, p0), (1, p1), (2, p2), (3, p3)):
        q = jnp.bitwise_xor(jnp.bitwise_xor(b, 2 * high + odd), flip)
        out_ref[quarter(q), :] = ref[...].astype(F32).T


def qkv_final_kernel(tab, p0, p1, p2, p3, out_ref, vec_ref):
    z = tab[1]
    refs = (p0, p1, p2, p3)
    for k in range(ULY):

        @pl.when(z == k)
        def _():
            for p in range(3):
                cols = [
                    refs[t ^ k][:OWN, p * HW : (p + 1) * HW].astype(F32) for t in range(ULY)
                ]
                out_ref[:, p * WIDTH : (p + 1) * WIDTH] = jnp.concatenate(cols, axis=1)

    total = jnp.zeros((16, 3 * HW), F32)
    for ref in refs:
        total = total + ref[OWN:, :].astype(F32)
    vec_ref[...] = total[:8, :]


def add_low(a, b):
    return (a.astype(F32) + b.astype(F32)).astype(BF16)


def xor_order(array, axis, index):
    shape = array.shape
    two = array.reshape(shape[:axis] + (2, 2) + shape[axis + 1 :])
    two = jnp.where((index & 1) == 1, jnp.flip(two, axis + 1), two)
    two = jnp.where((index & 2) == 2, jnp.flip(two, axis), two)
    return two.reshape(shape)


def body(
    inputs,
    cotangent,
    qkv_weight,
    query_bias,
    value_bias,
    out_weight,
    out_bias,
    norm1_gain,
    norm1_bias,
    norm2_gain,
    norm2_bias,
    up_weight,
    up_bias,
    down_weight,
    down_bias,
    doc_lengths,
    pad_mask,
):
    dp_count = lax.axis_size("dp")
    near = dp_count == 2
    dp = lax.axis_index("dp")
    z = lax.axis_index("uly")
    b = lax.axis_index("blk")
    core = b & 1
    rank = dp * BLK + b
    me = rank if near else jnp.int32(0)
    tab = jnp.stack([me, z, core, b, z & 1, z >> 1]).astype(jnp.int32)
    own_rows = WIDTH // (dp_count * BLK)
    axes = ("dp", "blk")

    x = inputs.reshape(ROWS, WIDTH)
    cot = cotangent.reshape(ROWS, WIDTH)

    if near:
        row0 = jnp.concatenate(
            [norm1_gain, norm1_bias, query_bias, value_bias, out_bias, norm2_gain]
        )
        row1 = jnp.concatenate([norm2_bias, down_bias, up_bias])
        vec_rows = jnp.concatenate(
            [row0[None], row1[None], jnp.zeros((14, 3 * HW), BF16)], axis=0
        )
        n0, panel = call(
            prep_kernel,
            [sds((ROWS, WIDTH), BF16), sds((PANEL, 3 * HW), BF16)],
            [tab, x, qkv_weight, vec_rows],
        )

        def spread(array):
            far = swap(array, "dp", 1)
            near_y = swap(array, "blk", 2)
            far_y = swap(far, "blk", 2)
            direct = [array, near_y, far, far_y]
            return direct + [swap(a, "blk", 1) for a in direct]

        a_parts = [a[None] for a in spread(panel)]
        o_parts = [a[None] for a in spread(out_weight)]
        four_bits = [[0], [2], [4], [6], [1], [3], [5], [7]]
        w_a, w_b = call(
            ffn_prep_kernel,
            [sds((2, 2, OWN, QUART), BF16)] * 2,
            [tab, up_weight, down_weight],
            scratch=[pltpu.VMEM((BLK, OWN, QUART), BF16)],
        )
        w_ax, w_bx = swap(w_a, "dp", 1), swap(w_b, "dp", 1)
        w_by, w_bxy = swap(w_b, "blk", 2), swap(w_bx, "blk", 2)
        w_parts = [w_a, w_by, w_ax, w_bxy]
        w_parts = w_parts + [swap(a, "blk", 1) for a in w_parts]
        w_plan = [
            (0, 0, 0), (1, 0, 2), (2, 0, 4), (3, 0, 6), (4, 1, 1), (5, 1, 3), (6, 1, 5), (7, 1, 7)
        ]
    else:
        (n0,) = call(norm_kernel, [sds((ROWS, WIDTH), BF16)], [tab, x])
        qkv_cols = lax.dynamic_index_in_dim(
            qkv_weight.reshape(own_rows, 3, ULY, HW), z, axis=2, keepdims=False
        ).reshape(own_rows, 3 * HW)

        def full(array):
            return lax.all_gather(array, axes, axis=0, tiled=True)

        def eight(vector):
            return full(vector).reshape(OWNERS, 1, -1)

        def mine(array):
            cols = full(array).reshape(WIDTH, BLK, QUART)
            return lax.dynamic_index_in_dim(cols, b, 1, False).reshape(OWNERS, OWN, QUART)

        row0 = jnp.concatenate(
            [
                eight(v)
                for v in (norm1_gain, norm1_bias, query_bias, value_bias, out_bias, norm2_gain)
            ],
            axis=2,
        )
        row1 = jnp.concatenate([eight(v) for v in (norm2_bias, down_bias, up_bias)], axis=2)
        a_parts = [
            jnp.concatenate(
                [
                    full(qkv_cols).reshape(OWNERS, OWN, 3 * HW),
                    row0,
                    row1,
                    jnp.zeros((OWNERS, 14, 3 * HW), BF16),
                ],
                axis=1,
            )
        ]
        four_bits = [list(range(OWNERS))]
        o_parts = [full(out_weight).reshape(OWNERS, OWN, WIDTH)]
        w_parts = [jnp.stack([mine(up_weight), mine(down_weight.T)], axis=1)]
        w_plan = [(0, o, o) for o in range(OWNERS)]
    n1, n2, n3 = (swap(n0, "uly", k) for k in (1, 2, 3))

    ends = jnp.cumsum(doc_lengths.reshape(-1), dtype=jnp.int32)
    zs = jnp.arange(ULY, dtype=jnp.int32) ^ z
    bs = jnp.arange(BLK, dtype=jnp.int32) ^ b
    within = jnp.arange(ROWS, dtype=jnp.int32)
    kplace = ((zs[None, :, None] * BLK + bs[:, None, None]) * ROWS + within).reshape(KEYS)
    kseg = jnp.sum((kplace[:, None] >= ends[None, :]).astype(jnp.int32), axis=1)
    valid = pad_mask.reshape(ULY, BLK, ROWS)
    valid = xor_order(xor_order(valid, 0, z), 1, b).transpose(1, 0, 2).reshape(KEYS)
    kcode = jnp.where(valid > 0, kseg, kplace + 64)
    qcodes = jnp.stack([kseg[:GROUP], kplace[:GROUP] + 64])

    q, kv, h1, w_qkv, vv = call(
        functools.partial(qkv_kernel, four_bits),
        [
            sds((GROUP, HW), BF16),
            sds((GROUP, 2 * HW), BF16),
            sds((GROUP, WIDTH), BF16),
            sds((WIDTH, 3 * HW), BF16),
            sds((OWNERS, 16, 3 * HW), BF16),
        ],
        [tab, n0, n1, n2, n3, *a_parts],
        flops=2 * GROUP * WIDTH * 3 * HW,
    )
    kv_y = swap(kv, "blk", 2)
    kv_c = swap(kv, "blk", 1)
    kv_yc = swap(kv_y, "blk", 1)
    kvs = [kv, kv_c, kv_y, kv_yc]

    *attn_slots, attn_all, lse = call(
        attend_kernel,
        [sds((ROWS, HW), BF16)] * ULY + [sds((GROUP, HW), BF16), sds((GROUP, 128), F32)],
        [tab, q, *kvs, qcodes.T, kcode[None, :]],
        flops=4 * GROUP * KEYS * HW,
    )
    attn = [attn_slots[0]] + [swap(attn_slots[k], "uly", k) for k in (1, 2, 3)]

    resid, h2, ow = call(
        functools.partial(mix_kernel, four_bits),
        [sds((ROWS, WIDTH), F32), sds((ROWS, WIDTH), BF16), sds((WIDTH, WIDTH), BF16)],
        [tab, *attn, x, vv, *o_parts],
        flops=2 * ROWS * WIDTH * WIDTH,
    )
    cb = cot.astype(BF16)

    def around(array):
        near_y = swap(array, "blk", 2)
        return [array, swap(array, "blk", 1), near_y, swap(near_y, "blk", 1)]

    cbs = around(cb)
    h2s = around(h2)
    parts = len(w_parts)
    act, dhid, yo, *sums = call(
        functools.partial(ffn_kernel, w_plan),
        [sds((GROUP, QUART), BF16)] * 2
        + ([sds((ROWS, WIDTH), F32)] + [sds((ROWS, WIDTH), BF16)] * 3) * 2,
        [tab, *h2s, *cbs, vv, *w_parts],
        scratch=[
            pltpu.VMEM((WIDTH, QUART), BF16),
            pltpu.VMEM((WIDTH, QUART), BF16),
            pltpu.VMEM((GROUP, WIDTH), BF16),
            pltpu.VMEM((GROUP, WIDTH), BF16),
            pltpu.VMEM((1, QUART), F32),
            pltpu.VMEM((GROUP, WIDTH), F32),
            pltpu.VMEM((GROUP, WIDTH), F32),
            pltpu.SemaphoreType.DMA((2 * OWNERS,)),
        ],
        flops=8 * GROUP * WIDTH * QUART,
        in_any=range(10, 10 + parts),
    )
    ys, go, gs = sums[:3], sums[3], sums[4:]
    gs = [swap(g, "blk", k) for k, g in ((1, gs[0]), (2, gs[1]), (3, gs[2]))]
    ys = [swap(y, "blk", k) for k, y in ((1, ys[0]), (2, ys[1]), (3, ys[2]))]
    (output,) = call(output_kernel, [sds((ROWS, WIDTH), F32)], [tab, resid, yo, *ys, vv])

    dres, dmix, *dattn_slots, vs2 = call(
        back_mix_kernel,
        [sds((ROWS, WIDTH), F32), sds((ROWS, WIDTH), BF16)]
        + [sds((ROWS, HW), BF16)] * ULY
        + [sds((8, WIDTH), F32)],
        [tab, resid, cot, go, *gs, ow, vv],
        flops=2 * ROWS * WIDTH * WIDTH,
    )
    dattn = [dattn_slots[0]] + [swap(dattn_slots[k], "uly", k) for k in (1, 2, 3)]

    def panel_grad(rows, right):
        return call(
            ffn_grad_kernel,
            [sds((BLK, OWN, QUART), BF16)] * 2,
            [tab, *rows, right],
            scratch=[pltpu.VMEM((WIDTH, GROUP), BF16)],
            flops=2 * GROUP * WIDTH * QUART,
        )

    ukeep, usend = panel_grad(h2s, dhid)
    dkeep, dsend = panel_grad(cbs, act)
    okeep, osend = call(
        out_grad_kernel,
        [sds((4, PANEL, WIDTH), BF16)] * 2,
        [tab, *attn, dmix, vs2, dhid, cb],
        scratch=[pltpu.VMEM((WIDTH, ROWS), BF16), pltpu.VMEM((OWNERS, 16, WIDTH), BF16)],
        flops=2 * ROWS * WIDTH * WIDTH,
    )

    dq, keep_kv, send_kv = call(
        back_attend_kernel,
        [sds((GROUP, HW), BF16), sds((2, GROUP, 2 * HW), BF16), sds((2, GROUP, 2 * HW), BF16)],
        [tab, q, *kvs, *dattn, attn_all, lse, qcodes, kcode[:, None]],
        scratch=[pltpu.VMEM((BLK, GROUP, 2 * HW), F32), pltpu.VMEM((GROUP, HW), BF16)],
        flops=10 * GROUP * KEYS * HW,
    )
    got = swap(send_kv, "blk", 1)
    kv_keep = add_low(keep_kv[0], got[0])
    kv_got = swap(add_low(keep_kv[1], got[1]), "blk", 2)
    dproj, g0, g1, g2, g3, vs1 = call(
        back_proj_kernel,
        [sds((GROUP, 3 * HW), BF16), sds((ROWS, WIDTH), F32)]
        + [sds((ROWS, WIDTH), BF16)] * 3
        + [sds((8, WIDTH), F32)],
        [tab, dq, kv_keep, kv_got, w_qkv, n0, n1, n2, n3],
        flops=2 * GROUP * WIDTH * 3 * HW,
    )
    qkeep, qsend = call(
        qkv_grad_kernel,
        [sds((4, PANEL, 3 * HW), BF16)] * 2,
        [tab, h1, dproj, vs1],
        scratch=[pltpu.VMEM((WIDTH, GROUP), BF16), pltpu.VMEM((OWNERS, 16, 3 * HW), BF16)],
        flops=2 * GROUP * WIDTH * 3 * HW,
    )
    g1, g2, g3 = (swap(g, "uly", k) for k, g in ((1, g1), (2, g2), (3, g3)))
    (grad_inputs,) = call(
        back_norm_kernel, [sds((ROWS, WIDTH), F32)], [tab, x, dres, g0, g1, g2, g3, vv]
    )

    if near:
        def owned_panel(keep, send, first, second, final, shape):
            got = swap(send, "dp", 1)
            there = add_low(keep[2:], got[2:])
            here = add_low(keep[:2], got[:2])
            there = swap(there, "blk", 2)
            pieces = [here, swap(here, "blk", 1), there, swap(there, "blk", 1)]
            pair = sds((2, OWN, QUART), BF16)
            one = sds((OWN, QUART), BF16)
            steps = {1: 4, 2: 5}
            kept, sent = call(
                functools.partial(split_kernel, steps[first]), [pair] * 2, [tab, *pieces]
            )
            kept, sent = call(
                functools.partial(merge_kernel, steps[second]),
                [one] * 2,
                [tab, kept, swap(sent, "uly", first)],
            )
            total = add_low(kept, swap(sent, "uly", second))
            two = swap(total, "uly", 2)
            sums = [total, swap(total, "uly", 1), two, swap(two, "uly", 1)]
            return call(final, [sds(shape, F32)], [tab, *sums])[0]

        grad_up = owned_panel(ukeep, usend, 1, 2, up_final_kernel, (OWN, FF))
        grad_down = owned_panel(dkeep, dsend, 2, 1, down_final_kernel, (FF, OWN))

        o1 = add_low(okeep, swap(osend, "blk", 1))
        o2 = add_low(o1[:2], swap(o1[2:], "blk", 2))
        o3 = add_low(o2[0], swap(o2[1], "dp", 1))
        o4 = add_low(o3, swap(o3, "uly", 1))
        o5 = o4.astype(F32) + swap(o4, "uly", 2).astype(F32)
        grad_ow = o5[:OWN]
        grad_obias, grad_gain2, grad_shift2 = (o5[OWN, k * OWN : (k + 1) * OWN] for k in range(3))
        grad_ubias, grad_dbias = o5[OWN, 288:672], o5[OWN, 672:768]

        q1 = add_low(qkeep, swap(qsend, "blk", 1))
        q2 = add_low(q1[:2], swap(q1[2:], "blk", 2))
        q3 = add_low(q2[0], swap(q2[1], "dp", 1))
        grad_qkv, qvec = call(
            qkv_final_kernel,
            [sds((OWN, 3 * WIDTH), F32), sds((8, 3 * HW), F32)],
            [tab, q3] + [swap(q3, "uly", k) for k in (1, 2, 3)],
        )
        grad_gain1, grad_shift1, grad_qbias, grad_vbias = (
            qvec[0, k * OWN : (k + 1) * OWN] for k in range(4)
        )
    else:

        def owned(array):
            shard = lax.psum_scatter(
                array.astype(F32), axes, scatter_dimension=0, tiled=True
            )
            return lax.psum(shard.astype(BF16), "uly").astype(F32)

        def by_owner(keep, send, order):
            both = jnp.concatenate([keep, send], axis=0)
            return both[jnp.array(order)]

        o8 = by_owner(okeep, osend, [0, 4, 2, 6, 1, 5, 3, 7])
        q8 = by_owner(qkeep, qsend, [0, 4, 2, 6, 1, 5, 3, 7])

        def widen(keep, send):
            flat = jnp.concatenate([keep, send], axis=0).reshape(WIDTH, 1, QUART)
            place = (jnp.arange(BLK) == b)[None, :, None]
            return jnp.where(place, flat, jnp.zeros_like(flat)).reshape(WIDTH, FF)

        grad_up = owned(widen(ukeep, usend))
        grad_down = owned(widen(dkeep, dsend)).T
        grad_ubias = owned(o8[:, OWN, 288:672].reshape(FF))
        grad_dbias = owned(o8[:, OWN, 672:768].reshape(WIDTH))
        grad_ow = owned(o8[:, :OWN].reshape(WIDTH, WIDTH))
        grad_obias, grad_gain2, grad_shift2 = (
            owned(o8[:, OWN, k * OWN : (k + 1) * OWN].reshape(WIDTH)) for k in range(3)
        )
        mine = q8[:, :OWN].reshape(WIDTH, 3, 1, HW)
        spread = jnp.where(
            (jnp.arange(ULY) == z)[None, None, :, None], mine, jnp.zeros_like(mine)
        )
        grad_qkv = owned(spread.reshape(WIDTH, 3 * WIDTH))
        grad_gain1, grad_shift1, grad_qbias, grad_vbias = (
            owned(q8[:, OWN, k * OWN : (k + 1) * OWN].reshape(WIDTH)) for k in range(4)
        )

    return (
        output.reshape(inputs.shape),
        grad_inputs.reshape(inputs.shape),
        grad_qkv,
        grad_qbias,
        grad_vbias,
        grad_ow,
        grad_obias,
        grad_gain1,
        grad_shift1,
        grad_gain2,
        grad_shift2,
        grad_up,
        grad_ubias,
        grad_down,
        grad_dbias,
    )


def solution(mesh):
    rows = P(None, ("dp", "uly", "blk"), None)
    first = P(("dp", "blk"), None)
    flat = P(("dp", "blk"))
    second = P(None, ("dp", "blk"))
    return jax.shard_map(
        body,
        mesh=mesh,
        in_specs=(
            rows,
            rows,
            first,
            flat,
            flat,
            first,
            flat,
            flat,
            flat,
            flat,
            flat,
            first,
            flat,
            second,
            flat,
            P(None, "dp", None),
            P(None, "dp"),
        ),
        out_specs=(
            rows,
            rows,
            first,
            flat,
            flat,
            first,
            flat,
            flat,
            flat,
            flat,
            flat,
            first,
            flat,
            second,
            flat,
        ),
        check_vma=False,
    )
```

profile of v0, /device:TPU:0, one launch (start us, length us, event | category | flops | bytes accessed | tf_op | source)
XLA Modules:
  0.0 278.6 jit_solution(9793871520656753928)
XLA Ops:
  0.7 4.2 %concatenate.9 = bf16[576]{0:T(1024)(128)(2,1)S(1)} concatenate(bf16[96]{0:T(256)(128)(2,1)} %param.24, bf16[96]{0:T(256)(128)(2,1)} %param.25, bf16[96]{0:T(256)(128)(2,1)} %param.20, bf16[96]{0:T(256)(128)(2,1)} %param.21, bf16[96]{0:T(256)(128)(2,1)} %param.23, bf16[96]{0:T(256)(128)(2,1)} %param.26), dimensions={0} | concatenate | bytes 2304 | tf_op jit(solution)/shard_map/concatenate | solution.py:577
  9.1 3.1 %collective-permute-start = (bf16[128,768]{1,0:T(8,128)(2,1)}, bf16[128,768]{1,0:T(8,128)(2,1)S(1)}, u32[]{:S(2)}, u32[]{:S(2)}) collective-permute-start(bf16[128,768]{1,0:T(8,128)(2,1)} %get-tuple-element.77.n0), channel_id=1, source_target_pairs={{0,4},{4,0},{8,12},{12,8},{1,5},{5,1},{9,13},{13,9},{2,6},{6,2},{1... | collective-permute-start | bytes 589832 | tf_op jit(solution)/shard_map/ppermute | solution.py:35
  33.6 3.5 %shard_map.281 = (bf16[512,192]{1,0:T(8,128)(2,1)}, bf16[512,384]{1,0:T(8,128)(2,1)}, bf16[512,768]{1,0:T(8,128)(2,1)}, bf16[768,576]{1,0:T(8,128)(2,1)}, bf16[8,16,576]{2,1,0:T(8,128)(2,1)}) custom-call(s32[6]{0:T(128)} %stack.34.tab, bf16[128,768]{1,0:T(8,128)(2,1)} %get-tuple-element.77.n0, bf16[128,768]{1,0:T(8,128)(2,1)} %copy-done.3, ...), custom_call_target="tpu_custom_call" | custom-call | flops 452984832 | bytes 4227096 | tf_op jit(solution)/shard_map/pallas_call | solution.py:55
  40.9 11.3 %collective-permute-done.18 = bf16[96,768]{1,0:T(8,128)(2,1)S(1)} collective-permute-done((bf16[96,768]{1,0:T(8,128)(2,1)S(1)}, bf16[96,768]{1,0:T(8,128)(2,1)S(1)}, u32[]{:S(2)}, u32[]{:S(2)}) %collective-permute-start.18) | collective-permute-done | bytes 147488 | tf_op jit(solution)/shard_map/ppermute | solution.py:35
  59.0 9.7 %shard_map.282 = (bf16[128,192]{1,0:T(8,128)(2,1)}, bf16[128,192]{1,0:T(8,128)(2,1)}, bf16[128,192]{1,0:T(8,128)(2,1)}, bf16[128,192]{1,0:T(8,128)(2,1)}, bf16[512,192]{1,0:T(8,128)(2,1)}, /*index=5*/f32[512,128]{1,0:T(8,128)}) custom-call(s32[6]{0:T(128)} %stack.34.tab, bf16[512,192]{1,0:T(8,128)(2,1)} %get-tuple-element.79.q_ref, ...), custom_call_target="tpu_custom_call" | custom-call | flops 805306368 | bytes 2437144 | tf_op jit(solution)/shard_map/pallas_call | solution.py:55
  68.8 4.0 %collective-permute-start.13 = (bf16[128,192]{1,0:T(8,128)(2,1)}, bf16[128,192]{1,0:T(8,128)(2,1)S(1)}, u32[]{:S(2)}, u32[]{:S(2)}) collective-permute-start(bf16[128,192]{1,0:T(8,128)(2,1)} %get-tuple-element.82), channel_id=1, source_target_pairs={{0,4},{4,0},{8,12},{12,8},{1,5},{5,1},{9,13},{13,9},{2,6},{6,2},{1... | collective-permute-start | bytes 147464 | tf_op jit(solution)/shard_map/ppermute | solution.py:35
  75.4 4.1 %collective-permute-done.32.rest_3_ = bf16[2,2,96,768]{3,2,1,0:T(8,128)(2,1)} collective-permute-done((bf16[2,2,96,768]{3,2,1,0:T(8,128)(2,1)}, bf16[2,2,96,768]{3,2,1,0:T(8,128)(2,1)}, u32[]{:S(2)}, u32[]{:S(2)}) %collective-permute-start.32) | collective-permute-done | bytes 589856 | tf_op jit(solution)/shard_map/ppermute | solution.py:35
  82.1 3.3 %shard_map.283 = (f32[128,768]{1,0:T(8,128)}, bf16[128,768]{1,0:T(8,128)(2,1)}, bf16[768,768]{1,0:T(8,128)(2,1)}) custom-call(s32[6]{0:T(128)} %stack.34.tab, bf16[128,192]{1,0:T(8,128)(2,1)} %get-tuple-element.81.a0, bf16[128,192]{1,0:T(8,128)(2,1)} %copy-done.25, bf16[128,192]{1,0:T(8,128)(2,1)} %copy-done.26, bf16[128,192]{1,0:T(8,128)(2,1)} %copy-done.27, ...), custom_call_target="tpu_custom_call" | custom-call | flops 150994944 | bytes 3686424 | tf_op jit(solution)/shard_map/pallas_call | solution.py:55
  86.3 6.6 %collective-permute-done.24.h2.r2 = bf16[128,768]{1,0:T(8,128)(2,1)S(1)} collective-permute-done((bf16[128,768]{1,0:T(8,128)(2,1)}, bf16[128,768]{1,0:T(8,128)(2,1)S(1)}, u32[]{:S(2)}, u32[]{:S(2)}) %collective-permute-start.24) | collective-permute-done | bytes 196640 | tf_op jit(solution)/shard_map/ppermute | solution.py:35
  96.0 8.5 %shard_map.285 = (bf16[512,768]{1,0:T(8,128)(2,1)}, bf16[512,768]{1,0:T(8,128)(2,1)}, f32[128,768]{1,0:T(8,128)}, bf16[128,768]{1,0:T(8,128)(2,1)}, bf16[128,768...) custom-call(s32[6]{0:T(128)} %stack.34.tab, ...), custom_call_target="tpu_custom_call" | custom-call | flops 2415919104 | bytes 9977880 | tf_op jit(solution)/shard_map/pallas_call | solution.py:55
  106.4 3.7 %shard_map.298 = (bf16[4,96,768]{2,1,0:T(8,128)(2,1)}, bf16[4,96,768]{2,1,0:T(8,128)(2,1)}) custom-call(s32[6]{0:T(128)} %stack.34.tab, bf16[128,768]{1,0:T(8,128)(2,1)} %copy-done.7, bf16[128,768]{1,0:T(8,128)(2,1)} %copy-done.73, bf16[128,768]{1,0:T(8,128)(2,1)} %collective-permute-done.27.c2.r2, bf16[128,768]{1,0:T(8,128)(2,1)} %copy-done.80, ...), custom_call_target="tpu_custom_call" | custom-call | flops 603979776 | bytes 2752536 | tf_op jit(solution)/shard_map/pallas_call | solution.py:55
  116.3 3.3 %shard_map.287 = (f32[128,768]{1,0:T(8,128)}, bf16[128,768]{1,0:T(8,128)(2,1)}, bf16[128,192]{1,0:T(8,128)(2,1)}, bf16[128,192]{1,0:T(8,128)(2,1)}, bf16[128,192...) custom-call(s32[6]{0:T(128)} %stack.34.tab, f32[128,768]{1,0:T(8,128)} %get-tuple-element.86.resid_ref, ...), custom_call_target="tpu_custom_call" | custom-call | flops 150994944 | bytes 3907608 | tf_op jit(solution)/shard_map/pallas_call | solution.py:55
  119.7 3.1 %shard_map.293 = (bf16[4,112,768]{2,1,0:T(8,128)(2,1)}, bf16[4,112,768]{2,1,0:T(8,128)(2,1)}) custom-call(s32[6]{0:T(128)} %stack.34.tab, bf16[128,192]{1,0:T(8,128)(2,1)} %get-tuple-element.81.a0, bf16[128,192]{1,0:T(8,128)(2,1)} %copy-done.25, bf16[128,192]{1,0:T(8,128)(2,1)} %copy-done.26, bf16[128,192]{1,0:T(8,128)(2,1)} %copy-done.27, ...), custom_call_target="tpu_custom_call" | custom-call | flops 150994944 | bytes 2777112 | tf_op jit(solution)/shard_map/pallas_call | solution.py:55
  131.9 3.7 %shard_map.294 = (bf16[4,96,768]{2,1,0:T(8,128)(2,1)}, bf16[4,96,768]{2,1,0:T(8,128)(2,1)}) custom-call(s32[6]{0:T(128)} %stack.34.tab, bf16[128,768]{1,0:T(8,128)(2,1)} %get-tuple-element.87.h0.r0, bf16[128,768]{1,0:T(8,128)(2,1)} %copy-done.78, bf16[128,768]{1,0:T(8,128)(2,1)} %copy-done.76, bf16[128,768]{1,0:T(8,128)(2,1)} %copy-done.79, ...), custom_call_target="tpu_custom_call" | custom-call | flops 603979776 | bytes 2752536 | tf_op jit(solution)/shard_map/pallas_call | solution.py:55
  138.3 18.3 %shard_map.288 = (bf16[512,192]{1,0:T(8,128)(2,1)}, bf16[2,512,384]{2,1,0:T(8,128)(2,1)}, bf16[2,512,384]{2,1,0:T(8,128)(2,1)}) custom-call(s32[6]{0:T(128)} %stack.34.tab, bf16[512,192]{1,0:T(8,128)(2,1)} %get-tuple-element.79.q_ref, bf16[512,384]{1,0:T(8,128)(2,1)} %get-tuple-element.80.k0, bf16[512,384]{1,0:T(8,128)(2,1)} %collective-permute-done.10.k1, ...), custom_call_target="tpu_custom_call" | custom-call | flops 2013265920 | bytes 4206616 | tf_op jit(solution)/shard_map/pallas_call | solution.py:55
  160.9 7.4 %collective-permute-done.73.by_ref = bf16[2,96,768]{2,1,0:T(8,128)(2,1)S(1)} collective-permute-done((bf16[2,96,768]{2,1,0:T(8,128)(2,1)S(1)}, bf16[2,96,768]{2,1,0:T(8,128)(2,1)S(1)}, u32[]{:S(2)}, u32[]{:S(2)}) %collective-permute-start.73) | collective-permute-done | bytes 294944 | tf_op jit(solution)/shard_map/ppermute | solution.py:35
  169.5 6.1 %collective-permute-done.58 = bf16[2,112,768]{2,1,0:T(8,128)(2,1)S(1)} collective-permute-done((bf16[2,112,768]{2,1,0:T(8,128)(2,1)S(1)}, bf16[2,112,768]{2,1,0:T(8,128)(2,1)S(1)}, u32[]{:S(2)}, u32[]{:S(2)}) %collective-permute-start.58) | collective-permute-done | bytes 344096 | tf_op jit(solution)/shard_map/ppermute | solution.py:35
  176.2 5.8 %collective-permute-done.64.by_ref = bf16[2,96,768]{2,1,0:T(8,128)(2,1)S(1)} collective-permute-done((bf16[2,96,768]{2,1,0:T(8,128)(2,1)S(1)}, bf16[2,96,768]{2,1,0:T(8,128)(2,1)S(1)}, u32[]{:S(2)}, u32[]{:S(2)}) %collective-permute-start.64) | collective-permute-done | bytes 294944 | tf_op jit(solution)/shard_map/ppermute | solution.py:35
  192.4 3.9 %shard_map.289 = (bf16[512,576]{1,0:T(8,128)(2,1)}, f32[128,768]{1,0:T(8,128)}, bf16[128,768]{1,0:T(8,128)(2,1)}, bf16[128,768]{1,0:T(8,128)(2,1)}, bf16[128,768]{1,0:T(8,128)(2,1)}, /*index=5*/f32[8,768]{1,0:T(8,128)}) custom-call(s32[6]{0:T(128)} %stack.34.tab, bf16[512,192]{1,0:T(8,128)(2,1)} %get-tuple-element.106.dq_ref, ...), custom_call_target="tpu_custom_call" | custom-call | flops 452984832 | bytes 4251672 | tf_op jit(solution)/shard_map/pallas_call | solution.py:55
  196.3 3.6 %shard_map.291 = (bf16[4,112,576]{2,1,0:T(8,128)(2,1)}, bf16[4,112,576]{2,1,0:T(8,128)(2,1)}) custom-call(s32[6]{0:T(128)} %stack.34.tab, bf16[512,768]{1,0:T(8,128)(2,1)} %get-tuple-element.114.h_ref, bf16[512,576]{1,0:T(8,128)(2,1)} %get-tuple-element.115.dproj_ref, f32[8,768]{1,0:T(8,128)} %get-tuple-element.116.vs_ref), custom_call_target="tpu_custom_call" | custom-call | flops 452984832 | bytes 2433048 | tf_op jit(solution)/shard_map/pallas_call | solution.py:55
  209.2 6.8 %collective-permute-done.66.b_ref = bf16[2,96,768]{2,1,0:T(8,128)(2,1)S(1)} collective-permute-done((bf16[2,96,768]{2,1,0:T(8,128)(2,1)S(1)}, bf16[2,96,768]{2,1,0:T(8,128)(2,1)S(1)}, u32[]{:S(2)}, u32[]{:S(2)}) %collective-permute-start.66) | collective-permute-done | bytes 294944 | tf_op jit(solution)/shard_map/ppermute | solution.py:35
  222.8 8.6 %collective-permute-done.76 = bf16[96,768]{1,0:T(8,128)(2,1)S(1)} collective-permute-done((bf16[96,768]{1,0:T(8,128)(2,1)}, bf16[96,768]{1,0:T(8,128)(2,1)S(1)}, u32[]{:S(2)}, u32[]{:S(2)}) %collective-permute-start.76) | collective-permute-done | bytes 147488 | tf_op jit(solution)/shard_map/ppermute | solution.py:35
  243.2 7.5 %collective-permute-done.61 = bf16[112,768]{1,0:T(8,128)(2,1)S(1)} collective-permute-done((bf16[112,768]{1,0:T(8,128)(2,1)S(1)}, bf16[112,768]{1,0:T(8,128)(2,1)S(1)}, u32[]{:S(2)}, u32[]{:S(2)}) %collective-permute-start.61) | collective-permute-done | bytes 172064 | tf_op jit(solution)/shard_map/ppermute | solution.py:35
  254.2 3.1 %collective-permute-done.69.p2 = bf16[96,768]{1,0:T(8,128)(2,1)S(1)} collective-permute-done((bf16[96,768]{1,0:T(8,128)(2,1)S(1)}, bf16[96,768]{1,0:T(8,128)(2,1)S(1)}, u32[]{:S(2)}, u32[]{:S(2)}) %collective-permute-start.69) | collective-permute-done | bytes 147488 | tf_op jit(solution)/shard_map/ppermute | solution.py:35
  (386 shorter events, 133.8 us)
Async XLA Ops:
  9.1 17.9 %collective-permute-start = (bf16[128,768]{1,0:T(8,128)(2,1)}, bf16[128,768]{1,0:T(8,128)(2,1)S(1)}, u32[]{:S(2)}, u32[]{:S(2)}) collective-permute-start(bf16[128,768]{1,0:T(8,128)(2,1)} %get-tuple-element.77.n0), channel_id=1, source_target_pairs={{0,4},{4,0},{8,12},{12,8},{1,5},{5,1},{9,13},{13,9},{2,6},{6,2},{1... | collective-permute-start | bytes 589832 | tf_op jit(solution)/shard_map/ppermute | solution.py:35
  29.8 24.4 %collective-permute-start.31 = (bf16[2,2,96,768]{3,2,1,0:T(8,128)(2,1)}, bf16[2,2,96,768]{3,2,1,0:T(8,128)(2,1)}, u32[]{:S(2)}, u32[]{:S(2)}) collective-permute-start(bf16[2,2,96,768]{3,2,1,0:T(8,128)(2,1)} %get-tuple-element.89), channel_id=1, source_target_pairs={{0,16},{16,0},{1,17},{17,1},{2,18},{18,2},{3,19},{19,3},{4,20},{20... | collective-permute-start | bytes 1769480 | tf_op jit(solution)/shard_map/ppermute | solution.py:35
  37.6 17.3 %collective-permute-start.11 = (bf16[512,384]{1,0:T(8,128)(2,1)}, bf16[512,384]{1,0:T(8,128)(2,1)S(1)}, u32[]{:S(2)}, u32[]{:S(2)}) collective-permute-start(bf16[512,384]{1,0:T(8,128)(2,1)} %get-tuple-element.80.k0), channel_id=1, source_target_pairs={{0,2},{1,3},{2,0},{3,1},{4,6},{5,7},{6,4},{7,5},{8,10},{9,11},{10,... | collective-permute-start | bytes 1179656 | tf_op jit(solution)/shard_map/ppermute | solution.py:35
  52.2 21.8 %collective-permute-start.29 = (bf16[2,2,96,768]{3,2,1,0:T(8,128)(2,1)S(1)}, bf16[2,2,96,768]{3,2,1,0:T(8,128)(2,1)S(1)}, u32[]{:S(2)}, u32[]{:S(2)}) collective-permute-start(bf16[2,2,96,768]{3,2,1,0:T(8,128)(2,1)S(1)} %copy-done.65), channel_id=1, source_target_pairs={{0,2},{1,3},{2,0},{3,1},{4,6},{5,7},{6,4},{7,5},{8,10},{9,11},{10,... | collective-permute-start | bytes 1769480 | tf_op jit(solution)/shard_map/ppermute | solution.py:35
  53.6 19.3 %collective-permute-start.30 = (bf16[2,2,96,768]{3,2,1,0:T(8,128)(2,1)S(1)}, bf16[2,2,96,768]{3,2,1,0:T(8,128)(2,1)}, u32[]{:S(2)}, u32[]{:S(2)}) collective-permute-start(bf16[2,2,96,768]{3,2,1,0:T(8,128)(2,1)S(1)} %copy-done.64), channel_id=1, source_target_pairs={{0,16},{16,0},{1,17},{17,1},{2,18},{18,2},{3,19},{19,3},{4,20},{20... | collective-permute-start | bytes 1769480 | tf_op jit(solution)/shard_map/ppermute | solution.py:35
  54.2 25.3 %collective-permute-start.32 = (bf16[2,2,96,768]{3,2,1,0:T(8,128)(2,1)}, bf16[2,2,96,768]{3,2,1,0:T(8,128)(2,1)}, u32[]{:S(2)}, u32[]{:S(2)}) collective-permute-start(bf16[2,2,96,768]{3,2,1,0:T(8,128)(2,1)} %collective-permute-done.31), channel_id=1, source_target_pairs={{0,2},{1,3},{2,0},{3,1},{4,6},{5,7},{6,4},{7,5},{8,10},{9,11},{10,... | collective-permute-start | bytes 1769480 | tf_op jit(solution)/shard_map/ppermute | solution.py:35
  56.3 29.9 %collective-permute-start.33 = (bf16[2,2,96,768]{3,2,1,0:T(8,128)(2,1)S(1)}, bf16[2,2,96,768]{3,2,1,0:T(8,128)(2,1)}, u32[]{:S(2)}, u32[]{:S(2)}) collective-permute-start(bf16[2,2,96,768]{3,2,1,0:T(8,128)(2,1)S(1)} %copy-done.64), channel_id=1, source_target_pairs={{0,1},{1,0},{2,3},{3,2},{4,5},{5,4},{6,7},{7,6},{8,9},{9,8},{10,11... | collective-permute-start | bytes 1769480 | tf_op jit(solution)/shard_map/ppermute | solution.py:35
  110.1 47.0 %collective-permute-start.71 = (bf16[4,96,768]{2,1,0:T(8,128)(2,1)}, bf16[4,96,768]{2,1,0:T(8,128)(2,1)}, u32[]{:S(2)}, u32[]{:S(2)}) collective-permute-start(bf16[4,96,768]{2,1,0:T(8,128)(2,1)} %get-tuple-element.134), channel_id=1, source_target_pairs={{0,16},{16,0},{1,17},{17,1},{2,18},{18,2},{3,19},{19,3},{4,20},{20... | collective-permute-start | bytes 1769480 | tf_op jit(solution)/shard_map/ppermute | solution.py:35
  122.8 35.9 %collective-permute-start.57 = (bf16[4,112,768]{2,1,0:T(8,128)(2,1)}, bf16[4,112,768]{2,1,0:T(8,128)(2,1)S(1)}, u32[]{:S(2)}, u32[]{:S(2)}) collective-permute-start(bf16[4,112,768]{2,1,0:T(8,128)(2,1)} %get-tuple-element.125), channel_id=1, source_target_pairs={{0,1},{1,0},{2,3},{3,2},{4,5},{5,4},{6,7},{7,6},{8,9},{9,8},{10,11... | collective-permute-start | bytes 2064392 | tf_op jit(solution)/shard_map/ppermute | solution.py:35
  135.7 23.3 %collective-permute-start.62 = (bf16[4,96,768]{2,1,0:T(8,128)(2,1)}, bf16[4,96,768]{2,1,0:T(8,128)(2,1)S(1)}, u32[]{:S(2)}, u32[]{:S(2)}) collective-permute-start(bf16[4,96,768]{2,1,0:T(8,128)(2,1)} %get-tuple-element.127), channel_id=1, source_target_pairs={{0,16},{16,0},{1,17},{17,1},{2,18},{18,2},{3,19},{19,3},{4,20},{20... | collective-permute-start | bytes 1769480 | tf_op jit(solution)/shard_map/ppermute | solution.py:35
  156.6 43.3 %collective-permute-start.37 = (bf16[128,768]{1,0:T(8,128)(2,1)}, bf16[128,768]{1,0:T(8,128)(2,1)S(1)}, u32[]{:S(2)}, u32[]{:S(2)}) collective-permute-start(bf16[128,768]{1,0:T(8,128)(2,1)} %get-tuple-element.91), channel_id=1, source_target_pairs={{0,1},{1,0},{2,3},{3,2},{4,5},{5,4},{6,7},{7,6},{8,9},{9,8},{10,11... | collective-permute-start | bytes 589832 | tf_op jit(solution)/shard_map/ppermute | solution.py:35
  158.7 17.3 %collective-permute-start.72 = (bf16[2,96,768]{2,1,0:T(8,128)(2,1)S(1)}, bf16[2,96,768]{2,1,0:T(8,128)(2,1)S(1)}, u32[]{:S(2)}, u32[]{:S(2)}) collective-permute-start(bf16[2,96,768]{2,1,0:T(8,128)(2,1)S(1)} %get-tuple-element.187.a_ref), channel_id=1, source_target_pairs={{0,1},{1,0},{2,3},{3,2},{4,5},{5,4},{6,7},{7,6},{8,9},{9,8},{10,11... | collective-permute-start | bytes 884744 | tf_op jit(solution)/shard_map/ppermute | solution.py:35
  159.0 16.6 %collective-permute-start.58 = (bf16[2,112,768]{2,1,0:T(8,128)(2,1)S(1)}, bf16[2,112,768]{2,1,0:T(8,128)(2,1)S(1)}, u32[]{:S(2)}, u32[]{:S(2)}) collective-permute-start(bf16[2,112,768]{2,1,0:T(8,128)(2,1)S(1)} %slice.138), channel_id=1, source_target_pairs={{0,2},{1,3},{2,0},{3,1},{4,6},{5,7},{6,4},{7,5},{8,10},{9,11},{10,... | collective-permute-start | bytes 1032200 | tf_op jit(solution)/shard_map/ppermute | solution.py:35
  182.0 18.7 %collective-permute-start.59 = (bf16[112,768]{1,0:T(8,128)(2,1)S(1)}, bf16[112,768]{1,0:T(8,128)(2,1)S(1)}, u32[]{:S(2)}, u32[]{:S(2)}) collective-permute-start(bf16[112,768]{1,0:T(8,128)(2,1)S(1)} %slice_bitcast_fusion), channel_id=1, source_target_pairs={{0,16},{16,0},{1,17},{17,1},{2,18},{18,2},{3,19},{19,3},{4,20},{20... | collective-permute-start | bytes 516104 | tf_op jit(solution)/shard_map/ppermute | solution.py:35
  185.3 16.9 %collective-permute-start.39 = (bf16[128,768]{1,0:T(8,128)(2,1)}, bf16[128,768]{1,0:T(8,128)(2,1)S(1)}, u32[]{:S(2)}, u32[]{:S(2)}) collective-permute-start(bf16[128,768]{1,0:T(8,128)(2,1)} %get-tuple-element.93), channel_id=1, source_target_pairs={{0,3},{1,2},{2,1},{3,0},{4,7},{5,6},{6,5},{7,4},{8,11},{9,10},{10,... | collective-permute-start | bytes 589832 | tf_op jit(solution)/shard_map/ppermute | solution.py:35
  200.7 19.5 %collective-permute-start.51 = (bf16[4,112,576]{2,1,0:T(8,128)(2,1)}, bf16[4,112,576]{2,1,0:T(8,128)(2,1)S(1)}, u32[]{:S(2)}, u32[]{:S(2)}) collective-permute-start(bf16[4,112,576]{2,1,0:T(8,128)(2,1)} %get-tuple-element.118), channel_id=1, source_target_pairs={{0,1},{1,0},{2,3},{3,2},{4,5},{5,4},{6,7},{7,6},{8,9},{9,8},{10,11... | collective-permute-start | bytes 1548296 | tf_op jit(solution)/shard_map/ppermute | solution.py:35
  200.8 19.3 %collective-permute-start.60 = (bf16[112,768]{1,0:T(8,128)(2,1)S(1)}, bf16[112,768]{1,0:T(8,128)(2,1)S(1)}, u32[]{:S(2)}, u32[]{:S(2)}) collective-permute-start(bf16[112,768]{1,0:T(8,128)(2,1)S(1)} %fusion.2), channel_id=1, source_target_pairs={{0,4},{4,0},{8,12},{12,8},{1,5},{5,1},{9,13},{13,9},{2,6},{6,2},{1... | collective-permute-start | bytes 516104 | tf_op jit(solution)/shard_map/ppermute | solution.py:35
  205.2 29.4 %collective-permute-start.48 = (bf16[128,768]{1,0:T(8,128)(2,1)S(1)}, bf16[128,768]{1,0:T(8,128)(2,1)S(1)}, u32[]{:S(2)}, u32[]{:S(2)}) collective-permute-start(bf16[128,768]{1,0:T(8,128)(2,1)S(1)} %copy-done.77), channel_id=1, source_target_pairs={{0,4},{4,0},{8,12},{12,8},{1,5},{5,1},{9,13},{13,9},{2,6},{6,2},{1... | collective-permute-start | bytes 589832 | tf_op jit(solution)/shard_map/ppermute | solution.py:35
  205.9 31.6 %collective-permute-start.49 = (bf16[128,768]{1,0:T(8,128)(2,1)S(1)}, bf16[128,768]{1,0:T(8,128)(2,1)S(1)}, u32[]{:S(2)}, u32[]{:S(2)}) collective-permute-start(bf16[128,768]{1,0:T(8,128)(2,1)S(1)} %copy-done.75), channel_id=1, source_target_pairs={{0,8},{4,12},{8,0},{12,4},{1,9},{5,13},{9,1},{13,5},{2,10},{6,14},... | collective-permute-start | bytes 589832 | tf_op jit(solution)/shard_map/ppermute | solution.py:35
  216.0 21.6 %collective-permute-start.50 = (bf16[128,768]{1,0:T(8,128)(2,1)S(1)}, bf16[128,768]{1,0:T(8,128)(2,1)S(1)}, u32[]{:S(2)}, u32[]{:S(2)}) collective-permute-start(bf16[128,768]{1,0:T(8,128)(2,1)S(1)} %copy-done.74), channel_id=1, source_target_pairs={{0,12},{4,8},{8,4},{12,0},{1,13},{5,9},{9,5},{13,1},{2,14},{6,10},... | collective-permute-start | bytes 589832 | tf_op jit(solution)/shard_map/ppermute | solution.py:35
  234.6 19.6 %collective-permute-start.78 = (bf16[96,768]{1,0:T(8,128)(2,1)S(1)}, bf16[96,768]{1,0:T(8,128)(2,1)S(1)}, u32[]{:S(2)}, u32[]{:S(2)}) collective-permute-start(bf16[96,768]{1,0:T(8,128)(2,1)S(1)} %add_convert_fusion.11.p0), channel_id=1, source_target_pairs={{0,8},{4,12},{8,0},{12,4},{1,9},{5,13},{9,1},{13,5},{2,10},{6,14},... | collective-permute-start | bytes 442376 | tf_op jit(solution)/shard_map/ppermute | solution.py:35
  237.6 21.9 %collective-permute-start.77 = (bf16[96,768]{1,0:T(8,128)(2,1)S(1)}, bf16[96,768]{1,0:T(8,128)(2,1)S(1)}, u32[]{:S(2)}, u32[]{:S(2)}) collective-permute-start(bf16[96,768]{1,0:T(8,128)(2,1)S(1)} %add_convert_fusion.11.p0), channel_id=1, source_target_pairs={{0,4},{4,0},{8,12},{12,8},{1,5},{5,1},{9,13},{13,9},{2,6},{6,2},{1... | collective-permute-start | bytes 442376 | tf_op jit(solution)/shard_map/ppermute | solution.py:35
  237.6 19.7 %collective-permute-start.69 = (bf16[96,768]{1,0:T(8,128)(2,1)S(1)}, bf16[96,768]{1,0:T(8,128)(2,1)S(1)}, u32[]{:S(2)}, u32[]{:S(2)}) collective-permute-start(bf16[96,768]{1,0:T(8,128)(2,1)S(1)} %add_convert_fusion.12.p0), channel_id=1, source_target_pairs={{0,8},{4,12},{8,0},{12,4},{1,9},{5,13},{9,1},{13,5},{2,10},{6,14},... | collective-permute-start | bytes 442376 | tf_op jit(solution)/shard_map/ppermute | solution.py:35
  242.9 27.2 %collective-permute-start.68 = (bf16[96,768]{1,0:T(8,128)(2,1)S(1)}, bf16[96,768]{1,0:T(8,128)(2,1)S(1)}, u32[]{:S(2)}, u32[]{:S(2)}) collective-permute-start(bf16[96,768]{1,0:T(8,128)(2,1)S(1)} %add_convert_fusion.12.p0), channel_id=1, source_target_pairs={{0,4},{4,0},{8,12},{12,8},{1,5},{5,1},{9,13},{13,9},{2,6},{6,2},{1... | collective-permute-start | bytes 442376 | tf_op jit(solution)/shard_map/ppermute | solution.py:35
  (144 other events, 1179.1 us)
where the time goes:
time: 279 us
  Pallas kernels  89.4 us (32%)
  waiting for transfers between devices  88.9 us (32%)
  starting transfers between devices  69.4 us (25%)
  local copies, waits for them, and re-layouts  22 us (8%)
  other arithmetic  7.26 us (3%)
    pallas_call x22, Pallas kernels, call(): pl.pallas_call(kernel, out_shape=outs, in_specs=specs, out_specs=[vm() fo...  89.4 us
    ppermute x80, waiting for transfers between devices, swap(): return lax.ppermute(array, axis, [(i, i ^ by) for i in range(peers)])  88.9 us
    ppermute x80, starting transfers between devices, swap(): return lax.ppermute(array, axis, [(i, i ^ by) for i in range(peers)])  69.4 us
    unnamed x178, local copies, waits for them, and re-layouts  11.1 us
  transfers between devices with their start and end apart: 80, of which 27 were waited for; matrix products, arithmetic and copies ran while one was open for 5% of the time, Pallas kernels for 27%

commit v1 on v0

--- a/solution.py
+++ b/solution.py
@@ -27,12 +27,20 @@
 OWN = WIDTH // OWNERS
 PANEL = OWN + 16
 QUART = FF // BLK
-COST = 1
 
 
 def swap(array, axis, by):
     peers = lax.axis_size(axis)
     return lax.ppermute(array, axis, [(i, i ^ by) for i in range(peers)])
+
+
+def cross(array, by):
+    peers = lax.axis_size("dp") * lax.axis_size("blk")
+    return lax.ppermute(array, ("dp", "blk"), [(i, i ^ by) for i in range(peers)])
+
+
+def after(array, *others):
+    return lax.optimization_barrier((array, *others))[0]
 
 
 def vm():
@@ -52,14 +60,16 @@
     nbytes = sum(a.size * a.dtype.itemsize for a in args) + sum(
         o.size * o.dtype.itemsize for o in outs
     )
+    nbytes = nbytes if flops else 1
     return pl.pallas_call(
         kernel,
+        name=getattr(kernel, "func", kernel).__name__,
         out_shape=outs,
         in_specs=specs,
         out_specs=[vm() for _ in outs],
         scratch_shapes=list(scratch),
         cost_estimate=pl.CostEstimate(
-            flops=flops // COST, bytes_accessed=nbytes // COST, transcendentals=0
+            flops=flops, bytes_accessed=nbytes, transcendentals=0
         ),
         compiler_params=pltpu.CompilerParams(vmem_limit_bytes=VMEM_LIMIT),
     )(*args)
@@ -103,9 +113,18 @@
     n_ref[...] = norm_stats(x_ref[...])[0].astype(BF16)
 
 
-def prep_kernel(tab, x_ref, w_ref, rows_ref, n_ref, panel_ref):
+def prep_kernel(tab, x_ref, w_ref, *rest):
+    vectors, (n_ref, panel_ref) = rest[:9], rest[9:]
     z = tab[1]
-    panel_ref[OWN:, :] = rows_ref[...]
+    rows = [v[...].astype(F32).reshape(1, v.shape[0]) for v in vectors]
+    panel_ref[OWN:, :] = jnp.concatenate(
+        [
+            jnp.concatenate(rows[:6], axis=1),
+            jnp.concatenate(rows[6:], axis=1),
+            jnp.zeros((14, 3 * HW), F32),
+        ],
+        axis=0,
+    ).astype(BF16)
     for k in range(ULY):
 
         @pl.when(z == k)
@@ -120,16 +139,12 @@
     return pl.ds(pl.multiple_of(index * QUART, 128), QUART)
 
 
-def ffn_prep_kernel(tab, u_ref, d_ref, a_ref, b_ref, turned):
+def ffn_prep_kernel(tab, u_ref, d_ref, *outs):
     b = tab[3]
-    for q in range(BLK):
-        part = d_ref[q * QUART : (q + 1) * QUART, :]
-        turned[q] = part.astype(F32).T.astype(BF16)
-    for s in range(BLK):
-        q = jnp.bitwise_xor(b, s)
-        ref = (a_ref, b_ref)[s // 2]
-        ref[s % 2, 0] = u_ref[:, quarter(q)]
-        ref[s % 2, 1] = turned[q]
+    for s, ref in enumerate(outs):
+        q = quarter(jnp.bitwise_xor(b, s))
+        ref[0] = u_ref[:, q]
+        ref[1] = d_ref[:, q]
 
 
 def qkv_kernel(owner_bits, tab, n0, n1, n2, n3, *rest):
@@ -222,14 +237,21 @@
         outs[i][...] = all_ref[i * ROWS : (i + 1) * ROWS, :]
 
 
-def mix_kernel(owner_bits, tab, a0, a1, a2, a3, x_ref, vv_ref, *rest):
-    arrays = rest[: len(owner_bits)]
-    resid_ref, h_ref, ow_ref = rest[len(owner_bits) :]
+def mix_kernel(plan, tab, a0, a1, a2, a3, x_ref, vv_ref, *rest):
+    parts, (resid_ref, h_ref, ow_ref, sems) = rest[:-4], rest[-4:]
     me, z = tab[0], tab[1]
-    for ref, bits in zip(arrays, owner_bits):
-        for i, bit in enumerate(bits):
-            ow_ref[rows_at(jnp.bitwise_xor(me, bit), OWN), :] = ref[i]
+    copies = []
+    for index, place, bit in plan:
+        copy = pltpu.make_async_copy(
+            parts[index].at[place],
+            ow_ref.at[rows_at(jnp.bitwise_xor(me, bit), OWN), :],
+            sems.at[len(copies)],
+        )
+        copy.start()
+        copies.append(copy)
     acc = x_ref[...] + vec(vv_ref, 0, 4 * OWN)
+    for copy in copies:
+        copy.wait()
     for j, ref in enumerate((a0, a1, a2, a3)):
         acc = acc + nn(ref[...], ow_ref[rows_at(jnp.bitwise_xor(z, j), HW), :])
     resid_ref[...] = acc
@@ -241,17 +263,17 @@
 
 
 def ffn_kernel(plan, tab, h0, h1, h2, h3, c0, c1, c2, c3, vv_ref, *rest):
-    count = 1 + max(index for index, _, _ in plan)
+    count = len(rest) - 16
     parts = rest[:count]
-    act_ref, dhid_ref, yo_ref, y1, y2, y3, go_ref, g1, g2, g3 = rest[count : count + 10]
-    u_ref, d_ref, hall, call_ref, bias_ref, yacc, gacc, sems = rest[count + 10 :]
+    act_ref, dhid_ref, ykeep, ysend, go_ref, g1, g2, g3 = rest[count : count + 8]
+    u_ref, d_ref, hall, call_ref, bias_ref, yacc, gacc, sems = rest[count + 8 :]
     me, b = tab[0], tab[3]
     copies = []
-    for index, slot, bit in plan:
+    for u_place, d_place, bit in plan:
         rows = rows_at(jnp.bitwise_xor(me, bit), OWN)
-        for k, target in enumerate((u_ref, d_ref)):
+        for (index, slot), target in ((u_place, u_ref), (d_place, d_ref)):
             copy = pltpu.make_async_copy(
-                parts[index].at[slot, k], target.at[rows, :], sems.at[len(copies)]
+                parts[index].at[slot], target.at[rows, :], sems.at[len(copies)]
             )
             copy.start()
             copies.append(copy)
@@ -281,22 +303,28 @@
         return carry
 
     lax.fori_loop(0, QUART // CHUNK, step, 0)
-    yo_ref[...] = yacc[:ROWS, :]
-    go_ref[...] = gacc[:ROWS, :]
-    for i, (y_ref, g_ref) in enumerate(((y1, g1), (y2, g2), (y3, g3)), 1):
-        rows = slice(i * ROWS, (i + 1) * ROWS)
-        y_ref[...] = yacc[rows, :].astype(BF16)
-        g_ref[...] = gacc[rows, :].astype(BF16)
-
-
-def ffn_grad_kernel(tab, r0, r1, r2, r3, right_ref, keep, send, left):
+    for i, y_ref in enumerate((ykeep, ysend, ykeep, ysend)):
+        y_ref[i // 2] = yacc[i * ROWS : (i + 1) * ROWS, :].astype(y_ref.dtype)
+    for i, g_ref in enumerate((go_ref, g1, g2, g3)):
+        g_ref[...] = gacc[i * ROWS : (i + 1) * ROWS, :].astype(g_ref.dtype)
+
+
+def ffn_grad_kernel(tab, *refs):
     me = tab[0]
-    for i, ref in enumerate((r0, r1, r2, r3)):
-        left[:, i * ROWS : (i + 1) * ROWS] = ref[...].T
-    for ref, base in ((send, 4), (keep, 0)):
-        for s in range(BLK):
-            o = jnp.bitwise_xor(me, base + s)
-            ref[s] = nn(left[rows_at(o, OWN), :], right_ref[...]).astype(BF16)
+    h_refs, c_refs = refs[:4], refs[4:8]
+    dhid_ref, act_ref, usend, ukeep, dthere, dhere, left, left2 = refs[8:]
+    for i in range(BLK):
+        left[:, i * ROWS : (i + 1) * ROWS] = h_refs[i][...].T
+        left2[:, i * ROWS : (i + 1) * ROWS] = c_refs[i][...].T
+    for source, right_ref, ref, bits in (
+        (left, dhid_ref, usend, (4, 5, 6, 7)),
+        (left, dhid_ref, ukeep, (0, 1, 2, 3)),
+        (left2, act_ref, dthere, (2, 6, 3, 7)),
+        (left2, act_ref, dhere, (0, 4, 1, 5)),
+    ):
+        for s, bit in enumerate(bits):
+            o = jnp.bitwise_xor(me, bit)
+            ref[s] = nn(source[rows_at(o, OWN), :], right_ref[...]).astype(BF16)
 
 
 def back_mix_kernel(
@@ -415,13 +443,15 @@
 
 
 def back_proj_kernel(
-    tab, dq_ref, keep, recv, w_ref, n0, n1, n2, n3, dproj_ref, h0, h1, h2, h3, vs_ref
+    tab, dq_ref, keep, got, recv, w_ref, n0, n1, n2, n3, dproj_ref, h0, h1, send, vs_ref
 ):
     dproj_ref[:, :HW] = dq_ref[...]
-    dproj_ref[:, HW:] = (keep[...].astype(F32) + recv[...].astype(F32)).astype(BF16)
+    total = keep[0].astype(F32) + got[0].astype(F32) + recv[...].astype(F32)
+    dproj_ref[:, HW:] = total.astype(BF16)
     gain = jnp.zeros((1, WIDTH), F32)
     shift = jnp.zeros((1, WIDTH), F32)
-    for i, (n_ref, out) in enumerate(((n0, h0), (n1, h1), (n2, h2), (n3, h3))):
+    outs = (h0, h1, send.at[0], send.at[1])
+    for i, (n_ref, out) in enumerate(zip((n0, n1, n2, n3), outs)):
         rows = slice(i * ROWS, (i + 1) * ROWS)
         grad = nt(dproj_ref[rows, :], w_ref[...])
         out[...] = grad.astype(out.dtype)
@@ -454,8 +484,8 @@
             ref[s, OWN:, :] = vrow[o]
 
 
-def back_norm_kernel(tab, x_ref, dres_ref, h0, h1, h2, h3, vv_ref, out_ref):
-    grad = h0[...] + h1[...].astype(F32) + h2[...].astype(F32) + h3[...].astype(F32)
+def back_norm_kernel(tab, x_ref, dres_ref, h0, got2, got1, vv_ref, out_ref):
+    grad = h0[...] + got2[0].astype(F32) + got1[...].astype(F32)
     n, r = norm_stats(x_ref[...])
     dn = grad * vec(vv_ref, 0, 0)
     out_ref[...] = dres_ref[...] + r * (
@@ -465,9 +495,14 @@
     )
 
 
-def output_kernel(tab, resid_ref, yo_ref, y1, y2, y3, vv_ref, out_ref):
-    got = y1[...].astype(F32) + y2[...].astype(F32) + y3[...].astype(F32)
-    out_ref[...] = resid_ref[...] + yo_ref[...] + got + vec(vv_ref, 1, OWN)
+def output_kernel(tab, resid_ref, keep, got, last, vv_ref, out_ref):
+    out_ref[...] = (
+        resid_ref[...]
+        + keep[0]
+        + got[0].astype(F32)
+        + last[...].astype(F32)
+        + vec(vv_ref, 1, OWN)
+    )
 
 
 def low_sum(a, b):
@@ -485,6 +520,21 @@
             high_out[1] = byc_ref[1]
 
 
+def pack_kernel(tab, a_ref, ac_ref, by_ref, byc_ref, out_ref):
+    for s, (ref, place) in enumerate(((a_ref, 1), (ac_ref, 3), (by_ref, 1), (byc_ref, 3))):
+        out_ref[s] = ref[place]
+
+
+def split_add_kernel(bit, tab, a_ref, ac_ref, by_ref, byc_ref, got, keep, send):
+    refs = ((a_ref, 0), (ac_ref, 2), (by_ref, 0), (byc_ref, 2))
+    for value, low_out, high_out in ((0, keep, send), (1, send, keep)):
+
+        @pl.when(tab[bit] == value)
+        def _():
+            for s, (ref, place) in enumerate(refs):
+                (low_out, high_out)[s // 2][s % 2] = low_sum(ref[place], got[s])
+
+
 def merge_kernel(bit, tab, a_ref, b_ref, keep, send):
     for value, low_out, high_out in ((0, keep, send), (1, send, keep)):
 
@@ -494,23 +544,16 @@
             high_out[...] = low_sum(a_ref[1], b_ref[1])
 
 
-def up_final_kernel(tab, p0, p1, p2, p3, out_ref):
+def final_kernel(tab, pair, got, out_ref):
     b, odd, high = tab[3], tab[4], tab[5]
-    for flip, ref in ((0, p0), (2, p1), (1, p2), (3, p3)):
+    for flip, ref in ((0, pair.at[0]), (1, pair.at[1]), (2, got.at[0]), (3, got.at[1])):
         q = jnp.bitwise_xor(jnp.bitwise_xor(b, 2 * odd + high), flip)
         out_ref[:, quarter(q)] = ref[...].astype(F32)
 
 
-def down_final_kernel(tab, p0, p1, p2, p3, out_ref):
-    b, odd, high = tab[3], tab[4], tab[5]
-    for flip, ref in ((0, p0), (1, p1), (2, p2), (3, p3)):
-        q = jnp.bitwise_xor(jnp.bitwise_xor(b, 2 * high + odd), flip)
-        out_ref[quarter(q), :] = ref[...].astype(F32).T
-
-
-def qkv_final_kernel(tab, p0, p1, p2, p3, out_ref, vec_ref):
+def qkv_final_kernel(tab, pair, got, out_ref, vec_ref):
     z = tab[1]
-    refs = (p0, p1, p2, p3)
+    refs = (pair.at[0], pair.at[1], got.at[0], got.at[1])
     for k in range(ULY):
 
         @pl.when(z == k)
@@ -574,44 +617,34 @@
     cot = cotangent.reshape(ROWS, WIDTH)
 
     if near:
-        row0 = jnp.concatenate(
-            [norm1_gain, norm1_bias, query_bias, value_bias, out_bias, norm2_gain]
-        )
-        row1 = jnp.concatenate([norm2_bias, down_bias, up_bias])
-        vec_rows = jnp.concatenate(
-            [row0[None], row1[None], jnp.zeros((14, 3 * HW), BF16)], axis=0
-        )
+        vectors = [norm1_gain, norm1_bias, query_bias, value_bias, out_bias, norm2_gain]
+        vectors += [norm2_bias, down_bias, up_bias]
         n0, panel = call(
             prep_kernel,
             [sds((ROWS, WIDTH), BF16), sds((PANEL, 3 * HW), BF16)],
-            [tab, x, qkv_weight, vec_rows],
+            [tab, x, qkv_weight, *vectors],
         )
-
-        def spread(array):
-            far = swap(array, "dp", 1)
-            near_y = swap(array, "blk", 2)
-            far_y = swap(far, "blk", 2)
-            direct = [array, near_y, far, far_y]
-            return direct + [swap(a, "blk", 1) for a in direct]
-
-        a_parts = [a[None] for a in spread(panel)]
-        o_parts = [a[None] for a in spread(out_weight)]
-        four_bits = [[0], [2], [4], [6], [1], [3], [5], [7]]
-        w_a, w_b = call(
+        n1, n2, n3 = (swap(n0, "uly", k) for k in (1, 2, 3))
+        a_0 = jnp.stack([panel, swap(panel, "dp", 1)])
+        a_2 = swap(a_0, "blk", 2)
+        four_bits = [[0, 4], [2, 6], [1, 5], [3, 7]]
+        w_mine = call(
             ffn_prep_kernel,
-            [sds((2, 2, OWN, QUART), BF16)] * 2,
-            [tab, up_weight, down_weight],
-            scratch=[pltpu.VMEM((BLK, OWN, QUART), BF16)],
+            [sds((2, OWN, QUART), BF16)] * BLK,
+            [tab, up_weight, down_weight.T],
         )
-        w_ax, w_bx = swap(w_a, "dp", 1), swap(w_b, "dp", 1)
-        w_by, w_bxy = swap(w_b, "blk", 2), swap(w_bx, "blk", 2)
-        w_parts = [w_a, w_by, w_ax, w_bxy]
-        w_parts = w_parts + [swap(a, "blk", 1) for a in w_parts]
-        w_plan = [
-            (0, 0, 0), (1, 0, 2), (2, 0, 4), (3, 0, 6), (4, 1, 1), (5, 1, 3), (6, 1, 5), (7, 1, 7)
+        n1 = after(n1, w_mine[0])
+        a_2c = swap(a_2, "blk", 1)
+        a_0c = swap(after(a_0, a_2c), "blk", 1)
+        a_parts = [a_0, a_2, a_0c, a_2c]
+        w_parts = [w_mine[0], None, cross(after(w_mine[2], a_0c), 2)] + [None] * 5
+        w_plan = [((i, 0), (i, 1), i) for i in range(OWNERS)]
+        o_plan = [
+            (i, k, bit) for i, bits in enumerate(four_bits) for k, bit in enumerate(bits)
         ]
     else:
         (n0,) = call(norm_kernel, [sds((ROWS, WIDTH), BF16)], [tab, x])
+        n1, n2, n3 = (swap(n0, "uly", k) for k in (1, 2, 3))
         qkv_cols = lax.dynamic_index_in_dim(
             qkv_weight.reshape(own_rows, 3, ULY, HW), z, axis=2, keepdims=False
         ).reshape(own_rows, 3 * HW)
@@ -647,9 +680,9 @@
         ]
         four_bits = [list(range(OWNERS))]
         o_parts = [full(out_weight).reshape(OWNERS, OWN, WIDTH)]
-        w_parts = [jnp.stack([mine(up_weight), mine(down_weight.T)], axis=1)]
-        w_plan = [(0, o, o) for o in range(OWNERS)]
-    n1, n2, n3 = (swap(n0, "uly", k) for k in (1, 2, 3))
+        w_parts = [mine(up_weight), mine(down_weight.T)]
+        w_plan = [((0, o), (1, o), o) for o in range(OWNERS)]
+        o_plan = [(0, o, o) for o in range(OWNERS)]
 
     ends = jnp.cumsum(doc_lengths.reshape(-1), dtype=jnp.int32)
     zs = jnp.arange(ULY, dtype=jnp.int32) ^ z
@@ -662,6 +695,9 @@
     kcode = jnp.where(valid > 0, kseg, kplace + 64)
     qcodes = jnp.stack([kseg[:GROUP], kplace[:GROUP] + 64])
 
+    n1, q_cols, q_rows, k_cols, k_rows = lax.optimization_barrier(
+        (n1, qcodes.T, qcodes, kcode[:, None], kcode[None, :])
+    )
     q, kv, h1, w_qkv, vv = call(
         functools.partial(qkv_kernel, four_bits),
         [
@@ -674,38 +710,66 @@
         [tab, n0, n1, n2, n3, *a_parts],
         flops=2 * GROUP * WIDTH * 3 * HW,
     )
-    kv_y = swap(kv, "blk", 2)
+    cb = cot.astype(BF16)
+    if near:
+        kv_y = swap(after(kv, w_parts[2]), "blk", 2)
+        cb_y = swap(after(cb, kv_y), "blk", 2)
+        w_parts[4] = cross(after(w_mine[0], kv), 4)
+        w_parts[5] = cross(after(w_mine[1], kv), 5)
+        o_0 = jnp.stack([out_weight, swap(after(out_weight, kv), "dp", 1)])
+        o_0c = swap(o_0, "blk", 1)
+        o_2 = swap(after(o_0, kv_y), "blk", 2)
+    else:
+        kv_y = swap(kv, "blk", 2)
     kv_c = swap(kv, "blk", 1)
     kv_yc = swap(kv_y, "blk", 1)
+    if near:
+        cb_c = swap(after(cb, kv), "blk", 1)
+        w_parts[1] = cross(after(w_mine[1], kv), 1)
+        kv_yc = after(kv_yc, o_0c, w_parts[1], cb_c)
     kvs = [kv, kv_c, kv_y, kv_yc]
+
+    def around(array):
+        near_y = swap(array, "blk", 2)
+        return [array, swap(array, "blk", 1), near_y, swap(near_y, "blk", 1)]
+
+    if near:
+        w_parts[3] = cross(after(w_mine[3], kv_y), 3)
+    else:
+        cbs = around(cb)
 
     *attn_slots, attn_all, lse = call(
         attend_kernel,
         [sds((ROWS, HW), BF16)] * ULY + [sds((GROUP, HW), BF16), sds((GROUP, 128), F32)],
-        [tab, q, *kvs, qcodes.T, kcode[None, :]],
+        [tab, q, *kvs, q_cols, k_rows],
         flops=4 * GROUP * KEYS * HW,
     )
+    if near:
+        attn_slots = after(attn_slots, w_parts[4], w_parts[5], o_2)
+        o_2c = swap(after(o_2, attn_slots[0]), "blk", 1)
+        o_parts = [o_0, o_2, o_0c, o_2c]
     attn = [attn_slots[0]] + [swap(attn_slots[k], "uly", k) for k in (1, 2, 3)]
-
     resid, h2, ow = call(
-        functools.partial(mix_kernel, four_bits),
+        functools.partial(mix_kernel, o_plan),
         [sds((ROWS, WIDTH), F32), sds((ROWS, WIDTH), BF16), sds((WIDTH, WIDTH), BF16)],
         [tab, *attn, x, vv, *o_parts],
+        scratch=[pltpu.SemaphoreType.DMA((OWNERS,))],
         flops=2 * ROWS * WIDTH * WIDTH,
-    )
-    cb = cot.astype(BF16)
-
-    def around(array):
-        near_y = swap(array, "blk", 2)
-        return [array, swap(array, "blk", 1), near_y, swap(near_y, "blk", 1)]
-
-    cbs = around(cb)
+        in_any=range(7, 7 + len(o_parts)),
+    )
+
+    if near:
+        w_parts[6] = cross(after(w_mine[2], attn[1]), 6)
+        w_parts[7] = cross(after(w_mine[3], attn[2], cb_y, w_parts[3]), 7)
+        h2 = after(h2, w_parts[6], w_parts[7])
+        cbs = [cb, cb_c, cb_y, swap(after(cb_y, h2), "blk", 1)]
     h2s = around(h2)
     parts = len(w_parts)
-    act, dhid, yo, *sums = call(
+    act, dhid, y_keep, y_send, go, *gs = call(
         functools.partial(ffn_kernel, w_plan),
         [sds((GROUP, QUART), BF16)] * 2
-        + ([sds((ROWS, WIDTH), F32)] + [sds((ROWS, WIDTH), BF16)] * 3) * 2,
+        + [sds((2, ROWS, WIDTH), F32), sds((2, ROWS, WIDTH), BF16), sds((ROWS, WIDTH), F32)]
+        + [sds((ROWS, WIDTH), BF16)] * 3,
         [tab, *h2s, *cbs, vv, *w_parts],
         scratch=[
             pltpu.VMEM((WIDTH, QUART), BF16),
@@ -720,10 +784,17 @@
         flops=8 * GROUP * WIDTH * QUART,
         in_any=range(10, 10 + parts),
     )
-    ys, go, gs = sums[:3], sums[3], sums[4:]
-    gs = [swap(g, "blk", k) for k, g in ((1, gs[0]), (2, gs[1]), (3, gs[2]))]
-    ys = [swap(y, "blk", k) for k, y in ((1, ys[0]), (2, ys[1]), (3, ys[2]))]
-    (output,) = call(output_kernel, [sds((ROWS, WIDTH), F32)], [tab, resid, yo, *ys, vv])
+    gs = [swap(g, "blk", k) for k, g in enumerate(gs, 1)]
+
+    y_got = swap(y_send, "blk", 1)
+    y_part = (y_keep[1] + y_got[1].astype(F32)).astype(BF16)
+    usend, ukeep, dthere, dhere = call(
+        ffn_grad_kernel,
+        [sds((BLK, OWN, QUART), BF16)] * 4,
+        [tab, *h2s, *cbs, dhid, act],
+        scratch=[pltpu.VMEM((WIDTH, GROUP), BF16)] * 2,
+    )
+    go = after(go, usend, dthere, y_part)
 
     dres, dmix, *dattn_slots, vs2 = call(
         back_mix_kernel,
@@ -733,43 +804,44 @@
         [tab, resid, cot, go, *gs, ow, vv],
         flops=2 * ROWS * WIDTH * WIDTH,
     )
+    pair = sds((2, OWN, QUART), BF16)
+    one = sds((OWN, QUART), BF16)
     dattn = [dattn_slots[0]] + [swap(dattn_slots[k], "uly", k) for k in (1, 2, 3)]
-
-    def panel_grad(rows, right):
-        return call(
-            ffn_grad_kernel,
-            [sds((BLK, OWN, QUART), BF16)] * 2,
-            [tab, *rows, right],
-            scratch=[pltpu.VMEM((WIDTH, GROUP), BF16)],
-            flops=2 * GROUP * WIDTH * QUART,
-        )
-
-    ukeep, usend = panel_grad(h2s, dhid)
-    dkeep, dsend = panel_grad(cbs, act)
+    if near:
+        u_got = swap(usend, "dp", 1)
+        d_there = swap(after(dthere, dmix), "blk", 2)
+    y_last = swap(after(y_part, dattn[1]), "blk", 2)
+
+    dq, keep_kv, send_kv = call(
+        back_attend_kernel,
+        [sds((GROUP, HW), BF16), sds((2, GROUP, 2 * HW), BF16), sds((2, GROUP, 2 * HW), BF16)],
+        [tab, q, *kvs, *dattn, attn_all, lse, q_rows, k_cols],
+        scratch=[pltpu.VMEM((BLK, GROUP, 2 * HW), F32), pltpu.VMEM((GROUP, HW), BF16)],
+        flops=10 * GROUP * KEYS * HW,
+    )
+    if near:
+        send_kv = after(send_kv, d_there, y_last)
+    got = swap(send_kv, "blk", 1)
+    kv_send = add_low(keep_kv[1], got[1])
+    kv_got = swap(kv_send, "blk", 2)
     okeep, osend = call(
         out_grad_kernel,
         [sds((4, PANEL, WIDTH), BF16)] * 2,
-        [tab, *attn, dmix, vs2, dhid, cb],
+        [tab, *attn, after(dmix, kv_send), vs2, dhid, cb],
         scratch=[pltpu.VMEM((WIDTH, ROWS), BF16), pltpu.VMEM((OWNERS, 16, WIDTH), BF16)],
-        flops=2 * ROWS * WIDTH * WIDTH,
-    )
-
-    dq, keep_kv, send_kv = call(
-        back_attend_kernel,
-        [sds((GROUP, HW), BF16), sds((2, GROUP, 2 * HW), BF16), sds((2, GROUP, 2 * HW), BF16)],
-        [tab, q, *kvs, *dattn, attn_all, lse, qcodes, kcode[:, None]],
-        scratch=[pltpu.VMEM((BLK, GROUP, 2 * HW), F32), pltpu.VMEM((GROUP, HW), BF16)],
-        flops=10 * GROUP * KEYS * HW,
-    )
-    got = swap(send_kv, "blk", 1)
-    kv_keep = add_low(keep_kv[0], got[0])
-    kv_got = swap(add_low(keep_kv[1], got[1]), "blk", 2)
-    dproj, g0, g1, g2, g3, vs1 = call(
+    )
+
+    if near:
+        dhere, d_there = after(dhere, kv_send), after(d_there, kv_send)
+        pieces = [dhere, swap(dhere, "blk", 1), d_there, swap(d_there, "blk", 1)]
+        (d_send,) = call(pack_kernel, [sds((BLK, OWN, QUART), BF16)], [tab, *pieces])
+        dq = after(dq, d_send, okeep)
+    dproj, g_own, g_one, g_send, vs1 = call(
         back_proj_kernel,
-        [sds((GROUP, 3 * HW), BF16), sds((ROWS, WIDTH), F32)]
-        + [sds((ROWS, WIDTH), BF16)] * 3
-        + [sds((8, WIDTH), F32)],
-        [tab, dq, kv_keep, kv_got, w_qkv, n0, n1, n2, n3],
+        [sds((GROUP, 3 * HW), BF16)]
+        + [sds((ROWS, WIDTH), F32)] * 2
+        + [sds((2, ROWS, WIDTH), BF16), sds((8, WIDTH), F32)],
+        [tab, dq, keep_kv, got, kv_got, w_qkv, n0, n1, n2, n3],
         flops=2 * GROUP * WIDTH * 3 * HW,
     )
     qkeep, qsend = call(
@@ -777,55 +849,69 @@
         [sds((4, PANEL, 3 * HW), BF16)] * 2,
         [tab, h1, dproj, vs1],
         scratch=[pltpu.VMEM((WIDTH, GROUP), BF16), pltpu.VMEM((OWNERS, 16, 3 * HW), BF16)],
-        flops=2 * GROUP * WIDTH * 3 * HW,
-    )
-    g1, g2, g3 = (swap(g, "uly", k) for k, g in ((1, g1), (2, g2), (3, g3)))
-    (grad_inputs,) = call(
-        back_norm_kernel, [sds((ROWS, WIDTH), F32)], [tab, x, dres, g0, g1, g2, g3, vv]
-    )
-
+    )
+    (output,) = call(
+        output_kernel,
+        [sds((ROWS, WIDTH), F32)],
+        [tab, after(resid, dproj), y_keep, y_got, y_last, vv],
+    )
     if near:
-        def owned_panel(keep, send, first, second, final, shape):
-            got = swap(send, "dp", 1)
-            there = add_low(keep[2:], got[2:])
-            here = add_low(keep[:2], got[:2])
-            there = swap(there, "blk", 2)
-            pieces = [here, swap(here, "blk", 1), there, swap(there, "blk", 1)]
-            pair = sds((2, OWN, QUART), BF16)
-            one = sds((OWN, QUART), BF16)
-            steps = {1: 4, 2: 5}
-            kept, sent = call(
-                functools.partial(split_kernel, steps[first]), [pair] * 2, [tab, *pieces]
+        o1 = add_low(okeep, swap(after(osend, dproj), "blk", 1))
+        u_got = after(u_got, dproj)
+        u_there = add_low(ukeep[2:], u_got[2:])
+        u_here = add_low(ukeep[:2], u_got[:2])
+        q1 = add_low(qkeep, swap(qsend, "blk", 1))
+        u_there = swap(u_there, "blk", 2)
+        upieces = [u_here, swap(u_here, "blk", 1), u_there, swap(u_there, "blk", 1)]
+        ukept, usent = call(functools.partial(split_kernel, 4), [pair] * 2, [tab, *upieces])
+        dkept, dsent = call(
+            functools.partial(split_add_kernel, 4),
+            [pair] * 2,
+            [tab, *pieces, after(swap(d_send, "dp", 1), dproj)],
+        )
+        gates = [q1, dsent, usent]
+    else:
+        gates = []
+    g_got = after(swap(g_send, "uly", 2), *gates)
+    g_last = swap((g_one + g_got[1].astype(F32)).astype(BF16), "uly", 1)
+    if near:
+
+        def over_uly(kept, sent):
+            return call(
+                functools.partial(merge_kernel, 5),
+                [one] * 2,
+                [tab, kept, after(swap(sent, "uly", 1), g_got)],
             )
-            kept, sent = call(
-                functools.partial(merge_kernel, steps[second]),
-                [one] * 2,
-                [tab, kept, swap(sent, "uly", first)],
-            )
-            total = add_low(kept, swap(sent, "uly", second))
-            two = swap(total, "uly", 2)
-            sums = [total, swap(total, "uly", 1), two, swap(two, "uly", 1)]
-            return call(final, [sds(shape, F32)], [tab, *sums])[0]
-
-        grad_up = owned_panel(ukeep, usend, 1, 2, up_final_kernel, (OWN, FF))
-        grad_down = owned_panel(dkeep, dsend, 2, 1, down_final_kernel, (FF, OWN))
-
-        o1 = add_low(okeep, swap(osend, "blk", 1))
+
+        def share(total):
+            pair = jnp.stack([total, swap(total, "uly", 2)])
+            return call(
+                final_kernel, [sds((OWN, FF), F32)], [tab, pair, swap(pair, "uly", 1)]
+            )[0]
+
+        dkept, dsent = over_uly(dkept, dsent)
+        ukept, usent = over_uly(ukept, usent)
+        d_total = add_low(dkept, swap(dsent, "uly", 2))
+        u_total = add_low(ukept, swap(usent, "uly", 2))
+        g_last = after(g_last, d_total, usent, output)
+        grad_down = share(d_total).T
+        grad_up = share(u_total)
+
         o2 = add_low(o1[:2], swap(o1[2:], "blk", 2))
         o3 = add_low(o2[0], swap(o2[1], "dp", 1))
-        o4 = add_low(o3, swap(o3, "uly", 1))
+        o4 = add_low(o3, swap(after(o3, d_total), "uly", 1))
         o5 = o4.astype(F32) + swap(o4, "uly", 2).astype(F32)
         grad_ow = o5[:OWN]
         grad_obias, grad_gain2, grad_shift2 = (o5[OWN, k * OWN : (k + 1) * OWN] for k in range(3))
         grad_ubias, grad_dbias = o5[OWN, 288:672], o5[OWN, 672:768]
 
-        q1 = add_low(qkeep, swap(qsend, "blk", 1))
         q2 = add_low(q1[:2], swap(q1[2:], "blk", 2))
         q3 = add_low(q2[0], swap(q2[1], "dp", 1))
+        q_pair = jnp.stack([q3, swap(q3, "uly", 1)])
         grad_qkv, qvec = call(
             qkv_final_kernel,
             [sds((OWN, 3 * WIDTH), F32), sds((8, 3 * HW), F32)],
-            [tab, q3] + [swap(q3, "uly", k) for k in (1, 2, 3)],
+            [tab, q_pair, swap(q_pair, "uly", 2)],
         )
         grad_gain1, grad_shift1, grad_qbias, grad_vbias = (
             qvec[0, k * OWN : (k + 1) * OWN] for k in range(4)
@@ -845,13 +931,14 @@
         o8 = by_owner(okeep, osend, [0, 4, 2, 6, 1, 5, 3, 7])
         q8 = by_owner(qkeep, qsend, [0, 4, 2, 6, 1, 5, 3, 7])
 
-        def widen(keep, send):
-            flat = jnp.concatenate([keep, send], axis=0).reshape(WIDTH, 1, QUART)
+        def widen(keep, send, order):
+            flat = jnp.concatenate([keep, send], axis=0)[jnp.array(order)]
+            flat = flat.reshape(WIDTH, 1, QUART)
             place = (jnp.arange(BLK) == b)[None, :, None]
             return jnp.where(place, flat, jnp.zeros_like(flat)).reshape(WIDTH, FF)
 
-        grad_up = owned(widen(ukeep, usend))
-        grad_down = owned(widen(dkeep, dsend)).T
+        grad_up = owned(widen(ukeep, usend, range(OWNERS)))
+        grad_down = owned(widen(dhere, dthere, [0, 2, 4, 6, 1, 3, 5, 7])).T
         grad_ubias = owned(o8[:, OWN, 288:672].reshape(FF))
         grad_dbias = owned(o8[:, OWN, 672:768].reshape(WIDTH))
         grad_ow = owned(o8[:, :OWN].reshape(WIDTH, WIDTH))
@@ -867,6 +954,9 @@
             owned(q8[:, OWN, k * OWN : (k + 1) * OWN].reshape(WIDTH)) for k in range(4)
         )
 
+    (grad_inputs,) = call(
+        back_norm_kernel, [sds((ROWS, WIDTH), F32)], [tab, x, dres, g_own, g_got, g_last, vv]
+    )
     return (
         output.reshape(inputs.shape),
         grad_inputs.reshape(inputs.shape),

time: 279 us -> 272 us (0.975)
  starting transfers between devices: 69.4 us -> 64 us
  local copies, waits for them, and re-layouts: 22 us -> 17.1 us
  other arithmetic: 7.26 us -> 10.3 us
    ppermute x80 -> x61, starting transfers between devices: 69.4 us -> 57.8 us  [swap(): return lax.ppermute(array, axis, [(i, i ^ by) for i in range(peers)])]
    ppermute x0 -> x7, starting transfers between devices: none -> 6.22 us  [cross(): lax.ppermute(array, ('dp', 'blk'), [(i, i ^ by) for i in range(peers)])]
    ppermute x80 -> x61, waiting for transfers between devices: 88.9 us -> 84.7 us  [swap(): return lax.ppermute(array, axis, [(i, i ^ by) for i in range(peers)])]
    concatenate x2 -> x0, local copies, waits for them, and re-layouts: 4.24 us -> none  [the longest x1 4.16 us: body(): jnp.concatenate([norm1_gain, norm1_bias, query_bias, value_bias, out_bias...]
    unnamed x178 -> x134, local copies, waits for them, and re-layouts: 11.1 us -> 10.3 us
  transfers between devices with their start and end apart: 80 -> 68, of which waited for: 27 -> 30; matrix products, arithmetic and copies ran while one was open for 5% -> 5% of each run, Pallas kernels for 27% -> 28%
where the time goes in v1:
time: 272 us; the launch traced here: 271 us
  Pallas kernels  90.7 us (33%)
  waiting for transfers between devices  87.4 us (32%)
  starting transfers between devices  64 us (24%)
  local copies, waits for them, and re-layouts  17.1 us (6%)
  other arithmetic  10.3 us (4%)
    pallas_call x22, Pallas kernels, call(): pl.pallas_call(kernel, name=getattr(kernel, 'func', kernel).__name__, out...  90.7 us
    ppermute x61, waiting for transfers between devices, swap(): return lax.ppermute(array, axis, [(i, i ^ by) for i in range(peers)])  84.7 us
    ppermute x61, starting transfers between devices, swap(): return lax.ppermute(array, axis, [(i, i ^ by) for i in range(peers)])  57.8 us
    unnamed x134, local copies, waits for them, and re-layouts  10.3 us
    ppermute x7, starting transfers between devices, cross(): lax.ppermute(array, ('dp', 'blk'), [(i, i ^ by) for i in range(peers)])  6.22 us
  transfers between devices with their start and end apart: 68, of which 30 were waited for; matrix products, arithmetic and copies ran while one was open for 5% of the time, Pallas kernels for 28%

profile of v1, /device:TPU:0, one launch (start us, length us, event | category | flops | bytes accessed | tf_op | source)
XLA Modules:
  0.0 271.1 jit_solution(1145256777579028800)
XLA Ops:
  3.6 3.1 %collective-permute-start = (bf16[128,768]{1,0:T(8,128)(2,1)}, bf16[128,768]{1,0:T(8,128)(2,1)S(1)}, u32[]{:S(2)}, u32[]{:S(2)}) collective-permute-start(bf16[128,768]{1,0:T(8,128)(2,1)} %get-tuple-element.119.n0), channel_id=1, source_target_pairs={{0,4},{4,0},{8,12},{12,8},{1,5},{5,1},{9,13},{13,9},{2,6},{6,2},{1... | collective-permute-start | bytes 589832 | tf_op jit(solution)/shard_map/ppermute | solution.py:34
  17.3 5.4 %collective-permute-done.4.rest_1_ = bf16[2,112,576]{2,1,0:T(8,128)(2,1)S(1)} collective-permute-done((bf16[2,112,576]{2,1,0:T(8,128)(2,1)S(1)}, bf16[2,112,576]{2,1,0:T(8,128)(2,1)S(1)}, u32[]{:S(2)}, u32[]{:S(2)}) %collective-permute-start.4) | collective-permute-done | bytes 258080 | tf_op jit(solution)/shard_map/ppermute | solution.py:34
  35.0 3.5 %qkv_kernel.1 = (bf16[512,192]{1,0:T(8,128)(2,1)}, bf16[512,384]{1,0:T(8,128)(2,1)}, bf16[512,768]{1,0:T(8,128)(2,1)}, bf16[768,576]{1,0:T(8,128)(2,1)}, bf16[8,16,576]{2,1,0:T(8,128)(2,1)}) custom-call(s32[6]{0:T(128)} %stack.79.tab, bf16[128,768]{1,0:T(8,128)(2,1)} %get-tuple-element.119.n0, bf16[128,768]{1,0:T(8,128)(2,1)} %copy-done.16, ...), custom_call_target="tpu_custom_call" | custom-call | flops 452984832 | bytes 4227096 | tf_op jit(solution)/shard_map/qkv_kernel/pallas_call | solution.py:64
  41.1 3.6 %collective-permute-done.11 = bf16[96,768]{1,0:T(8,128)(2,1)S(1)} collective-permute-done((bf16[96,768]{1,0:T(8,128)(2,1)S(1)}, bf16[96,768]{1,0:T(8,128)(2,1)S(1)}, u32[]{:S(2)}, u32[]{:S(2)}) %collective-permute-start.11) | collective-permute-done | bytes 147488 | tf_op jit(solution)/shard_map/ppermute | solution.py:34
  44.8 5.1 %collective-permute-done.9.k2 = bf16[512,384]{1,0:T(8,128)(2,1)S(1)} collective-permute-done((bf16[512,384]{1,0:T(8,128)(2,1)}, bf16[512,384]{1,0:T(8,128)(2,1)S(1)}, u32[]{:S(2)}, u32[]{:S(2)}) %collective-permute-start.9) | collective-permute-done | bytes 393248 | tf_op jit(solution)/shard_map/ppermute | solution.py:34
  56.7 9.7 %attend_kernel.1 = (bf16[128,192]{1,0:T(8,128)(2,1)}, bf16[128,192]{1,0:T(8,128)(2,1)}, bf16[128,192]{1,0:T(8,128)(2,1)}, bf16[128,192]{1,0:T(8,128)(2,1)}, bf16...) custom-call(s32[6]{0:T(128)} %stack.79.tab, bf16[512,192]{1,0:T(8,128)(2,1)} %get-tuple-element.125.q_ref, ...), custom_call_target="tpu_custom_call" | custom-call | flops 805306368 | bytes 2437144 | tf_op jit(solution)/shard_map/attend_kernel/pallas_call | solution.py:64
  69.2 3.5 %collective-permute-start.19 = (bf16[128,192]{1,0:T(8,128)(2,1)}, bf16[128,192]{1,0:T(8,128)(2,1)S(1)}, u32[]{:S(2)}, u32[]{:S(2)}) collective-permute-start(bf16[128,192]{1,0:T(8,128)(2,1)} %get-tuple-element.145), channel_id=1, source_target_pairs={{0,8},{4,12},{8,0},{12,4},{1,9},{5,13},{9,1},{13,5},{2,10},{6,14},... | collective-permute-start | bytes 147464 | tf_op jit(solution)/shard_map/ppermute | solution.py:34
  76.1 3.0 %collective-permute-start.20 = (bf16[128,192]{1,0:T(8,128)(2,1)}, bf16[128,192]{1,0:T(8,128)(2,1)S(1)}, u32[]{:S(2)}, u32[]{:S(2)}) collective-permute-start(bf16[128,192]{1,0:T(8,128)(2,1)} %get-tuple-element.146), channel_id=1, source_target_pairs={{0,12},{4,8},{8,4},{12,0},{1,13},{5,9},{9,5},{13,1},{2,14},{6,10},... | collective-permute-start | bytes 147464 | tf_op jit(solution)/shard_map/ppermute | solution.py:34
  79.1 3.3 %collective-permute-done.20.a3 = bf16[128,192]{1,0:T(8,128)(2,1)S(1)} collective-permute-done((bf16[128,192]{1,0:T(8,128)(2,1)}, bf16[128,192]{1,0:T(8,128)(2,1)S(1)}, u32[]{:S(2)}, u32[]{:S(2)}) %collective-permute-start.20) | collective-permute-done | bytes 49184 | tf_op jit(solution)/shard_map/ppermute | solution.py:34
  83.1 4.2 %mix_kernel.1 = (f32[128,768]{1,0:T(8,128)}, bf16[128,768]{1,0:T(8,128)(2,1)}, bf16[768,768]{1,0:T(8,128)(2,1)}) custom-call(s32[6]{0:T(128)} %stack.79.tab, bf16[128,192]{1,0:T(8,128)(2,1)} %get-tuple-element.143.a0, bf16[128,192]{1,0:T(8,128)(2,1)} %copy-done.37, bf16[128,192]{1,0:T(8,128)(2,1)} %copy-done.38, bf16[128,192]{1,0:T(8,128)(2,1)} %copy-done.39, ...), custom_call_target="tpu_custom_call" | custom-call | flops 150994944 | bytes 3686424 | tf_op jit(solution)/shard_map/mix_kernel/pallas_call | solution.py:64
  89.8 6.6 %collective-permute-done.27.h2.refs_2_ = bf16[128,768]{1,0:T(8,128)(2,1)S(1)} collective-permute-done((bf16[128,768]{1,0:T(8,128)(2,1)}, bf16[128,768]{1,0:T(8,128)(2,1)S(1)}, u32[]{:S(2)}, u32[]{:S(2)}) %collective-permute-start.27) | collective-permute-done | bytes 196640 | tf_op jit(solution)/shard_map/ppermute | solution.py:34
  98.6 8.4 %ffn_kernel.1 = (bf16[512,768]{1,0:T(8,128)(2,1)}, bf16[512,768]{1,0:T(8,128)(2,1)}, f32[2,128,768]{2,1,0:T(8,128)}, bf16[2,128,768]{2,1,0:T(8,128)(2,1)}, f32[1...) custom-call(s32[6]{0:T(128)} %stack.79.tab, ...), custom_call_target="tpu_custom_call" | custom-call | flops 2415919104 | bytes 7815192 | tf_op jit(solution)/shard_map/ffn_kernel/pallas_call | solution.py:64
  109.0 5.2 %ffn_grad_kernel.1 = (bf16[4,96,768]{2,1,0:T(8,128)(2,1)}, bf16[4,96,768]{2,1,0:T(8,128)(2,1)}, bf16[4,96,768]{2,1,0:T(8,128)(2,1)}, bf16[4,96,768]{2,1,0:T(8,128)(2,1)}) custom-call(s32[6]{0:T(128)} %stack.79.tab, bf16[128,768]{1,0:T(8,128)(2,1)} %get-tuple-element.156.h0.refs_0_, bf16[128,768]{1,0:T(8,128)(2,1)} %copy-done.48, ...), custom_call_target="tpu_custom_call" | custom-call | bytes 1 | tf_op jit(solution)/shard_map/ffn_grad_kernel/pallas_call | solution.py:64
  118.7 3.4 %back_mix_kernel.1 = (f32[128,768]{1,0:T(8,128)}, bf16[128,768]{1,0:T(8,128)(2,1)}, bf16[128,192]{1,0:T(8,128)(2,1)}, bf16[128,192]{1,0:T(8,128)(2,1)}, bf16[128...) custom-call(s32[6]{0:T(128)} %stack.79.tab, f32[128,768]{1,0:T(8,128)} %get-tuple-element.194.resid_ref, ...), custom_call_target="tpu_custom_call" | custom-call | flops 150994944 | bytes 3907608 | tf_op jit(solution)/shard_map/back_mix_kernel/pallas_call | solution.py:64
  122.7 3.1 %collective-permute-start.35 = (bf16[128,192]{1,0:T(8,128)(2,1)}, bf16[128,192]{1,0:T(8,128)(2,1)S(1)}, u32[]{:S(2)}, u32[]{:S(2)}) collective-permute-start(bf16[128,192]{1,0:T(8,128)(2,1)} %get-tuple-element.172), channel_id=1, source_target_pairs={{0,8},{4,12},{8,0},{12,4},{1,9},{5,13},{9,1},{13,5},{2,10},{6,14},... | collective-permute-start | bytes 147464 | tf_op jit(solution)/shard_map/ppermute | solution.py:34
  132.7 18.2 %back_attend_kernel.1 = (bf16[512,192]{1,0:T(8,128)(2,1)}, bf16[2,512,384]{2,1,0:T(8,128)(2,1)}, bf16[2,512,384]{2,1,0:T(8,128)(2,1)}) custom-call(s32[6]{0:T(128)} %stack.79.tab, bf16[512,192]{1,0:T(8,128)(2,1)} %get-tuple-element.125.q_ref, bf16[512,384]{1,0:T(8,128)(2,1)} %get-tuple-element.129.k0, bf16[512,384]{1,0:T(8,128)(2,1)} %copy-done.57, ...), custom_call_target="tpu_custom_call" | custom-call | flops 2013265920 | bytes 4206616 | tf_op jit(solution)/shard_map/back_attend_kernel/pallas_call | solution.py:64
  158.7 3.1 %out_grad_kernel.1 = (bf16[4,112,768]{2,1,0:T(8,128)(2,1)}, bf16[4,112,768]{2,1,0:T(8,128)(2,1)}) custom-call(s32[6]{0:T(128)} %stack.79.tab, bf16[128,192]{1,0:T(8,128)(2,1)} %get-tuple-element.143.a0, bf16[128,192]{1,0:T(8,128)(2,1)} %copy-done.37, bf16[128,192]{1,0:T(8,128)(2,1)} %copy-done.38, bf16[128,192]{1,0:T(8,128)(2,1)} %copy-done.39, ...), custom_call_target="tpu_custom_call" | custom-call | bytes 1 | tf_op jit(solution)/shard_map/out_grad_kernel/pallas_call | solution.py:64
  168.4 4.4 %back_proj_kernel.1 = (bf16[512,576]{1,0:T(8,128)(2,1)}, f32[128,768]{1,0:T(8,128)}, f32[128,768]{1,0:T(8,128)}, bf16[2,128,768]{2,1,0:T(8,128)(2,1)}, f32[8,768]{1,0:T(8,128)}) custom-call(s32[6]{0:T(128)} %stack.79.tab, bf16[512,192]{1,0:T(8,128)(2,1)} %get-tuple-element.191.dq_ref, bf16[2,512,384]{2,1,0:T(8,128)(2,1)} %get-tuple-element.180.keep, ...), custom_call_target="tpu_custom_call" | custom-call | flops 452984832 | bytes 5627928 | tf_op jit(solution)/shard_map/back_proj_kernel/pallas_call | solution.py:64
  172.7 3.6 %qkv_grad_kernel.1 = (bf16[4,112,576]{2,1,0:T(8,128)(2,1)}, bf16[4,112,576]{2,1,0:T(8,128)(2,1)}) custom-call(s32[6]{0:T(128)} %stack.79.tab, bf16[512,768]{1,0:T(8,128)(2,1)} %get-tuple-element.198.h_ref, bf16[512,576]{1,0:T(8,128)(2,1)} %get-tuple-element.193.dproj_ref, f32[8,768]{1,0:T(8,128)} %get-tuple-element.199.vs_ref), custom_call_target="tpu_custom_call" | custom-call | bytes 1 | tf_op jit(solution)/shard_map/qkv_grad_kernel/pallas_call | solution.py:64
  180.1 6.0 %collective-permute-done.48.by_ref = bf16[2,96,768]{2,1,0:T(8,128)(2,1)S(1)} collective-permute-done((bf16[2,96,768]{2,1,0:T(8,128)(2,1)S(1)}, bf16[2,96,768]{2,1,0:T(8,128)(2,1)S(1)}, u32[]{:S(2)}, u32[]{:S(2)}) %collective-permute-start.48) | collective-permute-done | bytes 294944 | tf_op jit(solution)/shard_map/ppermute | solution.py:34
  208.8 5.4 %collective-permute-done.53.b_ref = bf16[2,96,768]{2,1,0:T(8,128)(2,1)S(1)} collective-permute-done((bf16[2,96,768]{2,1,0:T(8,128)(2,1)}, bf16[2,96,768]{2,1,0:T(8,128)(2,1)S(1)}, u32[]{:S(2)}, u32[]{:S(2)}) %collective-permute-start.53) | collective-permute-done | bytes 294944 | tf_op jit(solution)/shard_map/ppermute | solution.py:34
  226.9 9.6 %collective-permute-done.63 = bf16[96,768]{1,0:T(8,128)(2,1)S(1)} collective-permute-done((bf16[96,768]{1,0:T(8,128)(2,1)}, bf16[96,768]{1,0:T(8,128)(2,1)S(1)}, u32[]{:S(2)}, u32[]{:S(2)}) %collective-permute-start.63) | collective-permute-done | bytes 147488 | tf_op jit(solution)/shard_map/ppermute | solution.py:34
  240.0 9.6 %collective-permute-done.64 = bf16[96,768]{1,0:T(8,128)(2,1)S(1)} collective-permute-done((bf16[96,768]{1,0:T(8,128)(2,1)S(1)}, bf16[96,768]{1,0:T(8,128)(2,1)S(1)}, u32[]{:S(2)}, u32[]{:S(2)}) %collective-permute-start.64) | collective-permute-done | bytes 147488 | tf_op jit(solution)/shard_map/ppermute | solution.py:34
  256.9 4.8 %collective-permute-done.67.got = bf16[2,96,768]{2,1,0:T(8,128)(2,1)S(1)} collective-permute-done((bf16[2,96,768]{2,1,0:T(8,128)(2,1)S(1)}, bf16[2,96,768]{2,1,0:T(8,128)(2,1)S(1)}, u32[]{:S(2)}, u32[]{:S(2)}) %collective-permute-start.67) | collective-permute-done | bytes 294944 | tf_op jit(solution)/shard_map/ppermute | solution.py:34
  (317 shorter events, 133.7 us)
Async XLA Ops:
  3.6 30.0 %collective-permute-start = (bf16[128,768]{1,0:T(8,128)(2,1)}, bf16[128,768]{1,0:T(8,128)(2,1)S(1)}, u32[]{:S(2)}, u32[]{:S(2)}) collective-permute-start(bf16[128,768]{1,0:T(8,128)(2,1)} %get-tuple-element.119.n0), channel_id=1, source_target_pairs={{0,4},{4,0},{8,12},{12,8},{1,5},{5,1},{9,13},{13,9},{2,6},{6,2},{1... | collective-permute-start | bytes 589832 | tf_op jit(solution)/shard_map/ppermute | solution.py:34
  6.7 26.9 %collective-permute-start.1 = (bf16[128,768]{1,0:T(8,128)(2,1)}, bf16[128,768]{1,0:T(8,128)(2,1)S(1)}, u32[]{:S(2)}, u32[]{:S(2)}) collective-permute-start(bf16[128,768]{1,0:T(8,128)(2,1)} %get-tuple-element.119.n0), channel_id=1, source_target_pairs={{0,8},{4,12},{8,0},{12,4},{1,9},{5,13},{9,1},{13,5},{2,10},{6,14},... | collective-permute-start | bytes 589832 | tf_op jit(solution)/shard_map/ppermute | solution.py:34
  9.3 24.4 %collective-permute-start.2 = (bf16[128,768]{1,0:T(8,128)(2,1)}, bf16[128,768]{1,0:T(8,128)(2,1)S(1)}, u32[]{:S(2)}, u32[]{:S(2)}) collective-permute-start(bf16[128,768]{1,0:T(8,128)(2,1)} %get-tuple-element.119.n0), channel_id=1, source_target_pairs={{0,12},{4,8},{8,4},{12,0},{1,13},{5,9},{9,5},{13,1},{2,14},{6,10},... | collective-permute-start | bytes 589832 | tf_op jit(solution)/shard_map/ppermute | solution.py:34
  51.9 15.9 %collective-permute-start.16 = (bf16[2,96,768]{2,1,0:T(8,128)(2,1)}, bf16[2,96,768]{2,1,0:T(8,128)(2,1)S(1)}, u32[]{:S(2)}, u32[]{:S(2)}) collective-permute-start(bf16[2,96,768]{2,1,0:T(8,128)(2,1)} %get-tuple-element.132), channel_id=1, source_target_pairs={{0,17},{1,16},{2,19},{3,18},{16,1},{17,0},{18,3},{19,2},{4,21},{5,... | collective-permute-start | bytes 884744 | tf_op jit(solution)/shard_map/ppermute | solution.py:39
  54.2 20.3 %collective-permute-start.24 = (bf16[2,96,768]{2,1,0:T(8,128)(2,1)}, bf16[2,96,768]{2,1,0:T(8,128)(2,1)}, u32[]{:S(2)}, u32[]{:S(2)}) collective-permute-start(bf16[2,96,768]{2,1,0:T(8,128)(2,1)} %get-tuple-element.155), channel_id=1, source_target_pairs={{0,3},{1,2},{2,1},{3,0},{16,19},{17,18},{18,17},{19,16},{4,7},{5,6... | collective-permute-start | bytes 884744 | tf_op jit(solution)/shard_map/ppermute | solution.py:39
  55.2 19.4 %collective-permute-start.23 = (bf16[128,768]{1,0:T(8,128)(2,1)S(1)}, bf16[128,768]{1,0:T(8,128)(2,1)S(1)}, u32[]{:S(2)}, u32[]{:S(2)}) collective-permute-start(bf16[128,768]{1,0:T(8,128)(2,1)S(1)} %bitcast_convert_fusion.c0.refs_4_.c_ref), channel_id=1, source_target_pairs={{0,2},{1,3},{2,0},{3,1},{4,6},{5,7},{6,4},{7,5},{8,10},{9,11},{10,... | collective-permute-start | bytes 589832 | tf_op jit(solution)/shard_map/ppermute | solution.py:34
  122.1 28.8 %collective-permute-start.37 = (bf16[4,96,768]{2,1,0:T(8,128)(2,1)S(1)}, bf16[4,96,768]{2,1,0:T(8,128)(2,1)S(1)}, u32[]{:S(2)}, u32[]{:S(2)}) collective-permute-start(bf16[4,96,768]{2,1,0:T(8,128)(2,1)S(1)} %copy-done.55), channel_id=1, source_target_pairs={{0,2},{1,3},{2,0},{3,1},{4,6},{5,7},{6,4},{7,5},{8,10},{9,11},{10,... | collective-permute-start | bytes 1769480 | tf_op jit(solution)/shard_map/ppermute | solution.py:34
  128.4 22.6 %collective-permute-start.38 = (bf16[128,768]{1,0:T(8,128)(2,1)S(1)}, bf16[128,768]{1,0:T(8,128)(2,1)S(1)}, u32[]{:S(2)}, u32[]{:S(2)}) collective-permute-start(bf16[128,768]{1,0:T(8,128)(2,1)S(1)} %fusion.4), channel_id=1, source_target_pairs={{0,2},{1,3},{2,0},{3,1},{4,6},{5,7},{6,4},{7,5},{8,10},{9,11},{10,... | collective-permute-start | bytes 589832 | tf_op jit(solution)/shard_map/ppermute | solution.py:34
  156.1 20.2 %collective-permute-start.46 = (bf16[4,96,768]{2,1,0:T(8,128)(2,1)}, bf16[4,96,768]{2,1,0:T(8,128)(2,1)S(1)}, u32[]{:S(2)}, u32[]{:S(2)}) collective-permute-start(bf16[4,96,768]{2,1,0:T(8,128)(2,1)} %get-tuple-element.161), channel_id=1, source_target_pairs={{0,16},{16,0},{1,17},{17,1},{2,18},{18,2},{3,19},{19,3},{4,20},{20... | collective-permute-start | bytes 1769480 | tf_op jit(solution)/shard_map/ppermute | solution.py:34
  165.9 24.3 %collective-permute-start.45 = (bf16[4,96,768]{2,1,0:T(8,128)(2,1)}, bf16[4,96,768]{2,1,0:T(8,128)(2,1)S(1)}, u32[]{:S(2)}, u32[]{:S(2)}) collective-permute-start(bf16[4,96,768]{2,1,0:T(8,128)(2,1)} %pack_kernel.1), channel_id=1, source_target_pairs={{0,16},{16,0},{1,17},{17,1},{2,18},{18,2},{3,19},{19,3},{4,20},{20... | collective-permute-start | bytes 1769480 | tf_op jit(solution)/shard_map/ppermute | solution.py:34
  176.3 22.7 %collective-permute-start.58 = (bf16[4,112,768]{2,1,0:T(8,128)(2,1)}, bf16[4,112,768]{2,1,0:T(8,128)(2,1)S(1)}, u32[]{:S(2)}, u32[]{:S(2)}) collective-permute-start(bf16[4,112,768]{2,1,0:T(8,128)(2,1)} %get-tuple-element.220), channel_id=1, source_target_pairs={{0,1},{1,0},{2,3},{3,2},{4,5},{5,4},{6,7},{7,6},{8,9},{9,8},{10,11... | collective-permute-start | bytes 2064392 | tf_op jit(solution)/shard_map/ppermute | solution.py:34
  178.6 20.4 %collective-permute-start.43 = (bf16[2,128,768]{2,1,0:T(8,128)(2,1)}, bf16[2,128,768]{2,1,0:T(8,128)(2,1)S(1)}, u32[]{:S(2)}, u32[]{:S(2)}) collective-permute-start(bf16[2,128,768]{2,1,0:T(8,128)(2,1)} %get-tuple-element.197), channel_id=1, source_target_pairs={{0,8},{4,12},{8,0},{12,4},{1,9},{5,13},{9,1},{13,5},{2,10},{6,14},... | collective-permute-start | bytes 1179656 | tf_op jit(solution)/shard_map/ppermute | solution.py:34
  198.1 16.2 %collective-permute-start.53 = (bf16[2,96,768]{2,1,0:T(8,128)(2,1)}, bf16[2,96,768]{2,1,0:T(8,128)(2,1)S(1)}, u32[]{:S(2)}, u32[]{:S(2)}) collective-permute-start(bf16[2,96,768]{2,1,0:T(8,128)(2,1)} %get-tuple-element.206), channel_id=1, source_target_pairs={{0,4},{4,0},{8,12},{12,8},{1,5},{5,1},{9,13},{13,9},{2,6},{6,2},{1... | collective-permute-start | bytes 884744 | tf_op jit(solution)/shard_map/ppermute | solution.py:34
  199.3 20.4 %collective-permute-start.59 = (bf16[2,112,768]{2,1,0:T(8,128)(2,1)S(1)}, bf16[2,112,768]{2,1,0:T(8,128)(2,1)S(1)}, u32[]{:S(2)}, u32[]{:S(2)}) collective-permute-start(bf16[2,112,768]{2,1,0:T(8,128)(2,1)S(1)} %slice.126), channel_id=1, source_target_pairs={{0,2},{1,3},{2,0},{3,1},{4,6},{5,7},{6,4},{7,5},{8,10},{9,11},{10,... | collective-permute-start | bytes 1032200 | tf_op jit(solution)/shard_map/ppermute | solution.py:34
  200.9 15.9 %collective-permute-start.55 = (bf16[112,576]{1,0:T(8,128)(2,1)S(1)}, bf16[112,576]{1,0:T(8,128)(2,1)S(1)}, u32[]{:S(2)}, u32[]{:S(2)}) collective-permute-start(bf16[112,576]{1,0:T(8,128)(2,1)S(1)} %slice_bitcast_fusion.2), channel_id=1, source_target_pairs={{0,16},{16,0},{1,17},{17,1},{2,18},{18,2},{3,19},{19,3},{4,20},{20... | collective-permute-start | bytes 387080 | tf_op jit(solution)/shard_map/ppermute | solution.py:34
  202.0 18.9 %collective-permute-start.50 = (bf16[128,768]{1,0:T(8,128)(2,1)S(1)}, bf16[128,768]{1,0:T(8,128)(2,1)S(1)}, u32[]{:S(2)}, u32[]{:S(2)}) collective-permute-start(bf16[128,768]{1,0:T(8,128)(2,1)S(1)} %fusion.1), channel_id=1, source_target_pairs={{0,4},{4,0},{8,12},{12,8},{1,5},{5,1},{9,13},{13,9},{2,6},{6,2},{1... | collective-permute-start | bytes 589832 | tf_op jit(solution)/shard_map/ppermute | solution.py:34
  216.8 19.7 %collective-permute-start.63 = (bf16[96,768]{1,0:T(8,128)(2,1)}, bf16[96,768]{1,0:T(8,128)(2,1)S(1)}, u32[]{:S(2)}, u32[]{:S(2)}) collective-permute-start(bf16[96,768]{1,0:T(8,128)(2,1)} %get-tuple-element.215), channel_id=1, source_target_pairs={{0,8},{4,12},{8,0},{12,4},{1,9},{5,13},{9,1},{13,5},{2,10},{6,14},... | collective-permute-start | bytes 442376 | tf_op jit(solution)/shard_map/ppermute | solution.py:34
  219.9 20.0 %collective-permute-start.66 = (bf16[96,768]{1,0:T(8,128)(2,1)S(1)}, bf16[96,768]{1,0:T(8,128)(2,1)S(1)}, u32[]{:S(2)}, u32[]{:S(2)}) collective-permute-start(bf16[96,768]{1,0:T(8,128)(2,1)S(1)} %add_convert_fusion.10), channel_id=1, source_target_pairs={{0,8},{4,12},{8,0},{12,4},{1,9},{5,13},{9,1},{13,5},{2,10},{6,14},... | collective-permute-start | bytes 442376 | tf_op jit(solution)/shard_map/ppermute | solution.py:34
  220.9 15.7 %collective-permute-start.60 = (bf16[112,768]{1,0:T(8,128)(2,1)S(1)}, bf16[112,768]{1,0:T(8,128)(2,1)S(1)}, u32[]{:S(2)}, u32[]{:S(2)}) collective-permute-start(bf16[112,768]{1,0:T(8,128)(2,1)S(1)} %slice_bitcast_fusion), channel_id=1, source_target_pairs={{0,16},{16,0},{1,17},{17,1},{2,18},{18,2},{3,19},{19,3},{4,20},{20... | collective-permute-start | bytes 516104 | tf_op jit(solution)/shard_map/ppermute | solution.py:34
  224.4 25.4 %collective-permute-start.57 = (bf16[2,112,576]{2,1,0:T(8,128)(2,1)S(1)}, bf16[2,112,576]{2,1,0:T(8,128)(2,1)S(1)}, u32[]{:S(2)}, u32[]{:S(2)}) collective-permute-start(bf16[2,112,576]{2,1,0:T(8,128)(2,1)S(1)} %pad_maximum_fusion.4.pair), channel_id=1, source_target_pairs={{0,8},{4,12},{8,0},{12,4},{1,9},{5,13},{9,1},{13,5},{2,10},{6,14},... | collective-permute-start | bytes 774152 | tf_op jit(solution)/shard_map/ppermute | solution.py:34
  236.7 16.0 %collective-permute-start.61 = (bf16[112,768]{1,0:T(8,128)(2,1)S(1)}, bf16[112,768]{1,0:T(8,128)(2,1)S(1)}, u32[]{:S(2)}, u32[]{:S(2)}) collective-permute-start(bf16[112,768]{1,0:T(8,128)(2,1)S(1)} %fusion.2), channel_id=1, source_target_pairs={{0,4},{4,0},{8,12},{12,8},{1,5},{5,1},{9,13},{13,9},{2,6},{6,2},{1... | collective-permute-start | bytes 516104 | tf_op jit(solution)/shard_map/ppermute | solution.py:34
  239.9 21.7 %collective-permute-start.67 = (bf16[2,96,768]{2,1,0:T(8,128)(2,1)S(1)}, bf16[2,96,768]{2,1,0:T(8,128)(2,1)S(1)}, u32[]{:S(2)}, u32[]{:S(2)}) collective-permute-start(bf16[2,96,768]{2,1,0:T(8,128)(2,1)S(1)} %pad_maximum_fusion.2.pair), channel_id=1, source_target_pairs={{0,4},{4,0},{8,12},{12,8},{1,5},{5,1},{9,13},{13,9},{2,6},{6,2},{1... | collective-permute-start | bytes 884744 | tf_op jit(solution)/shard_map/ppermute | solution.py:34
  249.7 16.4 %collective-permute-start.65 = (bf16[2,96,768]{2,1,0:T(8,128)(2,1)S(1)}, bf16[2,96,768]{2,1,0:T(8,128)(2,1)S(1)}, u32[]{:S(2)}, u32[]{:S(2)}) collective-permute-start(bf16[2,96,768]{2,1,0:T(8,128)(2,1)S(1)} %pad_maximum_fusion.1.pair), channel_id=1, source_target_pairs={{0,4},{4,0},{8,12},{12,8},{1,5},{5,1},{9,13},{13,9},{2,6},{6,2},{1... | collective-permute-start | bytes 884744 | tf_op jit(solution)/shard_map/ppermute | solution.py:34
  252.7 16.3 %collective-permute-start.62 = (bf16[112,768]{1,0:T(8,128)(2,1)S(1)}, bf16[112,768]{1,0:T(8,128)(2,1)S(1)}, u32[]{:S(2)}, u32[]{:S(2)}) collective-permute-start(bf16[112,768]{1,0:T(8,128)(2,1)S(1)} %add_convert_fusion.8), channel_id=1, source_target_pairs={{0,8},{4,12},{8,0},{12,4},{1,9},{5,13},{9,1},{13,5},{2,10},{6,14},... | collective-permute-start | bytes 516104 | tf_op jit(solution)/shard_map/ppermute | solution.py:34
  (111 other events, 812.7 us)

commit v2 on v1

--- a/solution.py
+++ b/solution.py
@@ -27,6 +27,8 @@
 OWN = WIDTH // OWNERS
 PANEL = OWN + 16
 QUART = FF // BLK
+STEP = 256
+BACK_STEP = 512
 
 
 def swap(array, axis, by):
@@ -199,10 +201,10 @@
     kvs = (k0, k1, k2, k3)
     outs = (o0, o1, o2, o3)
 
-    lane = lax.broadcasted_iota(jnp.int32, (ROWS, 128), 1)
+    lane = lax.broadcasted_iota(jnp.int32, (STEP, 128), 1)
 
     def step(i, carry):
-        rows = rows_at(i, ROWS)
+        rows = rows_at(i, STEP)
         code1 = qc_ref[rows, 0:1]
         code2 = qc_ref[rows, 1:2]
         masks = []
@@ -210,7 +212,7 @@
             kc = kc_ref[0:1, j * GROUP : (j + 1) * GROUP]
             masks.append((kc == code1) | (kc == code2))
         heads = []
-        lse = jnp.zeros((ROWS, 128), F32)
+        lse = jnp.zeros((STEP, 128), F32)
         for h in range(LOCAL_HEADS):
             kwin, kup = window(h)
             vwin, vup = window(LOCAL_HEADS + h)
@@ -219,8 +221,8 @@
                 jnp.where(masks[j], nt(qp, kvs[j][:, kwin]), NEG) for j in range(BLK)
             ]
             top = functools.reduce(jnp.maximum, [jnp.max(s, axis=1, keepdims=True) for s in scores])
-            total = jnp.zeros((ROWS, 1), F32)
-            acc = jnp.zeros((ROWS, 128), F32)
+            total = jnp.zeros((STEP, 1), F32)
+            acc = jnp.zeros((STEP, 128), F32)
             for j in range(BLK):
                 e = jnp.exp(scores[j] - top)
                 total = total + jnp.sum(e, axis=1, keepdims=True)
@@ -232,7 +234,7 @@
         lse_ref[rows, :] = lse
         return carry
 
-    lax.fori_loop(0, ULY, step, 0)
+    lax.fori_loop(0, GROUP // STEP, step, 0)
     for i in range(ULY):
         outs[i][...] = all_ref[i * ROWS : (i + 1) * ROWS, :]
 
@@ -397,12 +399,12 @@
     acc[...] = jnp.zeros_like(acc)
     for i, g_ref in enumerate((g0, g1, g2, g3)):
         gall[i * ROWS : (i + 1) * ROWS, :] = g_ref[...]
-    lane = lax.broadcasted_iota(jnp.int32, (ROWS, 128), 1)
+    lane = lax.broadcasted_iota(jnp.int32, (BACK_STEP, 128), 1)
 
     def step(i, carry):
-        rows = rows_at(i, ROWS)
+        rows = rows_at(i, BACK_STEP)
         prod = gall[rows, :].astype(F32) * all_ref[rows, :].astype(F32)
-        stat = jnp.zeros((ROWS, 128), F32)
+        stat = jnp.zeros((BACK_STEP, 128), F32)
         for h in range(LOCAL_HEADS):
             stat = jnp.where(
                 lane == h, jnp.sum(prod[:, head_cols(h)], axis=1, keepdims=True), stat
@@ -411,7 +413,7 @@
         lse = lse_ref[rows, :].T
         code1 = qr_ref[0:1, rows]
         code2 = qr_ref[1:2, rows]
-        dq = [jnp.zeros((ROWS, 128), F32) for _ in range(LOCAL_HEADS)]
+        dq = [jnp.zeros((BACK_STEP, 128), F32) for _ in range(LOCAL_HEADS)]
         for j in range(BLK):
             kc = kcol_ref[j * GROUP : (j + 1) * GROUP, :]
             mask = (kc == code1) | (kc == code2)
@@ -435,7 +437,7 @@
         dq_ref[rows, :] = (jnp.concatenate(parts, axis=1) * HEAD_DIM ** (-0.5)).astype(BF16)
         return carry
 
-    lax.fori_loop(0, ULY, step, 0)
+    lax.fori_loop(0, GROUP // BACK_STEP, step, 0)
     keep[0] = acc[0].astype(BF16)
     keep[1] = acc[2].astype(BF16)
     send[0] = acc[1].astype(BF16)
@@ -892,13 +894,14 @@
         dkept, dsent = over_uly(dkept, dsent)
         ukept, usent = over_uly(ukept, usent)
         d_total = add_low(dkept, swap(dsent, "uly", 2))
-        u_total = add_low(ukept, swap(usent, "uly", 2))
+        u_mid = swap(usent, "uly", 2)
         g_last = after(g_last, d_total, usent, output)
+
+        o2 = add_low(o1[:2], swap(o1[2:], "blk", 2))
+        o3 = add_low(o2[0], swap(o2[1], "dp", 1))
+        u_total = add_low(after(ukept, o3), u_mid)
         grad_down = share(d_total).T
         grad_up = share(u_total)
-
-        o2 = add_low(o1[:2], swap(o1[2:], "blk", 2))
-        o3 = add_low(o2[0], swap(o2[1], "dp", 1))
         o4 = add_low(o3, swap(after(o3, d_total), "uly", 1))
         o5 = o4.astype(F32) + swap(o4, "uly", 2).astype(F32)
         grad_ow = o5[:OWN]
@@ -911,7 +914,7 @@
         grad_qkv, qvec = call(
             qkv_final_kernel,
             [sds((OWN, 3 * WIDTH), F32), sds((8, 3 * HW), F32)],
-            [tab, q_pair, swap(q_pair, "uly", 2)],
+            [tab, q_pair, swap(after(q_pair, u_total), "uly", 2)],
         )
         grad_gain1, grad_shift1, grad_qbias, grad_vbias = (
             qvec[0, k * OWN : (k + 1) * OWN] for k in range(4)

time: 272 us -> 260 us (0.956)
  Pallas kernels: 90.7 us -> 84 us
  starting transfers between devices: 64 us -> 60 us
    pallas_call x22, Pallas kernels: 90.7 us -> 84 us  [call(): pl.pallas_call(kernel, name=getattr(kernel, 'func', kernel).__name__, out...]
    ppermute x61, starting transfers between devices: 57.8 us -> 53.8 us  [swap(): return lax.ppermute(array, axis, [(i, i ^ by) for i in range(peers)])]
    ppermute x61, waiting for transfers between devices: 84.7 us -> 81.4 us  [swap(): return lax.ppermute(array, axis, [(i, i ^ by) for i in range(peers)])]
  transfers between devices with their start and end apart: 68 -> 68, of which waited for: 30 -> 31; matrix products, arithmetic and copies ran while one was open for 5% -> 6% of each run, Pallas kernels for 28% -> 26%
where the time goes in v2:
time: 260 us; the launch traced here: 259 us
  waiting for transfers between devices  85.3 us (33%)
  Pallas kernels  84 us (32%)
  starting transfers between devices  60 us (23%)
  local copies, waits for them, and re-layouts  17.7 us (7%)
  other arithmetic  10.3 us (4%)
    pallas_call x22, Pallas kernels, call(): pl.pallas_call(kernel, name=getattr(kernel, 'func', kernel).__name__, out...  84 us
    ppermute x61, waiting for transfers between devices, swap(): return lax.ppermute(array, axis, [(i, i ^ by) for i in range(peers)])  81.4 us
    ppermute x61, starting transfers between devices, swap(): return lax.ppermute(array, axis, [(i, i ^ by) for i in range(peers)])  53.8 us
    unnamed x134, local copies, waits for them, and re-layouts  10.9 us
    ppermute x7, starting transfers between devices, cross(): lax.ppermute(array, ('dp', 'blk'), [(i, i ^ by) for i in range(peers)])  6.22 us
  transfers between devices with their start and end apart: 68, of which 31 were waited for; matrix products, arithmetic and copies ran while one was open for 6% of the time, Pallas kernels for 26%

profile of v2, /device:TPU:0, one launch (start us, length us, event | category | flops | bytes accessed | tf_op | source)
XLA Modules:
  0.0 258.7 jit_solution(15802588554858680962)
XLA Ops:
  3.6 3.1 %collective-permute-start = (bf16[128,768]{1,0:T(8,128)(2,1)}, bf16[128,768]{1,0:T(8,128)(2,1)S(1)}, u32[]{:S(2)}, u32[]{:S(2)}) collective-permute-start(bf16[128,768]{1,0:T(8,128)(2,1)} %get-tuple-element.121.n0), channel_id=1, source_target_pairs={{0,4},{4,0},{8,12},{12,8},{1,5},{5,1},{9,13},{13,9},{2,6},{6,2},{1... | collective-permute-start | bytes 589832 | tf_op jit(solution)/shard_map/ppermute | solution.py:36
  17.3 5.4 %collective-permute-done.4.rest_1_ = bf16[2,112,576]{2,1,0:T(8,128)(2,1)S(1)} collective-permute-done((bf16[2,112,576]{2,1,0:T(8,128)(2,1)S(1)}, bf16[2,112,576]{2,1,0:T(8,128)(2,1)S(1)}, u32[]{:S(2)}, u32[]{:S(2)}) %collective-permute-start.4) | collective-permute-done | bytes 258080 | tf_op jit(solution)/shard_map/ppermute | solution.py:36
  35.0 3.5 %qkv_kernel.1 = (bf16[512,192]{1,0:T(8,128)(2,1)}, bf16[512,384]{1,0:T(8,128)(2,1)}, bf16[512,768]{1,0:T(8,128)(2,1)}, bf16[768,576]{1,0:T(8,128)(2,1)}, bf16[8,16,576]{2,1,0:T(8,128)(2,1)}) custom-call(s32[6]{0:T(128)} %stack.79.tab, bf16[128,768]{1,0:T(8,128)(2,1)} %get-tuple-element.121.n0, bf16[128,768]{1,0:T(8,128)(2,1)} %copy-done.16, ...), custom_call_target="tpu_custom_call" | custom-call | flops 452984832 | bytes 4227096 | tf_op jit(solution)/shard_map/qkv_kernel/pallas_call | solution.py:66
  41.1 3.6 %collective-permute-done.11 = bf16[96,768]{1,0:T(8,128)(2,1)S(1)} collective-permute-done((bf16[96,768]{1,0:T(8,128)(2,1)S(1)}, bf16[96,768]{1,0:T(8,128)(2,1)S(1)}, u32[]{:S(2)}, u32[]{:S(2)}) %collective-permute-start.11) | collective-permute-done | bytes 147488 | tf_op jit(solution)/shard_map/ppermute | solution.py:36
  44.8 5.1 %collective-permute-done.9.k2 = bf16[512,384]{1,0:T(8,128)(2,1)S(1)} collective-permute-done((bf16[512,384]{1,0:T(8,128)(2,1)}, bf16[512,384]{1,0:T(8,128)(2,1)S(1)}, u32[]{:S(2)}, u32[]{:S(2)}) %collective-permute-start.9) | collective-permute-done | bytes 393248 | tf_op jit(solution)/shard_map/ppermute | solution.py:36
  56.7 8.4 %attend_kernel.1 = (bf16[128,192]{1,0:T(8,128)(2,1)}, bf16[128,192]{1,0:T(8,128)(2,1)}, bf16[128,192]{1,0:T(8,128)(2,1)}, bf16[128,192]{1,0:T(8,128)(2,1)}, bf16...) custom-call(s32[6]{0:T(128)} %stack.79.tab, bf16[512,192]{1,0:T(8,128)(2,1)} %get-tuple-element.127.q_ref, ...), custom_call_target="tpu_custom_call" | custom-call | flops 805306368 | bytes 2437144 | tf_op jit(solution)/shard_map/attend_kernel/pallas_call | solution.py:66
  69.2 3.5 %collective-permute-start.19 = (bf16[128,192]{1,0:T(8,128)(2,1)}, bf16[128,192]{1,0:T(8,128)(2,1)S(1)}, u32[]{:S(2)}, u32[]{:S(2)}) collective-permute-start(bf16[128,192]{1,0:T(8,128)(2,1)} %get-tuple-element.147), channel_id=1, source_target_pairs={{0,8},{4,12},{8,0},{12,4},{1,9},{5,13},{9,1},{13,5},{2,10},{6,14},... | collective-permute-start | bytes 147464 | tf_op jit(solution)/shard_map/ppermute | solution.py:36
  78.8 3.7 %collective-permute-done.20.a3 = bf16[128,192]{1,0:T(8,128)(2,1)S(1)} collective-permute-done((bf16[128,192]{1,0:T(8,128)(2,1)}, bf16[128,192]{1,0:T(8,128)(2,1)S(1)}, u32[]{:S(2)}, u32[]{:S(2)}) %collective-permute-start.20) | collective-permute-done | bytes 49184 | tf_op jit(solution)/shard_map/ppermute | solution.py:36
  83.3 4.2 %mix_kernel.1 = (f32[128,768]{1,0:T(8,128)}, bf16[128,768]{1,0:T(8,128)(2,1)}, bf16[768,768]{1,0:T(8,128)(2,1)}) custom-call(s32[6]{0:T(128)} %stack.79.tab, bf16[128,192]{1,0:T(8,128)(2,1)} %get-tuple-element.145.a0, bf16[128,192]{1,0:T(8,128)(2,1)} %copy-done.37, bf16[128,192]{1,0:T(8,128)(2,1)} %copy-done.38, bf16[128,192]{1,0:T(8,128)(2,1)} %copy-done.39, ...), custom_call_target="tpu_custom_call" | custom-call | flops 150994944 | bytes 3686424 | tf_op jit(solution)/shard_map/mix_kernel/pallas_call | solution.py:66
  89.8 6.6 %collective-permute-done.27.h2.refs_2_ = bf16[128,768]{1,0:T(8,128)(2,1)S(1)} collective-permute-done((bf16[128,768]{1,0:T(8,128)(2,1)}, bf16[128,768]{1,0:T(8,128)(2,1)S(1)}, u32[]{:S(2)}, u32[]{:S(2)}) %collective-permute-start.27) | collective-permute-done | bytes 196640 | tf_op jit(solution)/shard_map/ppermute | solution.py:36
  98.6 8.5 %ffn_kernel.1 = (bf16[512,768]{1,0:T(8,128)(2,1)}, bf16[512,768]{1,0:T(8,128)(2,1)}, f32[2,128,768]{2,1,0:T(8,128)}, bf16[2,128,768]{2,1,0:T(8,128)(2,1)}, f32[1...) custom-call(s32[6]{0:T(128)} %stack.79.tab, ...), custom_call_target="tpu_custom_call" | custom-call | flops 2415919104 | bytes 7815192 | tf_op jit(solution)/shard_map/ffn_kernel/pallas_call | solution.py:66
  109.2 5.2 %ffn_grad_kernel.1 = (bf16[4,96,768]{2,1,0:T(8,128)(2,1)}, bf16[4,96,768]{2,1,0:T(8,128)(2,1)}, bf16[4,96,768]{2,1,0:T(8,128)(2,1)}, bf16[4,96,768]{2,1,0:T(8,128)(2,1)}) custom-call(s32[6]{0:T(128)} %stack.79.tab, bf16[128,768]{1,0:T(8,128)(2,1)} %get-tuple-element.158.h0.refs_0_, bf16[128,768]{1,0:T(8,128)(2,1)} %copy-done.48, ...), custom_call_target="tpu_custom_call" | custom-call | bytes 1 | tf_op jit(solution)/shard_map/ffn_grad_kernel/pallas_call | solution.py:66
  118.9 3.4 %back_mix_kernel.1 = (f32[128,768]{1,0:T(8,128)}, bf16[128,768]{1,0:T(8,128)(2,1)}, bf16[128,192]{1,0:T(8,128)(2,1)}, bf16[128,192]{1,0:T(8,128)(2,1)}, bf16[128...) custom-call(s32[6]{0:T(128)} %stack.79.tab, f32[128,768]{1,0:T(8,128)} %get-tuple-element.196.resid_ref, ...), custom_call_target="tpu_custom_call" | custom-call | flops 150994944 | bytes 3907608 | tf_op jit(solution)/shard_map/back_mix_kernel/pallas_call | solution.py:66
  122.9 3.1 %collective-permute-start.35 = (bf16[128,192]{1,0:T(8,128)(2,1)}, bf16[128,192]{1,0:T(8,128)(2,1)S(1)}, u32[]{:S(2)}, u32[]{:S(2)}) collective-permute-start(bf16[128,192]{1,0:T(8,128)(2,1)} %get-tuple-element.174), channel_id=1, source_target_pairs={{0,8},{4,12},{8,0},{12,4},{1,9},{5,13},{9,1},{13,5},{2,10},{6,14},... | collective-permute-start | bytes 147464 | tf_op jit(solution)/shard_map/ppermute | solution.py:36
  132.9 12.6 %back_attend_kernel.1 = (bf16[512,192]{1,0:T(8,128)(2,1)}, bf16[2,512,384]{2,1,0:T(8,128)(2,1)}, bf16[2,512,384]{2,1,0:T(8,128)(2,1)}) custom-call(s32[6]{0:T(128)} %stack.79.tab, bf16[512,192]{1,0:T(8,128)(2,1)} %get-tuple-element.127.q_ref, bf16[512,384]{1,0:T(8,128)(2,1)} %get-tuple-element.131.k0, bf16[512,384]{1,0:T(8,128)(2,1)} %copy-done.57, ...), custom_call_target="tpu_custom_call" | custom-call | flops 2013265920 | bytes 4206616 | tf_op jit(solution)/shard_map/back_attend_kernel/pallas_call | solution.py:66
  153.2 3.1 %out_grad_kernel.1 = (bf16[4,112,768]{2,1,0:T(8,128)(2,1)}, bf16[4,112,768]{2,1,0:T(8,128)(2,1)}) custom-call(s32[6]{0:T(128)} %stack.79.tab, bf16[128,192]{1,0:T(8,128)(2,1)} %get-tuple-element.145.a0, bf16[128,192]{1,0:T(8,128)(2,1)} %copy-done.37, bf16[128,192]{1,0:T(8,128)(2,1)} %copy-done.38, bf16[128,192]{1,0:T(8,128)(2,1)} %copy-done.39, ...), custom_call_target="tpu_custom_call" | custom-call | bytes 1 | tf_op jit(solution)/shard_map/out_grad_kernel/pallas_call | solution.py:66
  162.9 4.4 %back_proj_kernel.1 = (bf16[512,576]{1,0:T(8,128)(2,1)}, f32[128,768]{1,0:T(8,128)}, f32[128,768]{1,0:T(8,128)}, bf16[2,128,768]{2,1,0:T(8,128)(2,1)}, f32[8,768]{1,0:T(8,128)}) custom-call(s32[6]{0:T(128)} %stack.79.tab, bf16[512,192]{1,0:T(8,128)(2,1)} %get-tuple-element.193.dq_ref, bf16[2,512,384]{2,1,0:T(8,128)(2,1)} %get-tuple-element.182.keep, ...), custom_call_target="tpu_custom_call" | custom-call | flops 452984832 | bytes 5627928 | tf_op jit(solution)/shard_map/back_proj_kernel/pallas_call | solution.py:66
  167.2 3.6 %qkv_grad_kernel.1 = (bf16[4,112,576]{2,1,0:T(8,128)(2,1)}, bf16[4,112,576]{2,1,0:T(8,128)(2,1)}) custom-call(s32[6]{0:T(128)} %stack.79.tab, bf16[512,768]{1,0:T(8,128)(2,1)} %get-tuple-element.200.h_ref, bf16[512,576]{1,0:T(8,128)(2,1)} %get-tuple-element.195.dproj_ref, f32[8,768]{1,0:T(8,128)} %get-tuple-element.201.vs_ref), custom_call_target="tpu_custom_call" | custom-call | bytes 1 | tf_op jit(solution)/shard_map/qkv_grad_kernel/pallas_call | solution.py:66
  174.6 6.0 %collective-permute-done.48.by_ref = bf16[2,96,768]{2,1,0:T(8,128)(2,1)S(1)} collective-permute-done((bf16[2,96,768]{2,1,0:T(8,128)(2,1)S(1)}, bf16[2,96,768]{2,1,0:T(8,128)(2,1)S(1)}, u32[]{:S(2)}, u32[]{:S(2)}) %collective-permute-start.48) | collective-permute-done | bytes 294944 | tf_op jit(solution)/shard_map/ppermute | solution.py:36
  203.3 5.5 %collective-permute-done.53.b_ref = bf16[2,96,768]{2,1,0:T(8,128)(2,1)S(1)} collective-permute-done((bf16[2,96,768]{2,1,0:T(8,128)(2,1)}, bf16[2,96,768]{2,1,0:T(8,128)(2,1)S(1)}, u32[]{:S(2)}, u32[]{:S(2)}) %collective-permute-start.53) | collective-permute-done | bytes 294944 | tf_op jit(solution)/shard_map/ppermute | solution.py:36
  219.9 5.4 %collective-permute-done.60 = bf16[96,768]{1,0:T(8,128)(2,1)S(1)} collective-permute-done((bf16[96,768]{1,0:T(8,128)(2,1)}, bf16[96,768]{1,0:T(8,128)(2,1)S(1)}, u32[]{:S(2)}, u32[]{:S(2)}) %collective-permute-start.60) | collective-permute-done | bytes 147488 | tf_op jit(solution)/shard_map/ppermute | solution.py:36
  231.0 2.9 %collective-permute-done.64 = bf16[96,768]{1,0:T(8,128)(2,1)S(1)} collective-permute-done((bf16[96,768]{1,0:T(8,128)(2,1)S(1)}, bf16[96,768]{1,0:T(8,128)(2,1)S(1)}, u32[]{:S(2)}, u32[]{:S(2)}) %collective-permute-start.64) | collective-permute-done | bytes 147488 | tf_op jit(solution)/shard_map/ppermute | solution.py:36
  234.0 6.9 %collective-permute-done.62 = bf16[112,768]{1,0:T(8,128)(2,1)S(1)} collective-permute-done((bf16[112,768]{1,0:T(8,128)(2,1)S(1)}, bf16[112,768]{1,0:T(8,128)(2,1)S(1)}, u32[]{:S(2)}, u32[]{:S(2)}) %collective-permute-start.62) | collective-permute-done | bytes 172064 | tf_op jit(solution)/shard_map/ppermute | solution.py:36
  241.1 4.7 %collective-permute-done.61.got = bf16[2,112,576]{2,1,0:T(8,128)(2,1)S(1)} collective-permute-done((bf16[2,112,576]{2,1,0:T(8,128)(2,1)S(1)}, bf16[2,112,576]{2,1,0:T(8,128)(2,1)S(1)}, u32[]{:S(2)}, u32[]{:S(2)}) %collective-permute-start.61) | collective-permute-done | bytes 258080 | tf_op jit(solution)/shard_map/ppermute | solution.py:36
  (317 shorter events, 134.9 us)
Async XLA Ops:
  3.6 30.0 %collective-permute-start = (bf16[128,768]{1,0:T(8,128)(2,1)}, bf16[128,768]{1,0:T(8,128)(2,1)S(1)}, u32[]{:S(2)}, u32[]{:S(2)}) collective-permute-start(bf16[128,768]{1,0:T(8,128)(2,1)} %get-tuple-element.121.n0), channel_id=1, source_target_pairs={{0,4},{4,0},{8,12},{12,8},{1,5},{5,1},{9,13},{13,9},{2,6},{6,2},{1... | collective-permute-start | bytes 589832 | tf_op jit(solution)/shard_map/ppermute | solution.py:36
  6.7 26.9 %collective-permute-start.1 = (bf16[128,768]{1,0:T(8,128)(2,1)}, bf16[128,768]{1,0:T(8,128)(2,1)S(1)}, u32[]{:S(2)}, u32[]{:S(2)}) collective-permute-start(bf16[128,768]{1,0:T(8,128)(2,1)} %get-tuple-element.121.n0), channel_id=1, source_target_pairs={{0,8},{4,12},{8,0},{12,4},{1,9},{5,13},{9,1},{13,5},{2,10},{6,14},... | collective-permute-start | bytes 589832 | tf_op jit(solution)/shard_map/ppermute | solution.py:36
  9.3 24.4 %collective-permute-start.2 = (bf16[128,768]{1,0:T(8,128)(2,1)}, bf16[128,768]{1,0:T(8,128)(2,1)S(1)}, u32[]{:S(2)}, u32[]{:S(2)}) collective-permute-start(bf16[128,768]{1,0:T(8,128)(2,1)} %get-tuple-element.121.n0), channel_id=1, source_target_pairs={{0,12},{4,8},{8,4},{12,0},{1,13},{5,9},{9,5},{13,1},{2,14},{6,10},... | collective-permute-start | bytes 589832 | tf_op jit(solution)/shard_map/ppermute | solution.py:36
  51.9 15.9 %collective-permute-start.16 = (bf16[2,96,768]{2,1,0:T(8,128)(2,1)}, bf16[2,96,768]{2,1,0:T(8,128)(2,1)S(1)}, u32[]{:S(2)}, u32[]{:S(2)}) collective-permute-start(bf16[2,96,768]{2,1,0:T(8,128)(2,1)} %get-tuple-element.134), channel_id=1, source_target_pairs={{0,17},{1,16},{2,19},{3,18},{16,1},{17,0},{18,3},{19,2},{4,21},{5,... | collective-permute-start | bytes 884744 | tf_op jit(solution)/shard_map/ppermute | solution.py:41
  53.2 14.7 %collective-permute-start.15 = (bf16[2,96,768]{2,1,0:T(8,128)(2,1)}, bf16[2,96,768]{2,1,0:T(8,128)(2,1)}, u32[]{:S(2)}, u32[]{:S(2)}) collective-permute-start(bf16[2,96,768]{2,1,0:T(8,128)(2,1)} %get-tuple-element.143.rest_0_), channel_id=1, source_target_pairs={{0,16},{1,17},{2,18},{3,19},{16,0},{17,1},{18,2},{19,3},{4,20},{5,... | collective-permute-start | bytes 884744 | tf_op jit(solution)/shard_map/ppermute | solution.py:41
  53.7 14.2 %collective-permute-start.17 = (bf16[2,96,768]{2,1,0:T(8,128)(2,1)S(1)}, bf16[2,96,768]{2,1,0:T(8,128)(2,1)S(1)}, u32[]{:S(2)}, u32[]{:S(2)}) collective-permute-start(bf16[2,96,768]{2,1,0:T(8,128)(2,1)S(1)} %pad_maximum_fusion.rest_0_), channel_id=1, source_target_pairs={{0,2},{1,3},{2,0},{3,1},{4,6},{5,7},{6,4},{7,5},{8,10},{9,11},{10,... | collective-permute-start | bytes 884744 | tf_op jit(solution)/shard_map/ppermute | solution.py:36
  54.2 20.3 %collective-permute-start.24 = (bf16[2,96,768]{2,1,0:T(8,128)(2,1)}, bf16[2,96,768]{2,1,0:T(8,128)(2,1)}, u32[]{:S(2)}, u32[]{:S(2)}) collective-permute-start(bf16[2,96,768]{2,1,0:T(8,128)(2,1)} %get-tuple-element.157), channel_id=1, source_target_pairs={{0,3},{1,2},{2,1},{3,0},{16,19},{17,18},{18,17},{19,16},{4,7},{5,6... | collective-permute-start | bytes 884744 | tf_op jit(solution)/shard_map/ppermute | solution.py:41
  55.2 19.4 %collective-permute-start.23 = (bf16[128,768]{1,0:T(8,128)(2,1)S(1)}, bf16[128,768]{1,0:T(8,128)(2,1)S(1)}, u32[]{:S(2)}, u32[]{:S(2)}) collective-permute-start(bf16[128,768]{1,0:T(8,128)(2,1)S(1)} %bitcast_convert_fusion.c0.refs_4_.c_ref), channel_id=1, source_target_pairs={{0,2},{1,3},{2,0},{3,1},{4,6},{5,7},{6,4},{7,5},{8,10},{9,11},{10,... | collective-permute-start | bytes 589832 | tf_op jit(solution)/shard_map/ppermute | solution.py:36
  73.1 14.4 %collective-permute-start.22 = (bf16[2,96,768]{2,1,0:T(8,128)(2,1)}, bf16[2,96,768]{2,1,0:T(8,128)(2,1)S(1)}, u32[]{:S(2)}, u32[]{:S(2)}) collective-permute-start(bf16[2,96,768]{2,1,0:T(8,128)(2,1)} %get-tuple-element.153), channel_id=1, source_target_pairs={{0,18},{1,19},{2,16},{3,17},{16,2},{17,3},{18,0},{19,1},{4,22},{5,... | collective-permute-start | bytes 884744 | tf_op jit(solution)/shard_map/ppermute | solution.py:41
  122.3 23.2 %collective-permute-start.37 = (bf16[4,96,768]{2,1,0:T(8,128)(2,1)S(1)}, bf16[4,96,768]{2,1,0:T(8,128)(2,1)S(1)}, u32[]{:S(2)}, u32[]{:S(2)}) collective-permute-start(bf16[4,96,768]{2,1,0:T(8,128)(2,1)S(1)} %copy-done.55), channel_id=1, source_target_pairs={{0,2},{1,3},{2,0},{3,1},{4,6},{5,7},{6,4},{7,5},{8,10},{9,11},{10,... | collective-permute-start | bytes 1769480 | tf_op jit(solution)/shard_map/ppermute | solution.py:36
  128.6 16.9 %collective-permute-start.38 = (bf16[128,768]{1,0:T(8,128)(2,1)S(1)}, bf16[128,768]{1,0:T(8,128)(2,1)S(1)}, u32[]{:S(2)}, u32[]{:S(2)}) collective-permute-start(bf16[128,768]{1,0:T(8,128)(2,1)S(1)} %fusion.4), channel_id=1, source_target_pairs={{0,2},{1,3},{2,0},{3,1},{4,6},{5,7},{6,4},{7,5},{8,10},{9,11},{10,... | collective-permute-start | bytes 589832 | tf_op jit(solution)/shard_map/ppermute | solution.py:36
  150.7 20.2 %collective-permute-start.46 = (bf16[4,96,768]{2,1,0:T(8,128)(2,1)}, bf16[4,96,768]{2,1,0:T(8,128)(2,1)S(1)}, u32[]{:S(2)}, u32[]{:S(2)}) collective-permute-start(bf16[4,96,768]{2,1,0:T(8,128)(2,1)} %get-tuple-element.163), channel_id=1, source_target_pairs={{0,16},{16,0},{1,17},{17,1},{2,18},{18,2},{3,19},{19,3},{4,20},{20... | collective-permute-start | bytes 1769480 | tf_op jit(solution)/shard_map/ppermute | solution.py:36
  160.4 24.2 %collective-permute-start.45 = (bf16[4,96,768]{2,1,0:T(8,128)(2,1)}, bf16[4,96,768]{2,1,0:T(8,128)(2,1)S(1)}, u32[]{:S(2)}, u32[]{:S(2)}) collective-permute-start(bf16[4,96,768]{2,1,0:T(8,128)(2,1)} %pack_kernel.1), channel_id=1, source_target_pairs={{0,16},{16,0},{1,17},{17,1},{2,18},{18,2},{3,19},{19,3},{4,20},{20... | collective-permute-start | bytes 1769480 | tf_op jit(solution)/shard_map/ppermute | solution.py:36
  170.8 22.7 %collective-permute-start.57 = (bf16[4,112,768]{2,1,0:T(8,128)(2,1)}, bf16[4,112,768]{2,1,0:T(8,128)(2,1)S(1)}, u32[]{:S(2)}, u32[]{:S(2)}) collective-permute-start(bf16[4,112,768]{2,1,0:T(8,128)(2,1)} %get-tuple-element.221), channel_id=1, source_target_pairs={{0,1},{1,0},{2,3},{3,2},{4,5},{5,4},{6,7},{7,6},{8,9},{9,8},{10,11... | collective-permute-start | bytes 2064392 | tf_op jit(solution)/shard_map/ppermute | solution.py:36
  173.1 20.4 %collective-permute-start.43 = (bf16[2,128,768]{2,1,0:T(8,128)(2,1)}, bf16[2,128,768]{2,1,0:T(8,128)(2,1)S(1)}, u32[]{:S(2)}, u32[]{:S(2)}) collective-permute-start(bf16[2,128,768]{2,1,0:T(8,128)(2,1)} %get-tuple-element.199), channel_id=1, source_target_pairs={{0,8},{4,12},{8,0},{12,4},{1,9},{5,13},{9,1},{13,5},{2,10},{6,14},... | collective-permute-start | bytes 1179656 | tf_op jit(solution)/shard_map/ppermute | solution.py:36
  192.6 16.2 %collective-permute-start.53 = (bf16[2,96,768]{2,1,0:T(8,128)(2,1)}, bf16[2,96,768]{2,1,0:T(8,128)(2,1)S(1)}, u32[]{:S(2)}, u32[]{:S(2)}) collective-permute-start(bf16[2,96,768]{2,1,0:T(8,128)(2,1)} %get-tuple-element.208), channel_id=1, source_target_pairs={{0,4},{4,0},{8,12},{12,8},{1,5},{5,1},{9,13},{13,9},{2,6},{6,2},{1... | collective-permute-start | bytes 884744 | tf_op jit(solution)/shard_map/ppermute | solution.py:36
  193.8 20.5 %collective-permute-start.58 = (bf16[2,112,768]{2,1,0:T(8,128)(2,1)S(1)}, bf16[2,112,768]{2,1,0:T(8,128)(2,1)S(1)}, u32[]{:S(2)}, u32[]{:S(2)}) collective-permute-start(bf16[2,112,768]{2,1,0:T(8,128)(2,1)S(1)} %slice.126), channel_id=1, source_target_pairs={{0,2},{1,3},{2,0},{3,1},{4,6},{5,7},{6,4},{7,5},{8,10},{9,11},{10,... | collective-permute-start | bytes 1032200 | tf_op jit(solution)/shard_map/ppermute | solution.py:36
  195.4 16.0 %collective-permute-start.55 = (bf16[112,576]{1,0:T(8,128)(2,1)S(1)}, bf16[112,576]{1,0:T(8,128)(2,1)S(1)}, u32[]{:S(2)}, u32[]{:S(2)}) collective-permute-start(bf16[112,576]{1,0:T(8,128)(2,1)S(1)} %slice_bitcast_fusion.2), channel_id=1, source_target_pairs={{0,16},{16,0},{1,17},{17,1},{2,18},{18,2},{3,19},{19,3},{4,20},{20... | collective-permute-start | bytes 387080 | tf_op jit(solution)/shard_map/ppermute | solution.py:36
  196.5 19.3 %collective-permute-start.50 = (bf16[128,768]{1,0:T(8,128)(2,1)S(1)}, bf16[128,768]{1,0:T(8,128)(2,1)S(1)}, u32[]{:S(2)}, u32[]{:S(2)}) collective-permute-start(bf16[128,768]{1,0:T(8,128)(2,1)S(1)} %fusion.1), channel_id=1, source_target_pairs={{0,4},{4,0},{8,12},{12,8},{1,5},{5,1},{9,13},{13,9},{2,6},{6,2},{1... | collective-permute-start | bytes 589832 | tf_op jit(solution)/shard_map/ppermute | solution.py:36
  211.4 14.0 %collective-permute-start.56 = (bf16[112,576]{1,0:T(8,128)(2,1)S(1)}, bf16[112,576]{1,0:T(8,128)(2,1)S(1)}, u32[]{:S(2)}, u32[]{:S(2)}) collective-permute-start(bf16[112,576]{1,0:T(8,128)(2,1)S(1)} %fusion.3), channel_id=1, source_target_pairs={{0,4},{4,0},{8,12},{12,8},{1,5},{5,1},{9,13},{13,9},{2,6},{6,2},{1... | collective-permute-start | bytes 387080 | tf_op jit(solution)/shard_map/ppermute | solution.py:36
  225.5 15.5 %collective-permute-start.62 = (bf16[112,768]{1,0:T(8,128)(2,1)S(1)}, bf16[112,768]{1,0:T(8,128)(2,1)S(1)}, u32[]{:S(2)}, u32[]{:S(2)}) collective-permute-start(bf16[112,768]{1,0:T(8,128)(2,1)S(1)} %fusion.2), channel_id=1, source_target_pairs={{0,4},{4,0},{8,12},{12,8},{1,5},{5,1},{9,13},{13,9},{2,6},{6,2},{1... | collective-permute-start | bytes 516104 | tf_op jit(solution)/shard_map/ppermute | solution.py:36
  228.5 22.5 %collective-permute-start.67 = (bf16[2,96,768]{2,1,0:T(8,128)(2,1)S(1)}, bf16[2,96,768]{2,1,0:T(8,128)(2,1)S(1)}, u32[]{:S(2)}, u32[]{:S(2)}) collective-permute-start(bf16[2,96,768]{2,1,0:T(8,128)(2,1)S(1)} %pad_maximum_fusion.2.pair), channel_id=1, source_target_pairs={{0,4},{4,0},{8,12},{12,8},{1,5},{5,1},{9,13},{13,9},{2,6},{6,2},{1... | collective-permute-start | bytes 884744 | tf_op jit(solution)/shard_map/ppermute | solution.py:36
  228.5 17.2 %collective-permute-start.61 = (bf16[2,112,576]{2,1,0:T(8,128)(2,1)S(1)}, bf16[2,112,576]{2,1,0:T(8,128)(2,1)S(1)}, u32[]{:S(2)}, u32[]{:S(2)}) collective-permute-start(bf16[2,112,576]{2,1,0:T(8,128)(2,1)S(1)} %pad_maximum_fusion.4.pair), channel_id=1, source_target_pairs={{0,8},{4,12},{8,0},{12,4},{1,9},{5,13},{9,1},{13,5},{2,10},{6,14},... | collective-permute-start | bytes 774152 | tf_op jit(solution)/shard_map/ppermute | solution.py:36
  233.9 21.9 %collective-permute-start.65 = (bf16[2,96,768]{2,1,0:T(8,128)(2,1)S(1)}, bf16[2,96,768]{2,1,0:T(8,128)(2,1)S(1)}, u32[]{:S(2)}, u32[]{:S(2)}) collective-permute-start(bf16[2,96,768]{2,1,0:T(8,128)(2,1)S(1)} %pad_maximum_fusion.1.pair), channel_id=1, source_target_pairs={{0,4},{4,0},{8,12},{12,8},{1,5},{5,1},{9,13},{13,9},{2,6},{6,2},{1... | collective-permute-start | bytes 884744 | tf_op jit(solution)/shard_map/ppermute | solution.py:36
  (111 other events, 786.4 us)

commit v3 on v2

--- a/solution.py
+++ b/solution.py
@@ -27,7 +27,7 @@
 OWN = WIDTH // OWNERS
 PANEL = OWN + 16
 QUART = FF // BLK
-STEP = 256
+STEP = 512
 BACK_STEP = 512
 
 
@@ -697,9 +697,7 @@
     kcode = jnp.where(valid > 0, kseg, kplace + 64)
     qcodes = jnp.stack([kseg[:GROUP], kplace[:GROUP] + 64])
 
-    n1, q_cols, q_rows, k_cols, k_rows = lax.optimization_barrier(
-        (n1, qcodes.T, qcodes, kcode[:, None], kcode[None, :])
-    )
+    n1, q_cols, k_rows = lax.optimization_barrier((n1, qcodes.T, kcode[None, :]))
     q, kv, h1, w_qkv, vv = call(
         functools.partial(qkv_kernel, four_bits),
         [
@@ -712,6 +710,8 @@
         [tab, n0, n1, n2, n3, *a_parts],
         flops=2 * GROUP * WIDTH * 3 * HW,
     )
+    q_rows, late = lax.optimization_barrier((qcodes, kcode, kv))[:2]
+    k_cols = late[:, None]
     cb = cot.astype(BF16)
     if near:
         kv_y = swap(after(kv, w_parts[2]), "blk", 2)

time: 260 us -> 257 us (0.988)
  waiting for transfers between devices: 85.3 us -> 76.8 us
  starting transfers between devices: 60 us -> 67.7 us
    ppermute x61, waiting for transfers between devices: 81.4 us -> 72.3 us  [swap(): return lax.ppermute(array, axis, [(i, i ^ by) for i in range(peers)])]
    ppermute x61, starting transfers between devices: 53.8 us -> 61.1 us  [swap(): return lax.ppermute(array, axis, [(i, i ^ by) for i in range(peers)])]
    unnamed x134 -> x138, local copies, waits for them, and re-layouts: 10.9 us -> 11.9 us
  transfers between devices with their start and end apart: 68 -> 68, of which waited for: 31 -> 29; matrix products, arithmetic and copies ran while one was open for 6% -> 5% of each run, Pallas kernels for 26% -> 26%
where the time goes in v3:
time: 257 us
  Pallas kernels  83.9 us (33%)
  waiting for transfers between devices  76.8 us (30%)
  starting transfers between devices  67.7 us (26%)
  local copies, waits for them, and re-layouts  18.2 us (7%)
  other arithmetic  8.6 us (3%)
    pallas_call x22, Pallas kernels, call(): pl.pallas_call(kernel, name=getattr(kernel, 'func', kernel).__name__, out...  83.9 us
    ppermute x61, waiting for transfers between devices, swap(): return lax.ppermute(array, axis, [(i, i ^ by) for i in range(peers)])  72.3 us
    ppermute x61, starting transfers between devices, swap(): return lax.ppermute(array, axis, [(i, i ^ by) for i in range(peers)])  61.1 us
    unnamed x138, local copies, waits for them, and re-layouts  11.9 us
    ppermute x7, starting transfers between devices, cross(): lax.ppermute(array, ('dp', 'blk'), [(i, i ^ by) for i in range(peers)])  6.52 us
  transfers between devices with their start and end apart: 68, of which 29 were waited for; matrix products, arithmetic and copies ran while one was open for 5% of the time, Pallas kernels for 26%

profile of v3, /device:TPU:0, one launch (start us, length us, event | category | flops | bytes accessed | tf_op | source)
XLA Modules:
  0.0 256.5 jit_solution(753741264999689422)
XLA Ops:
  3.6 3.1 %collective-permute-start = (bf16[128,768]{1,0:T(8,128)(2,1)}, bf16[128,768]{1,0:T(8,128)(2,1)S(1)}, u32[]{:S(2)}, u32[]{:S(2)}) collective-permute-start(bf16[128,768]{1,0:T(8,128)(2,1)} %get-tuple-element.121.n0), channel_id=1, source_target_pairs={{0,4},{4,0},{8,12},{12,8},{1,5},{5,1},{9,13},{13,9},{2,6},{6,2},{1... | collective-permute-start | bytes 589832 | tf_op jit(solution)/shard_map/ppermute | solution.py:36
  17.3 5.4 %collective-permute-done.4.rest_1_ = bf16[2,112,576]{2,1,0:T(8,128)(2,1)S(1)} collective-permute-done((bf16[2,112,576]{2,1,0:T(8,128)(2,1)S(1)}, bf16[2,112,576]{2,1,0:T(8,128)(2,1)S(1)}, u32[]{:S(2)}, u32[]{:S(2)}) %collective-permute-start.4) | collective-permute-done | bytes 258080 | tf_op jit(solution)/shard_map/ppermute | solution.py:36
  31.5 3.5 %qkv_kernel.1 = (bf16[512,192]{1,0:T(8,128)(2,1)}, bf16[512,384]{1,0:T(8,128)(2,1)}, bf16[512,768]{1,0:T(8,128)(2,1)}, bf16[768,576]{1,0:T(8,128)(2,1)}, bf16[8,16,576]{2,1,0:T(8,128)(2,1)}) custom-call(s32[6]{0:T(128)} %stack.79.tab, bf16[128,768]{1,0:T(8,128)(2,1)} %get-tuple-element.121.n0, bf16[128,768]{1,0:T(8,128)(2,1)} %copy-done.16, ...), custom_call_target="tpu_custom_call" | custom-call | flops 452984832 | bytes 4227096 | tf_op jit(solution)/shard_map/qkv_kernel/pallas_call | solution.py:66
  40.7 3.1 %collective-permute-done.11 = bf16[96,768]{1,0:T(8,128)(2,1)S(1)} collective-permute-done((bf16[96,768]{1,0:T(8,128)(2,1)S(1)}, bf16[96,768]{1,0:T(8,128)(2,1)S(1)}, u32[]{:S(2)}, u32[]{:S(2)}) %collective-permute-start.11) | collective-permute-done | bytes 147488 | tf_op jit(solution)/shard_map/ppermute | solution.py:36
  44.0 4.0 %collective-permute-done.9.k2 = bf16[512,384]{1,0:T(8,128)(2,1)S(1)} collective-permute-done((bf16[512,384]{1,0:T(8,128)(2,1)}, bf16[512,384]{1,0:T(8,128)(2,1)S(1)}, u32[]{:S(2)}, u32[]{:S(2)}) %collective-permute-start.9) | collective-permute-done | bytes 393248 | tf_op jit(solution)/shard_map/ppermute | solution.py:36
  55.7 8.3 %attend_kernel.1 = (bf16[128,192]{1,0:T(8,128)(2,1)}, bf16[128,192]{1,0:T(8,128)(2,1)}, bf16[128,192]{1,0:T(8,128)(2,1)}, bf16[128,192]{1,0:T(8,128)(2,1)}, bf16...) custom-call(s32[6]{0:T(128)} %stack.79.tab, bf16[512,192]{1,0:T(8,128)(2,1)} %get-tuple-element.127.q_ref, ...), custom_call_target="tpu_custom_call" | custom-call | flops 805306368 | bytes 2437144 | tf_op jit(solution)/shard_map/attend_kernel/pallas_call | solution.py:66
  67.3 3.5 %collective-permute-start.19 = (bf16[128,192]{1,0:T(8,128)(2,1)}, bf16[128,192]{1,0:T(8,128)(2,1)S(1)}, u32[]{:S(2)}, u32[]{:S(2)}) collective-permute-start(bf16[128,192]{1,0:T(8,128)(2,1)} %get-tuple-element.147), channel_id=1, source_target_pairs={{0,8},{4,12},{8,0},{12,4},{1,9},{5,13},{9,1},{13,5},{2,10},{6,14},... | collective-permute-start | bytes 147464 | tf_op jit(solution)/shard_map/ppermute | solution.py:36
  74.4 3.5 %collective-permute-start.20 = (bf16[128,192]{1,0:T(8,128)(2,1)}, bf16[128,192]{1,0:T(8,128)(2,1)S(1)}, u32[]{:S(2)}, u32[]{:S(2)}) collective-permute-start(bf16[128,192]{1,0:T(8,128)(2,1)} %get-tuple-element.148), channel_id=1, source_target_pairs={{0,12},{4,8},{8,4},{12,0},{1,13},{5,9},{9,5},{13,1},{2,14},{6,10},... | collective-permute-start | bytes 147464 | tf_op jit(solution)/shard_map/ppermute | solution.py:36
  77.8 2.9 %collective-permute-done.20.a3 = bf16[128,192]{1,0:T(8,128)(2,1)S(1)} collective-permute-done((bf16[128,192]{1,0:T(8,128)(2,1)}, bf16[128,192]{1,0:T(8,128)(2,1)S(1)}, u32[]{:S(2)}, u32[]{:S(2)}) %collective-permute-start.20) | collective-permute-done | bytes 49184 | tf_op jit(solution)/shard_map/ppermute | solution.py:36
  81.5 4.2 %mix_kernel.1 = (f32[128,768]{1,0:T(8,128)}, bf16[128,768]{1,0:T(8,128)(2,1)}, bf16[768,768]{1,0:T(8,128)(2,1)}) custom-call(s32[6]{0:T(128)} %stack.79.tab, bf16[128,192]{1,0:T(8,128)(2,1)} %get-tuple-element.145.a0, bf16[128,192]{1,0:T(8,128)(2,1)} %copy-done.37, bf16[128,192]{1,0:T(8,128)(2,1)} %copy-done.38, bf16[128,192]{1,0:T(8,128)(2,1)} %copy-done.39, ...), custom_call_target="tpu_custom_call" | custom-call | flops 150994944 | bytes 3686424 | tf_op jit(solution)/shard_map/mix_kernel/pallas_call | solution.py:66
  88.8 5.6 %collective-permute-done.27.h2.refs_2_ = bf16[128,768]{1,0:T(8,128)(2,1)S(1)} collective-permute-done((bf16[128,768]{1,0:T(8,128)(2,1)}, bf16[128,768]{1,0:T(8,128)(2,1)S(1)}, u32[]{:S(2)}, u32[]{:S(2)}) %collective-permute-start.27) | collective-permute-done | bytes 196640 | tf_op jit(solution)/shard_map/ppermute | solution.py:36
  96.6 8.5 %ffn_kernel.1 = (bf16[512,768]{1,0:T(8,128)(2,1)}, bf16[512,768]{1,0:T(8,128)(2,1)}, f32[2,128,768]{2,1,0:T(8,128)}, bf16[2,128,768]{2,1,0:T(8,128)(2,1)}, f32[1...) custom-call(s32[6]{0:T(128)} %stack.79.tab, ...), custom_call_target="tpu_custom_call" | custom-call | flops 2415919104 | bytes 7815192 | tf_op jit(solution)/shard_map/ffn_kernel/pallas_call | solution.py:66
  107.2 5.2 %ffn_grad_kernel.1 = (bf16[4,96,768]{2,1,0:T(8,128)(2,1)}, bf16[4,96,768]{2,1,0:T(8,128)(2,1)}, bf16[4,96,768]{2,1,0:T(8,128)(2,1)}, bf16[4,96,768]{2,1,0:T(8,128)(2,1)}) custom-call(s32[6]{0:T(128)} %stack.79.tab, bf16[128,768]{1,0:T(8,128)(2,1)} %get-tuple-element.158.h0.refs_0_, bf16[128,768]{1,0:T(8,128)(2,1)} %copy-done.48, ...), custom_call_target="tpu_custom_call" | custom-call | bytes 1 | tf_op jit(solution)/shard_map/ffn_grad_kernel/pallas_call | solution.py:66
  116.9 3.4 %back_mix_kernel.1 = (f32[128,768]{1,0:T(8,128)}, bf16[128,768]{1,0:T(8,128)(2,1)}, bf16[128,192]{1,0:T(8,128)(2,1)}, bf16[128,192]{1,0:T(8,128)(2,1)}, bf16[128...) custom-call(s32[6]{0:T(128)} %stack.79.tab, f32[128,768]{1,0:T(8,128)} %get-tuple-element.196.resid_ref, ...), custom_call_target="tpu_custom_call" | custom-call | flops 150994944 | bytes 3907608 | tf_op jit(solution)/shard_map/back_mix_kernel/pallas_call | solution.py:66
  131.4 12.6 %back_attend_kernel.1 = (bf16[512,192]{1,0:T(8,128)(2,1)}, bf16[2,512,384]{2,1,0:T(8,128)(2,1)}, bf16[2,512,384]{2,1,0:T(8,128)(2,1)}) custom-call(s32[6]{0:T(128)} %stack.79.tab, bf16[512,192]{1,0:T(8,128)(2,1)} %get-tuple-element.127.q_ref, bf16[512,384]{1,0:T(8,128)(2,1)} %get-tuple-element.131.k0, bf16[512,384]{1,0:T(8,128)(2,1)} %copy-done.58, ...), custom_call_target="tpu_custom_call" | custom-call | flops 2013265920 | bytes 4206616 | tf_op jit(solution)/shard_map/back_attend_kernel/pallas_call | solution.py:66
  151.2 3.1 %out_grad_kernel.1 = (bf16[4,112,768]{2,1,0:T(8,128)(2,1)}, bf16[4,112,768]{2,1,0:T(8,128)(2,1)}) custom-call(s32[6]{0:T(128)} %stack.79.tab, bf16[128,192]{1,0:T(8,128)(2,1)} %get-tuple-element.145.a0, bf16[128,192]{1,0:T(8,128)(2,1)} %copy-done.37, bf16[128,192]{1,0:T(8,128)(2,1)} %copy-done.38, bf16[128,192]{1,0:T(8,128)(2,1)} %copy-done.39, ...), custom_call_target="tpu_custom_call" | custom-call | bytes 1 | tf_op jit(solution)/shard_map/out_grad_kernel/pallas_call | solution.py:66
  161.9 4.4 %back_proj_kernel.1 = (bf16[512,576]{1,0:T(8,128)(2,1)}, f32[128,768]{1,0:T(8,128)}, f32[128,768]{1,0:T(8,128)}, bf16[2,128,768]{2,1,0:T(8,128)(2,1)}, f32[8,768]{1,0:T(8,128)}) custom-call(s32[6]{0:T(128)} %stack.79.tab, bf16[512,192]{1,0:T(8,128)(2,1)} %get-tuple-element.193.dq_ref, bf16[2,512,384]{2,1,0:T(8,128)(2,1)} %get-tuple-element.182.keep, ...), custom_call_target="tpu_custom_call" | custom-call | flops 452984832 | bytes 5627928 | tf_op jit(solution)/shard_map/back_proj_kernel/pallas_call | solution.py:66
  166.3 3.6 %qkv_grad_kernel.1 = (bf16[4,112,576]{2,1,0:T(8,128)(2,1)}, bf16[4,112,576]{2,1,0:T(8,128)(2,1)}) custom-call(s32[6]{0:T(128)} %stack.79.tab, bf16[512,768]{1,0:T(8,128)(2,1)} %get-tuple-element.200.h_ref, bf16[512,576]{1,0:T(8,128)(2,1)} %get-tuple-element.195.dproj_ref, f32[8,768]{1,0:T(8,128)} %get-tuple-element.201.vs_ref), custom_call_target="tpu_custom_call" | custom-call | bytes 1 | tf_op jit(solution)/shard_map/qkv_grad_kernel/pallas_call | solution.py:66
  172.8 6.8 %collective-permute-done.48.by_ref = bf16[2,96,768]{2,1,0:T(8,128)(2,1)S(1)} collective-permute-done((bf16[2,96,768]{2,1,0:T(8,128)(2,1)S(1)}, bf16[2,96,768]{2,1,0:T(8,128)(2,1)S(1)}, u32[]{:S(2)}, u32[]{:S(2)}) %collective-permute-start.48) | collective-permute-done | bytes 294944 | tf_op jit(solution)/shard_map/ppermute | solution.py:36
  209.4 4.3 %collective-permute-start.59 = (bf16[112,768]{1,0:T(8,128)(2,1)S(1)}, bf16[112,768]{1,0:T(8,128)(2,1)S(1)}, u32[]{:S(2)}, u32[]{:S(2)}) collective-permute-start(bf16[112,768]{1,0:T(8,128)(2,1)S(1)} %slice_bitcast_fusion), channel_id=1, source_target_pairs={{0,16},{16,0},{1,17},{17,1},{2,18},{18,2},{3,19},{19,3},{4,20},{20... | collective-permute-start | bytes 516104 | tf_op jit(solution)/shard_map/ppermute | solution.py:36
  217.6 3.4 %collective-permute-done.60 = bf16[96,768]{1,0:T(8,128)(2,1)S(1)} collective-permute-done((bf16[96,768]{1,0:T(8,128)(2,1)}, bf16[96,768]{1,0:T(8,128)(2,1)S(1)}, u32[]{:S(2)}, u32[]{:S(2)}) %collective-permute-start.60) | collective-permute-done | bytes 147488 | tf_op jit(solution)/shard_map/ppermute | solution.py:36
  223.9 3.5 %collective-permute-done.66 = bf16[96,768]{1,0:T(8,128)(2,1)S(1)} collective-permute-done((bf16[96,768]{1,0:T(8,128)(2,1)S(1)}, bf16[96,768]{1,0:T(8,128)(2,1)S(1)}, u32[]{:S(2)}, u32[]{:S(2)}) %collective-permute-start.66) | collective-permute-done | bytes 147488 | tf_op jit(solution)/shard_map/ppermute | solution.py:36
  230.6 7.2 %collective-permute-done.62 = bf16[112,768]{1,0:T(8,128)(2,1)S(1)} collective-permute-done((bf16[112,768]{1,0:T(8,128)(2,1)S(1)}, bf16[112,768]{1,0:T(8,128)(2,1)S(1)}, u32[]{:S(2)}, u32[]{:S(2)}) %collective-permute-start.62) | collective-permute-done | bytes 172064 | tf_op jit(solution)/shard_map/ppermute | solution.py:36
  237.9 6.5 %collective-permute-done.61.got = bf16[2,112,576]{2,1,0:T(8,128)(2,1)S(1)} collective-permute-done((bf16[2,112,576]{2,1,0:T(8,128)(2,1)S(1)}, bf16[2,112,576]{2,1,0:T(8,128)(2,1)S(1)}, u32[]{:S(2)}, u32[]{:S(2)}) %collective-permute-start.61) | collective-permute-done | bytes 258080 | tf_op jit(solution)/shard_map/ppermute | solution.py:36
  (319 shorter events, 135.5 us)
Async XLA Ops:
  3.6 26.5 %collective-permute-start = (bf16[128,768]{1,0:T(8,128)(2,1)}, bf16[128,768]{1,0:T(8,128)(2,1)S(1)}, u32[]{:S(2)}, u32[]{:S(2)}) collective-permute-start(bf16[128,768]{1,0:T(8,128)(2,1)} %get-tuple-element.121.n0), channel_id=1, source_target_pairs={{0,4},{4,0},{8,12},{12,8},{1,5},{5,1},{9,13},{13,9},{2,6},{6,2},{1... | collective-permute-start | bytes 589832 | tf_op jit(solution)/shard_map/ppermute | solution.py:36
  6.7 23.4 %collective-permute-start.1 = (bf16[128,768]{1,0:T(8,128)(2,1)}, bf16[128,768]{1,0:T(8,128)(2,1)S(1)}, u32[]{:S(2)}, u32[]{:S(2)}) collective-permute-start(bf16[128,768]{1,0:T(8,128)(2,1)} %get-tuple-element.121.n0), channel_id=1, source_target_pairs={{0,8},{4,12},{8,0},{12,4},{1,9},{5,13},{9,1},{13,5},{2,10},{6,14},... | collective-permute-start | bytes 589832 | tf_op jit(solution)/shard_map/ppermute | solution.py:36
  9.3 20.8 %collective-permute-start.2 = (bf16[128,768]{1,0:T(8,128)(2,1)}, bf16[128,768]{1,0:T(8,128)(2,1)S(1)}, u32[]{:S(2)}, u32[]{:S(2)}) collective-permute-start(bf16[128,768]{1,0:T(8,128)(2,1)} %get-tuple-element.121.n0), channel_id=1, source_target_pairs={{0,12},{4,8},{8,4},{12,0},{1,13},{5,9},{9,5},{13,1},{2,14},{6,10},... | collective-permute-start | bytes 589832 | tf_op jit(solution)/shard_map/ppermute | solution.py:36
  50.0 15.9 %collective-permute-start.16 = (bf16[2,96,768]{2,1,0:T(8,128)(2,1)}, bf16[2,96,768]{2,1,0:T(8,128)(2,1)S(1)}, u32[]{:S(2)}, u32[]{:S(2)}) collective-permute-start(bf16[2,96,768]{2,1,0:T(8,128)(2,1)} %get-tuple-element.134), channel_id=1, source_target_pairs={{0,17},{1,16},{2,19},{3,18},{16,1},{17,0},{18,3},{19,2},{4,21},{5,... | collective-permute-start | bytes 884744 | tf_op jit(solution)/shard_map/ppermute | solution.py:41
  51.2 14.7 %collective-permute-start.15 = (bf16[2,96,768]{2,1,0:T(8,128)(2,1)}, bf16[2,96,768]{2,1,0:T(8,128)(2,1)}, u32[]{:S(2)}, u32[]{:S(2)}) collective-permute-start(bf16[2,96,768]{2,1,0:T(8,128)(2,1)} %get-tuple-element.143.rest_0_), channel_id=1, source_target_pairs={{0,16},{1,17},{2,18},{3,19},{16,0},{17,1},{18,2},{19,3},{4,20},{5,... | collective-permute-start | bytes 884744 | tf_op jit(solution)/shard_map/ppermute | solution.py:41
  51.8 14.2 %collective-permute-start.17 = (bf16[2,96,768]{2,1,0:T(8,128)(2,1)S(1)}, bf16[2,96,768]{2,1,0:T(8,128)(2,1)S(1)}, u32[]{:S(2)}, u32[]{:S(2)}) collective-permute-start(bf16[2,96,768]{2,1,0:T(8,128)(2,1)S(1)} %pad_maximum_fusion.rest_0_), channel_id=1, source_target_pairs={{0,2},{1,3},{2,0},{3,1},{4,6},{5,7},{6,4},{7,5},{8,10},{9,11},{10,... | collective-permute-start | bytes 884744 | tf_op jit(solution)/shard_map/ppermute | solution.py:36
  53.3 20.3 %collective-permute-start.24 = (bf16[2,96,768]{2,1,0:T(8,128)(2,1)}, bf16[2,96,768]{2,1,0:T(8,128)(2,1)}, u32[]{:S(2)}, u32[]{:S(2)}) collective-permute-start(bf16[2,96,768]{2,1,0:T(8,128)(2,1)} %get-tuple-element.157), channel_id=1, source_target_pairs={{0,3},{1,2},{2,1},{3,0},{16,19},{17,18},{18,17},{19,16},{4,7},{5,6... | collective-permute-start | bytes 884744 | tf_op jit(solution)/shard_map/ppermute | solution.py:41
  53.3 20.3 %collective-permute-start.23 = (bf16[128,768]{1,0:T(8,128)(2,1)S(1)}, bf16[128,768]{1,0:T(8,128)(2,1)S(1)}, u32[]{:S(2)}, u32[]{:S(2)}) collective-permute-start(bf16[128,768]{1,0:T(8,128)(2,1)S(1)} %bitcast_convert_fusion.c0.refs_4_.c_ref), channel_id=1, source_target_pairs={{0,2},{1,3},{2,0},{3,1},{4,6},{5,7},{6,4},{7,5},{8,10},{9,11},{10,... | collective-permute-start | bytes 589832 | tf_op jit(solution)/shard_map/ppermute | solution.py:36
  71.1 14.6 %collective-permute-start.22 = (bf16[2,96,768]{2,1,0:T(8,128)(2,1)}, bf16[2,96,768]{2,1,0:T(8,128)(2,1)S(1)}, u32[]{:S(2)}, u32[]{:S(2)}) collective-permute-start(bf16[2,96,768]{2,1,0:T(8,128)(2,1)} %get-tuple-element.153), channel_id=1, source_target_pairs={{0,18},{1,19},{2,16},{3,17},{16,2},{17,3},{18,0},{19,1},{4,22},{5,... | collective-permute-start | bytes 884744 | tf_op jit(solution)/shard_map/ppermute | solution.py:41
  120.3 23.7 %collective-permute-start.37 = (bf16[4,96,768]{2,1,0:T(8,128)(2,1)S(1)}, bf16[4,96,768]{2,1,0:T(8,128)(2,1)S(1)}, u32[]{:S(2)}, u32[]{:S(2)}) collective-permute-start(bf16[4,96,768]{2,1,0:T(8,128)(2,1)S(1)} %copy-done.56), channel_id=1, source_target_pairs={{0,2},{1,3},{2,0},{3,1},{4,6},{5,7},{6,4},{7,5},{8,10},{9,11},{10,... | collective-permute-start | bytes 1769480 | tf_op jit(solution)/shard_map/ppermute | solution.py:36
  127.5 16.5 %collective-permute-start.38 = (bf16[128,768]{1,0:T(8,128)(2,1)S(1)}, bf16[128,768]{1,0:T(8,128)(2,1)S(1)}, u32[]{:S(2)}, u32[]{:S(2)}) collective-permute-start(bf16[128,768]{1,0:T(8,128)(2,1)S(1)} %fusion.4), channel_id=1, source_target_pairs={{0,2},{1,3},{2,0},{3,1},{4,6},{5,7},{6,4},{7,5},{8,10},{9,11},{10,... | collective-permute-start | bytes 589832 | tf_op jit(solution)/shard_map/ppermute | solution.py:36
  149.2 20.7 %collective-permute-start.46 = (bf16[4,96,768]{2,1,0:T(8,128)(2,1)}, bf16[4,96,768]{2,1,0:T(8,128)(2,1)S(1)}, u32[]{:S(2)}, u32[]{:S(2)}) collective-permute-start(bf16[4,96,768]{2,1,0:T(8,128)(2,1)} %get-tuple-element.163), channel_id=1, source_target_pairs={{0,16},{16,0},{1,17},{17,1},{2,18},{18,2},{3,19},{19,3},{4,20},{20... | collective-permute-start | bytes 1769480 | tf_op jit(solution)/shard_map/ppermute | solution.py:36
  158.5 25.3 %collective-permute-start.45 = (bf16[4,96,768]{2,1,0:T(8,128)(2,1)}, bf16[4,96,768]{2,1,0:T(8,128)(2,1)S(1)}, u32[]{:S(2)}, u32[]{:S(2)}) collective-permute-start(bf16[4,96,768]{2,1,0:T(8,128)(2,1)} %pack_kernel.1), channel_id=1, source_target_pairs={{0,16},{16,0},{1,17},{17,1},{2,18},{18,2},{3,19},{19,3},{4,20},{20... | collective-permute-start | bytes 1769480 | tf_op jit(solution)/shard_map/ppermute | solution.py:36
  169.9 21.7 %collective-permute-start.57 = (bf16[4,112,768]{2,1,0:T(8,128)(2,1)}, bf16[4,112,768]{2,1,0:T(8,128)(2,1)S(1)}, u32[]{:S(2)}, u32[]{:S(2)}) collective-permute-start(bf16[4,112,768]{2,1,0:T(8,128)(2,1)} %get-tuple-element.221), channel_id=1, source_target_pairs={{0,1},{1,0},{2,3},{3,2},{4,5},{5,4},{6,7},{7,6},{8,9},{9,8},{10,11... | collective-permute-start | bytes 2064392 | tf_op jit(solution)/shard_map/ppermute | solution.py:36
  171.1 20.4 %collective-permute-start.43 = (bf16[2,128,768]{2,1,0:T(8,128)(2,1)}, bf16[2,128,768]{2,1,0:T(8,128)(2,1)S(1)}, u32[]{:S(2)}, u32[]{:S(2)}) collective-permute-start(bf16[2,128,768]{2,1,0:T(8,128)(2,1)} %get-tuple-element.199), channel_id=1, source_target_pairs={{0,8},{4,12},{8,0},{12,4},{1,9},{5,13},{9,1},{13,5},{2,10},{6,14},... | collective-permute-start | bytes 1179656 | tf_op jit(solution)/shard_map/ppermute | solution.py:36
  191.8 17.5 %collective-permute-start.58 = (bf16[2,112,768]{2,1,0:T(8,128)(2,1)S(1)}, bf16[2,112,768]{2,1,0:T(8,128)(2,1)S(1)}, u32[]{:S(2)}, u32[]{:S(2)}) collective-permute-start(bf16[2,112,768]{2,1,0:T(8,128)(2,1)S(1)} %slice.126), channel_id=1, source_target_pairs={{0,2},{1,3},{2,0},{3,1},{4,6},{5,7},{6,4},{7,5},{8,10},{9,11},{10,... | collective-permute-start | bytes 1032200 | tf_op jit(solution)/shard_map/ppermute | solution.py:36
  195.1 19.1 %collective-permute-start.50 = (bf16[128,768]{1,0:T(8,128)(2,1)S(1)}, bf16[128,768]{1,0:T(8,128)(2,1)S(1)}, u32[]{:S(2)}, u32[]{:S(2)}) collective-permute-start(bf16[128,768]{1,0:T(8,128)(2,1)S(1)} %fusion.1), channel_id=1, source_target_pairs={{0,4},{4,0},{8,12},{12,8},{1,5},{5,1},{9,13},{13,9},{2,6},{6,2},{1... | collective-permute-start | bytes 589832 | tf_op jit(solution)/shard_map/ppermute | solution.py:36
  206.8 14.1 %collective-permute-start.60 = (bf16[96,768]{1,0:T(8,128)(2,1)}, bf16[96,768]{1,0:T(8,128)(2,1)S(1)}, u32[]{:S(2)}, u32[]{:S(2)}) collective-permute-start(bf16[96,768]{1,0:T(8,128)(2,1)} %get-tuple-element.217), channel_id=1, source_target_pairs={{0,8},{4,12},{8,0},{12,4},{1,9},{5,13},{9,1},{13,5},{2,10},{6,14},... | collective-permute-start | bytes 442376 | tf_op jit(solution)/shard_map/ppermute | solution.py:36
  213.8 13.6 %collective-permute-start.66 = (bf16[96,768]{1,0:T(8,128)(2,1)S(1)}, bf16[96,768]{1,0:T(8,128)(2,1)S(1)}, u32[]{:S(2)}, u32[]{:S(2)}) collective-permute-start(bf16[96,768]{1,0:T(8,128)(2,1)S(1)} %add_convert_fusion.10), channel_id=1, source_target_pairs={{0,8},{4,12},{8,0},{12,4},{1,9},{5,13},{9,1},{13,5},{2,10},{6,14},... | collective-permute-start | bytes 442376 | tf_op jit(solution)/shard_map/ppermute | solution.py:36
  221.1 16.6 %collective-permute-start.62 = (bf16[112,768]{1,0:T(8,128)(2,1)S(1)}, bf16[112,768]{1,0:T(8,128)(2,1)S(1)}, u32[]{:S(2)}, u32[]{:S(2)}) collective-permute-start(bf16[112,768]{1,0:T(8,128)(2,1)S(1)} %fusion.2), channel_id=1, source_target_pairs={{0,4},{4,0},{8,12},{12,8},{1,5},{5,1},{9,13},{13,9},{2,6},{6,2},{1... | collective-permute-start | bytes 516104 | tf_op jit(solution)/shard_map/ppermute | solution.py:36
  227.5 21.2 %collective-permute-start.67 = (bf16[2,96,768]{2,1,0:T(8,128)(2,1)S(1)}, bf16[2,96,768]{2,1,0:T(8,128)(2,1)S(1)}, u32[]{:S(2)}, u32[]{:S(2)}) collective-permute-start(bf16[2,96,768]{2,1,0:T(8,128)(2,1)S(1)} %pad_maximum_fusion.2.pair), channel_id=1, source_target_pairs={{0,4},{4,0},{8,12},{12,8},{1,5},{5,1},{9,13},{13,9},{2,6},{6,2},{1... | collective-permute-start | bytes 884744 | tf_op jit(solution)/shard_map/ppermute | solution.py:36
  227.5 16.9 %collective-permute-start.61 = (bf16[2,112,576]{2,1,0:T(8,128)(2,1)S(1)}, bf16[2,112,576]{2,1,0:T(8,128)(2,1)S(1)}, u32[]{:S(2)}, u32[]{:S(2)}) collective-permute-start(bf16[2,112,576]{2,1,0:T(8,128)(2,1)S(1)} %pad_maximum_fusion.4.pair), channel_id=1, source_target_pairs={{0,8},{4,12},{8,0},{12,4},{1,9},{5,13},{9,1},{13,5},{2,10},{6,14},... | collective-permute-start | bytes 774152 | tf_op jit(solution)/shard_map/ppermute | solution.py:36
  230.5 23.1 %collective-permute-start.65 = (bf16[2,96,768]{2,1,0:T(8,128)(2,1)S(1)}, bf16[2,96,768]{2,1,0:T(8,128)(2,1)S(1)}, u32[]{:S(2)}, u32[]{:S(2)}) collective-permute-start(bf16[2,96,768]{2,1,0:T(8,128)(2,1)S(1)} %pad_maximum_fusion.1.pair), channel_id=1, source_target_pairs={{0,4},{4,0},{8,12},{12,8},{1,5},{5,1},{9,13},{13,9},{2,6},{6,2},{1... | collective-permute-start | bytes 884744 | tf_op jit(solution)/shard_map/ppermute | solution.py:36
  237.8 13.7 %collective-permute-start.63 = (bf16[112,768]{1,0:T(8,128)(2,1)S(1)}, bf16[112,768]{1,0:T(8,128)(2,1)S(1)}, u32[]{:S(2)}, u32[]{:S(2)}) collective-permute-start(bf16[112,768]{1,0:T(8,128)(2,1)S(1)} %add_convert_fusion.8), channel_id=1, source_target_pairs={{0,8},{4,12},{8,0},{12,4},{1,9},{5,13},{9,1},{13,5},{2,10},{6,14},... | collective-permute-start | bytes 516104 | tf_op jit(solution)/shard_map/ppermute | solution.py:36
  (113 other events, 812.8 us)

commit v4 on v3

--- a/solution.py
+++ b/solution.py
@@ -697,7 +697,7 @@
     kcode = jnp.where(valid > 0, kseg, kplace + 64)
     qcodes = jnp.stack([kseg[:GROUP], kplace[:GROUP] + 64])
 
-    n1, q_cols, k_rows = lax.optimization_barrier((n1, qcodes.T, kcode[None, :]))
+    n1, k_rows = lax.optimization_barrier((n1, kcode[None, :]))
     q, kv, h1, w_qkv, vv = call(
         functools.partial(qkv_kernel, four_bits),
         [
@@ -712,6 +712,7 @@
     )
     q_rows, late = lax.optimization_barrier((qcodes, kcode, kv))[:2]
     k_cols = late[:, None]
+    q_cols = q_rows.T
     cb = cot.astype(BF16)
     if near:
         kv_y = swap(after(kv, w_parts[2]), "blk", 2)

time: 257 us -> 252 us (0.981)
    unnamed x138 -> x136, local copies, waits for them, and re-layouts: 11.9 us -> 11.2 us
  transfers between devices with their start and end apart: 68 -> 68, of which waited for: 29 -> 28; matrix products, arithmetic and copies ran while one was open for 5% -> 4% of each run, Pallas kernels for 26% -> 27%
where the time goes in v4:
time: 252 us; the launch traced here: 251 us
  Pallas kernels  84 us (33%)
  waiting for transfers between devices  74.5 us (30%)
  starting transfers between devices  66.2 us (26%)
  local copies, waits for them, and re-layouts  17.5 us (7%)
  other arithmetic  7.24 us (3%)
    pallas_call x22, Pallas kernels, call(): pl.pallas_call(kernel, name=getattr(kernel, 'func', kernel).__name__, out...  84 us
    ppermute x61, waiting for transfers between devices, swap(): return lax.ppermute(array, axis, [(i, i ^ by) for i in range(peers)])  70.8 us
    ppermute x61, starting transfers between devices, swap(): return lax.ppermute(array, axis, [(i, i ^ by) for i in range(peers)])  59.5 us
    unnamed x136, local copies, waits for them, and re-layouts  11.2 us
    ppermute x7, starting transfers between devices, cross(): lax.ppermute(array, ('dp', 'blk'), [(i, i ^ by) for i in range(peers)])  6.71 us
  transfers between devices with their start and end apart: 68, of which 28 were waited for; matrix products, arithmetic and copies ran while one was open for 4% of the time, Pallas kernels for 27%

profile of v4, /device:TPU:0, one launch (start us, length us, event | category | flops | bytes accessed | tf_op | source)
XLA Modules:
  0.0 251.0 jit_solution(17568344185265777522)
XLA Ops:
  3.6 3.0 %collective-permute-start.3 = (bf16[112,576]{1,0:T(8,128)(2,1)}, bf16[112,576]{1,0:T(8,128)(2,1)S(1)}, u32[]{:S(2)}, u32[]{:S(2)}) collective-permute-start(bf16[112,576]{1,0:T(8,128)(2,1)} %get-tuple-element.124), channel_id=1, source_target_pairs={{0,16},{16,0},{1,17},{17,1},{2,18},{18,2},{3,19},{19,3},{4,20},{20... | collective-permute-start | bytes 387080 | tf_op jit(solution)/shard_map/ppermute | solution.py:36
  13.5 6.0 %collective-permute-done.4.rest_1_ = bf16[2,112,576]{2,1,0:T(8,128)(2,1)S(1)} collective-permute-done((bf16[2,112,576]{2,1,0:T(8,128)(2,1)S(1)}, bf16[2,112,576]{2,1,0:T(8,128)(2,1)S(1)}, u32[]{:S(2)}, u32[]{:S(2)}) %collective-permute-start.4) | collective-permute-done | bytes 258080 | tf_op jit(solution)/shard_map/ppermute | solution.py:36
  27.7 3.5 %qkv_kernel.1 = (bf16[512,192]{1,0:T(8,128)(2,1)}, bf16[512,384]{1,0:T(8,128)(2,1)}, bf16[512,768]{1,0:T(8,128)(2,1)}, bf16[768,576]{1,0:T(8,128)(2,1)}, bf16[8,16,576]{2,1,0:T(8,128)(2,1)}) custom-call(s32[6]{0:T(128)} %stack.79.tab, bf16[128,768]{1,0:T(8,128)(2,1)} %get-tuple-element.120.n0, bf16[128,768]{1,0:T(8,128)(2,1)} %copy-done.16, ...), custom_call_target="tpu_custom_call" | custom-call | flops 452984832 | bytes 4227096 | tf_op jit(solution)/shard_map/qkv_kernel/pallas_call | solution.py:66
  37.9 6.3 %collective-permute-done.9.k2 = bf16[512,384]{1,0:T(8,128)(2,1)S(1)} collective-permute-done((bf16[512,384]{1,0:T(8,128)(2,1)}, bf16[512,384]{1,0:T(8,128)(2,1)S(1)}, u32[]{:S(2)}, u32[]{:S(2)}) %collective-permute-start.9) | collective-permute-done | bytes 393248 | tf_op jit(solution)/shard_map/ppermute | solution.py:36
  50.0 8.3 %attend_kernel.1 = (bf16[128,192]{1,0:T(8,128)(2,1)}, bf16[128,192]{1,0:T(8,128)(2,1)}, bf16[128,192]{1,0:T(8,128)(2,1)}, bf16[128,192]{1,0:T(8,128)(2,1)}, bf16...) custom-call(s32[6]{0:T(128)} %stack.79.tab, bf16[512,192]{1,0:T(8,128)(2,1)} %get-tuple-element.126.q_ref, ...), custom_call_target="tpu_custom_call" | custom-call | flops 805306368 | bytes 2437144 | tf_op jit(solution)/shard_map/attend_kernel/pallas_call | solution.py:66
  68.7 3.2 %collective-permute-start.20 = (bf16[128,192]{1,0:T(8,128)(2,1)}, bf16[128,192]{1,0:T(8,128)(2,1)S(1)}, u32[]{:S(2)}, u32[]{:S(2)}) collective-permute-start(bf16[128,192]{1,0:T(8,128)(2,1)} %get-tuple-element.147), channel_id=1, source_target_pairs={{0,12},{4,8},{8,4},{12,0},{1,13},{5,9},{9,5},{13,1},{2,14},{6,10},... | collective-permute-start | bytes 147464 | tf_op jit(solution)/shard_map/ppermute | solution.py:36
  71.9 3.2 %collective-permute-done.20.a3 = bf16[128,192]{1,0:T(8,128)(2,1)S(1)} collective-permute-done((bf16[128,192]{1,0:T(8,128)(2,1)}, bf16[128,192]{1,0:T(8,128)(2,1)S(1)}, u32[]{:S(2)}, u32[]{:S(2)}) %collective-permute-start.20) | collective-permute-done | bytes 49184 | tf_op jit(solution)/shard_map/ppermute | solution.py:36
  75.8 4.2 %mix_kernel.1 = (f32[128,768]{1,0:T(8,128)}, bf16[128,768]{1,0:T(8,128)(2,1)}, bf16[768,768]{1,0:T(8,128)(2,1)}) custom-call(s32[6]{0:T(128)} %stack.79.tab, bf16[128,192]{1,0:T(8,128)(2,1)} %get-tuple-element.144.a0, bf16[128,192]{1,0:T(8,128)(2,1)} %copy-done.37, bf16[128,192]{1,0:T(8,128)(2,1)} %copy-done.38, bf16[128,192]{1,0:T(8,128)(2,1)} %copy-done.39, ...), custom_call_target="tpu_custom_call" | custom-call | flops 150994944 | bytes 3686424 | tf_op jit(solution)/shard_map/mix_kernel/pallas_call | solution.py:66
  83.3 5.5 %collective-permute-done.27.h2.refs_2_ = bf16[128,768]{1,0:T(8,128)(2,1)S(1)} collective-permute-done((bf16[128,768]{1,0:T(8,128)(2,1)}, bf16[128,768]{1,0:T(8,128)(2,1)S(1)}, u32[]{:S(2)}, u32[]{:S(2)}) %collective-permute-start.27) | collective-permute-done | bytes 196640 | tf_op jit(solution)/shard_map/ppermute | solution.py:36
  91.0 8.6 %ffn_kernel.1 = (bf16[512,768]{1,0:T(8,128)(2,1)}, bf16[512,768]{1,0:T(8,128)(2,1)}, f32[2,128,768]{2,1,0:T(8,128)}, bf16[2,128,768]{2,1,0:T(8,128)(2,1)}, f32[1...) custom-call(s32[6]{0:T(128)} %stack.79.tab, ...), custom_call_target="tpu_custom_call" | custom-call | flops 2415919104 | bytes 7815192 | tf_op jit(solution)/shard_map/ffn_kernel/pallas_call | solution.py:66
  101.7 5.3 %ffn_grad_kernel.1 = (bf16[4,96,768]{2,1,0:T(8,128)(2,1)}, bf16[4,96,768]{2,1,0:T(8,128)(2,1)}, bf16[4,96,768]{2,1,0:T(8,128)(2,1)}, bf16[4,96,768]{2,1,0:T(8,128)(2,1)}) custom-call(s32[6]{0:T(128)} %stack.79.tab, bf16[128,768]{1,0:T(8,128)(2,1)} %get-tuple-element.157.h0.refs_0_, bf16[128,768]{1,0:T(8,128)(2,1)} %copy-done.48, ...), custom_call_target="tpu_custom_call" | custom-call | bytes 1 | tf_op jit(solution)/shard_map/ffn_grad_kernel/pallas_call | solution.py:66
  111.3 3.4 %back_mix_kernel.1 = (f32[128,768]{1,0:T(8,128)}, bf16[128,768]{1,0:T(8,128)(2,1)}, bf16[128,192]{1,0:T(8,128)(2,1)}, bf16[128,192]{1,0:T(8,128)(2,1)}, bf16[128...) custom-call(s32[6]{0:T(128)} %stack.79.tab, f32[128,768]{1,0:T(8,128)} %get-tuple-element.194.resid_ref, ...), custom_call_target="tpu_custom_call" | custom-call | flops 150994944 | bytes 3907608 | tf_op jit(solution)/shard_map/back_mix_kernel/pallas_call | solution.py:66
  125.9 12.6 %back_attend_kernel.1 = (bf16[512,192]{1,0:T(8,128)(2,1)}, bf16[2,512,384]{2,1,0:T(8,128)(2,1)}, bf16[2,512,384]{2,1,0:T(8,128)(2,1)}) custom-call(s32[6]{0:T(128)} %stack.79.tab, bf16[512,192]{1,0:T(8,128)(2,1)} %get-tuple-element.126.q_ref, bf16[512,384]{1,0:T(8,128)(2,1)} %get-tuple-element.130.k0, bf16[512,384]{1,0:T(8,128)(2,1)} %copy-done.58, ...), custom_call_target="tpu_custom_call" | custom-call | flops 2013265920 | bytes 4206616 | tf_op jit(solution)/shard_map/back_attend_kernel/pallas_call | solution.py:66
  145.7 3.1 %out_grad_kernel.1 = (bf16[4,112,768]{2,1,0:T(8,128)(2,1)}, bf16[4,112,768]{2,1,0:T(8,128)(2,1)}) custom-call(s32[6]{0:T(128)} %stack.79.tab, bf16[128,192]{1,0:T(8,128)(2,1)} %get-tuple-element.144.a0, bf16[128,192]{1,0:T(8,128)(2,1)} %copy-done.37, bf16[128,192]{1,0:T(8,128)(2,1)} %copy-done.38, bf16[128,192]{1,0:T(8,128)(2,1)} %copy-done.39, ...), custom_call_target="tpu_custom_call" | custom-call | bytes 1 | tf_op jit(solution)/shard_map/out_grad_kernel/pallas_call | solution.py:66
  156.3 4.4 %back_proj_kernel.1 = (bf16[512,576]{1,0:T(8,128)(2,1)}, f32[128,768]{1,0:T(8,128)}, f32[128,768]{1,0:T(8,128)}, bf16[2,128,768]{2,1,0:T(8,128)(2,1)}, f32[8,768]{1,0:T(8,128)}) custom-call(s32[6]{0:T(128)} %stack.79.tab, bf16[512,192]{1,0:T(8,128)(2,1)} %get-tuple-element.191.dq_ref, bf16[2,512,384]{2,1,0:T(8,128)(2,1)} %get-tuple-element.180.keep, ...), custom_call_target="tpu_custom_call" | custom-call | flops 452984832 | bytes 5627928 | tf_op jit(solution)/shard_map/back_proj_kernel/pallas_call | solution.py:66
  160.7 3.6 %qkv_grad_kernel.1 = (bf16[4,112,576]{2,1,0:T(8,128)(2,1)}, bf16[4,112,576]{2,1,0:T(8,128)(2,1)}) custom-call(s32[6]{0:T(128)} %stack.79.tab, bf16[512,768]{1,0:T(8,128)(2,1)} %get-tuple-element.198.h_ref, bf16[512,576]{1,0:T(8,128)(2,1)} %get-tuple-element.193.dproj_ref, f32[8,768]{1,0:T(8,128)} %get-tuple-element.199.vs_ref), custom_call_target="tpu_custom_call" | custom-call | bytes 1 | tf_op jit(solution)/shard_map/qkv_grad_kernel/pallas_call | solution.py:66
  167.1 7.0 %collective-permute-done.48.by_ref = bf16[2,96,768]{2,1,0:T(8,128)(2,1)S(1)} collective-permute-done((bf16[2,96,768]{2,1,0:T(8,128)(2,1)S(1)}, bf16[2,96,768]{2,1,0:T(8,128)(2,1)S(1)}, u32[]{:S(2)}, u32[]{:S(2)}) %collective-permute-start.48) | collective-permute-done | bytes 294944 | tf_op jit(solution)/shard_map/ppermute | solution.py:36
  203.8 4.3 %collective-permute-start.59 = (bf16[112,768]{1,0:T(8,128)(2,1)S(1)}, bf16[112,768]{1,0:T(8,128)(2,1)S(1)}, u32[]{:S(2)}, u32[]{:S(2)}) collective-permute-start(bf16[112,768]{1,0:T(8,128)(2,1)S(1)} %slice_bitcast_fusion), channel_id=1, source_target_pairs={{0,16},{16,0},{1,17},{17,1},{2,18},{18,2},{3,19},{19,3},{4,20},{20... | collective-permute-start | bytes 516104 | tf_op jit(solution)/shard_map/ppermute | solution.py:36
  211.7 3.7 %collective-permute-done.60 = bf16[96,768]{1,0:T(8,128)(2,1)S(1)} collective-permute-done((bf16[96,768]{1,0:T(8,128)(2,1)}, bf16[96,768]{1,0:T(8,128)(2,1)S(1)}, u32[]{:S(2)}, u32[]{:S(2)}) %collective-permute-start.60) | collective-permute-done | bytes 147488 | tf_op jit(solution)/shard_map/ppermute | solution.py:36
  215.6 2.8 %collective-permute-start.62 = (bf16[112,768]{1,0:T(8,128)(2,1)S(1)}, bf16[112,768]{1,0:T(8,128)(2,1)S(1)}, u32[]{:S(2)}, u32[]{:S(2)}) collective-permute-start(bf16[112,768]{1,0:T(8,128)(2,1)S(1)} %fusion.2), channel_id=1, source_target_pairs={{0,4},{4,0},{8,12},{12,8},{1,5},{5,1},{9,13},{13,9},{2,6},{6,2},{1... | collective-permute-start | bytes 516104 | tf_op jit(solution)/shard_map/ppermute | solution.py:36
  218.4 3.4 %collective-permute-done.66 = bf16[96,768]{1,0:T(8,128)(2,1)S(1)} collective-permute-done((bf16[96,768]{1,0:T(8,128)(2,1)S(1)}, bf16[96,768]{1,0:T(8,128)(2,1)S(1)}, u32[]{:S(2)}, u32[]{:S(2)}) %collective-permute-start.66) | collective-permute-done | bytes 147488 | tf_op jit(solution)/shard_map/ppermute | solution.py:36
  222.0 2.8 %collective-permute-start.61 = (bf16[2,112,576]{2,1,0:T(8,128)(2,1)S(1)}, bf16[2,112,576]{2,1,0:T(8,128)(2,1)S(1)}, u32[]{:S(2)}, u32[]{:S(2)}) collective-permute-start(bf16[2,112,576]{2,1,0:T(8,128)(2,1)S(1)} %pad_maximum_fusion.4.pair), channel_id=1, source_target_pairs={{0,8},{4,12},{8,0},{12,4},{1,9},{5,13},{9,1},{13,5},{2,10},{6,14},... | collective-permute-start | bytes 774152 | tf_op jit(solution)/shard_map/ppermute | solution.py:36
  225.0 7.2 %collective-permute-done.62 = bf16[112,768]{1,0:T(8,128)(2,1)S(1)} collective-permute-done((bf16[112,768]{1,0:T(8,128)(2,1)S(1)}, bf16[112,768]{1,0:T(8,128)(2,1)S(1)}, u32[]{:S(2)}, u32[]{:S(2)}) %collective-permute-start.62) | collective-permute-done | bytes 172064 | tf_op jit(solution)/shard_map/ppermute | solution.py:36
  232.3 6.5 %collective-permute-done.61.got = bf16[2,112,576]{2,1,0:T(8,128)(2,1)S(1)} collective-permute-done((bf16[2,112,576]{2,1,0:T(8,128)(2,1)S(1)}, bf16[2,112,576]{2,1,0:T(8,128)(2,1)S(1)}, u32[]{:S(2)}, u32[]{:S(2)}) %collective-permute-start.61) | collective-permute-done | bytes 258080 | tf_op jit(solution)/shard_map/ppermute | solution.py:36
  (317 shorter events, 127.5 us)
Async XLA Ops:
  6.6 19.7 %collective-permute-start = (bf16[128,768]{1,0:T(8,128)(2,1)}, bf16[128,768]{1,0:T(8,128)(2,1)S(1)}, u32[]{:S(2)}, u32[]{:S(2)}) collective-permute-start(bf16[128,768]{1,0:T(8,128)(2,1)} %get-tuple-element.120.n0), channel_id=1, source_target_pairs={{0,4},{4,0},{8,12},{12,8},{1,5},{5,1},{9,13},{13,9},{2,6},{6,2},{1... | collective-permute-start | bytes 589832 | tf_op jit(solution)/shard_map/ppermute | solution.py:36
  8.2 18.1 %collective-permute-start.1 = (bf16[128,768]{1,0:T(8,128)(2,1)}, bf16[128,768]{1,0:T(8,128)(2,1)S(1)}, u32[]{:S(2)}, u32[]{:S(2)}) collective-permute-start(bf16[128,768]{1,0:T(8,128)(2,1)} %get-tuple-element.120.n0), channel_id=1, source_target_pairs={{0,8},{4,12},{8,0},{12,4},{1,9},{5,13},{9,1},{13,5},{2,10},{6,14},... | collective-permute-start | bytes 589832 | tf_op jit(solution)/shard_map/ppermute | solution.py:36
  10.8 15.5 %collective-permute-start.2 = (bf16[128,768]{1,0:T(8,128)(2,1)}, bf16[128,768]{1,0:T(8,128)(2,1)S(1)}, u32[]{:S(2)}, u32[]{:S(2)}) collective-permute-start(bf16[128,768]{1,0:T(8,128)(2,1)} %get-tuple-element.120.n0), channel_id=1, source_target_pairs={{0,12},{4,8},{8,4},{12,0},{1,13},{5,9},{9,5},{13,1},{2,14},{6,10},... | collective-permute-start | bytes 589832 | tf_op jit(solution)/shard_map/ppermute | solution.py:36
  44.2 16.0 %collective-permute-start.16 = (bf16[2,96,768]{2,1,0:T(8,128)(2,1)}, bf16[2,96,768]{2,1,0:T(8,128)(2,1)S(1)}, u32[]{:S(2)}, u32[]{:S(2)}) collective-permute-start(bf16[2,96,768]{2,1,0:T(8,128)(2,1)} %get-tuple-element.133), channel_id=1, source_target_pairs={{0,17},{1,16},{2,19},{3,18},{16,1},{17,0},{18,3},{19,2},{4,21},{5,... | collective-permute-start | bytes 884744 | tf_op jit(solution)/shard_map/ppermute | solution.py:41
  45.8 14.4 %collective-permute-start.15 = (bf16[2,96,768]{2,1,0:T(8,128)(2,1)}, bf16[2,96,768]{2,1,0:T(8,128)(2,1)}, u32[]{:S(2)}, u32[]{:S(2)}) collective-permute-start(bf16[2,96,768]{2,1,0:T(8,128)(2,1)} %get-tuple-element.142.rest_0_), channel_id=1, source_target_pairs={{0,16},{1,17},{2,18},{3,19},{16,0},{17,1},{18,2},{19,3},{4,20},{5,... | collective-permute-start | bytes 884744 | tf_op jit(solution)/shard_map/ppermute | solution.py:41
  46.4 13.8 %collective-permute-start.17 = (bf16[2,96,768]{2,1,0:T(8,128)(2,1)S(1)}, bf16[2,96,768]{2,1,0:T(8,128)(2,1)S(1)}, u32[]{:S(2)}, u32[]{:S(2)}) collective-permute-start(bf16[2,96,768]{2,1,0:T(8,128)(2,1)S(1)} %pad_maximum_fusion.rest_0_), channel_id=1, source_target_pairs={{0,2},{1,3},{2,0},{3,1},{4,6},{5,7},{6,4},{7,5},{8,10},{9,11},{10,... | collective-permute-start | bytes 884744 | tf_op jit(solution)/shard_map/ppermute | solution.py:36
  47.9 19.9 %collective-permute-start.24 = (bf16[2,96,768]{2,1,0:T(8,128)(2,1)}, bf16[2,96,768]{2,1,0:T(8,128)(2,1)}, u32[]{:S(2)}, u32[]{:S(2)}) collective-permute-start(bf16[2,96,768]{2,1,0:T(8,128)(2,1)} %get-tuple-element.156), channel_id=1, source_target_pairs={{0,3},{1,2},{2,1},{3,0},{16,19},{17,18},{18,17},{19,16},{4,7},{5,6... | collective-permute-start | bytes 884744 | tf_op jit(solution)/shard_map/ppermute | solution.py:41
  48.0 19.9 %collective-permute-start.23 = (bf16[128,768]{1,0:T(8,128)(2,1)S(1)}, bf16[128,768]{1,0:T(8,128)(2,1)S(1)}, u32[]{:S(2)}, u32[]{:S(2)}) collective-permute-start(bf16[128,768]{1,0:T(8,128)(2,1)S(1)} %bitcast_convert_fusion.c0.refs_4_.c_ref), channel_id=1, source_target_pairs={{0,2},{1,3},{2,0},{3,1},{4,6},{5,7},{6,4},{7,5},{8,10},{9,11},{10,... | collective-permute-start | bytes 589832 | tf_op jit(solution)/shard_map/ppermute | solution.py:36
  65.4 14.6 %collective-permute-start.22 = (bf16[2,96,768]{2,1,0:T(8,128)(2,1)}, bf16[2,96,768]{2,1,0:T(8,128)(2,1)S(1)}, u32[]{:S(2)}, u32[]{:S(2)}) collective-permute-start(bf16[2,96,768]{2,1,0:T(8,128)(2,1)} %get-tuple-element.152), channel_id=1, source_target_pairs={{0,18},{1,19},{2,16},{3,17},{16,2},{17,3},{18,0},{19,1},{4,22},{5,... | collective-permute-start | bytes 884744 | tf_op jit(solution)/shard_map/ppermute | solution.py:41
  114.7 23.7 %collective-permute-start.37 = (bf16[4,96,768]{2,1,0:T(8,128)(2,1)S(1)}, bf16[4,96,768]{2,1,0:T(8,128)(2,1)S(1)}, u32[]{:S(2)}, u32[]{:S(2)}) collective-permute-start(bf16[4,96,768]{2,1,0:T(8,128)(2,1)S(1)} %copy-done.56), channel_id=1, source_target_pairs={{0,2},{1,3},{2,0},{3,1},{4,6},{5,7},{6,4},{7,5},{8,10},{9,11},{10,... | collective-permute-start | bytes 1769480 | tf_op jit(solution)/shard_map/ppermute | solution.py:36
  122.0 16.5 %collective-permute-start.38 = (bf16[128,768]{1,0:T(8,128)(2,1)S(1)}, bf16[128,768]{1,0:T(8,128)(2,1)S(1)}, u32[]{:S(2)}, u32[]{:S(2)}) collective-permute-start(bf16[128,768]{1,0:T(8,128)(2,1)S(1)} %fusion.4), channel_id=1, source_target_pairs={{0,2},{1,3},{2,0},{3,1},{4,6},{5,7},{6,4},{7,5},{8,10},{9,11},{10,... | collective-permute-start | bytes 589832 | tf_op jit(solution)/shard_map/ppermute | solution.py:36
  143.7 20.7 %collective-permute-start.46 = (bf16[4,96,768]{2,1,0:T(8,128)(2,1)}, bf16[4,96,768]{2,1,0:T(8,128)(2,1)S(1)}, u32[]{:S(2)}, u32[]{:S(2)}) collective-permute-start(bf16[4,96,768]{2,1,0:T(8,128)(2,1)} %get-tuple-element.162), channel_id=1, source_target_pairs={{0,16},{16,0},{1,17},{17,1},{2,18},{18,2},{3,19},{19,3},{4,20},{20... | collective-permute-start | bytes 1769480 | tf_op jit(solution)/shard_map/ppermute | solution.py:36
  153.0 25.2 %collective-permute-start.45 = (bf16[4,96,768]{2,1,0:T(8,128)(2,1)}, bf16[4,96,768]{2,1,0:T(8,128)(2,1)S(1)}, u32[]{:S(2)}, u32[]{:S(2)}) collective-permute-start(bf16[4,96,768]{2,1,0:T(8,128)(2,1)} %pack_kernel.1), channel_id=1, source_target_pairs={{0,16},{16,0},{1,17},{17,1},{2,18},{18,2},{3,19},{19,3},{4,20},{20... | collective-permute-start | bytes 1769480 | tf_op jit(solution)/shard_map/ppermute | solution.py:36
  164.3 21.7 %collective-permute-start.57 = (bf16[4,112,768]{2,1,0:T(8,128)(2,1)}, bf16[4,112,768]{2,1,0:T(8,128)(2,1)S(1)}, u32[]{:S(2)}, u32[]{:S(2)}) collective-permute-start(bf16[4,112,768]{2,1,0:T(8,128)(2,1)} %get-tuple-element.219), channel_id=1, source_target_pairs={{0,1},{1,0},{2,3},{3,2},{4,5},{5,4},{6,7},{7,6},{8,9},{9,8},{10,11... | collective-permute-start | bytes 2064392 | tf_op jit(solution)/shard_map/ppermute | solution.py:36
  165.6 20.4 %collective-permute-start.43 = (bf16[2,128,768]{2,1,0:T(8,128)(2,1)}, bf16[2,128,768]{2,1,0:T(8,128)(2,1)S(1)}, u32[]{:S(2)}, u32[]{:S(2)}) collective-permute-start(bf16[2,128,768]{2,1,0:T(8,128)(2,1)} %get-tuple-element.197), channel_id=1, source_target_pairs={{0,8},{4,12},{8,0},{12,4},{1,9},{5,13},{9,1},{13,5},{2,10},{6,14},... | collective-permute-start | bytes 1179656 | tf_op jit(solution)/shard_map/ppermute | solution.py:36
  186.3 17.4 %collective-permute-start.58 = (bf16[2,112,768]{2,1,0:T(8,128)(2,1)S(1)}, bf16[2,112,768]{2,1,0:T(8,128)(2,1)S(1)}, u32[]{:S(2)}, u32[]{:S(2)}) collective-permute-start(bf16[2,112,768]{2,1,0:T(8,128)(2,1)S(1)} %slice.126), channel_id=1, source_target_pairs={{0,2},{1,3},{2,0},{3,1},{4,6},{5,7},{6,4},{7,5},{8,10},{9,11},{10,... | collective-permute-start | bytes 1032200 | tf_op jit(solution)/shard_map/ppermute | solution.py:36
  189.6 18.8 %collective-permute-start.50 = (bf16[128,768]{1,0:T(8,128)(2,1)S(1)}, bf16[128,768]{1,0:T(8,128)(2,1)S(1)}, u32[]{:S(2)}, u32[]{:S(2)}) collective-permute-start(bf16[128,768]{1,0:T(8,128)(2,1)S(1)} %fusion.1), channel_id=1, source_target_pairs={{0,4},{4,0},{8,12},{12,8},{1,5},{5,1},{9,13},{13,9},{2,6},{6,2},{1... | collective-permute-start | bytes 589832 | tf_op jit(solution)/shard_map/ppermute | solution.py:36
  201.3 14.1 %collective-permute-start.60 = (bf16[96,768]{1,0:T(8,128)(2,1)}, bf16[96,768]{1,0:T(8,128)(2,1)S(1)}, u32[]{:S(2)}, u32[]{:S(2)}) collective-permute-start(bf16[96,768]{1,0:T(8,128)(2,1)} %get-tuple-element.215), channel_id=1, source_target_pairs={{0,8},{4,12},{8,0},{12,4},{1,9},{5,13},{9,1},{13,5},{2,10},{6,14},... | collective-permute-start | bytes 442376 | tf_op jit(solution)/shard_map/ppermute | solution.py:36
  208.2 13.7 %collective-permute-start.66 = (bf16[96,768]{1,0:T(8,128)(2,1)S(1)}, bf16[96,768]{1,0:T(8,128)(2,1)S(1)}, u32[]{:S(2)}, u32[]{:S(2)}) collective-permute-start(bf16[96,768]{1,0:T(8,128)(2,1)S(1)} %add_convert_fusion.10), channel_id=1, source_target_pairs={{0,8},{4,12},{8,0},{12,4},{1,9},{5,13},{9,1},{13,5},{2,10},{6,14},... | collective-permute-start | bytes 442376 | tf_op jit(solution)/shard_map/ppermute | solution.py:36
  215.6 16.6 %collective-permute-start.62 = (bf16[112,768]{1,0:T(8,128)(2,1)S(1)}, bf16[112,768]{1,0:T(8,128)(2,1)S(1)}, u32[]{:S(2)}, u32[]{:S(2)}) collective-permute-start(bf16[112,768]{1,0:T(8,128)(2,1)S(1)} %fusion.2), channel_id=1, source_target_pairs={{0,4},{4,0},{8,12},{12,8},{1,5},{5,1},{9,13},{13,9},{2,6},{6,2},{1... | collective-permute-start | bytes 516104 | tf_op jit(solution)/shard_map/ppermute | solution.py:36
  221.9 21.2 %collective-permute-start.67 = (bf16[2,96,768]{2,1,0:T(8,128)(2,1)S(1)}, bf16[2,96,768]{2,1,0:T(8,128)(2,1)S(1)}, u32[]{:S(2)}, u32[]{:S(2)}) collective-permute-start(bf16[2,96,768]{2,1,0:T(8,128)(2,1)S(1)} %pad_maximum_fusion.2.pair), channel_id=1, source_target_pairs={{0,4},{4,0},{8,12},{12,8},{1,5},{5,1},{9,13},{13,9},{2,6},{6,2},{1... | collective-permute-start | bytes 884744 | tf_op jit(solution)/shard_map/ppermute | solution.py:36
  222.0 16.9 %collective-permute-start.61 = (bf16[2,112,576]{2,1,0:T(8,128)(2,1)S(1)}, bf16[2,112,576]{2,1,0:T(8,128)(2,1)S(1)}, u32[]{:S(2)}, u32[]{:S(2)}) collective-permute-start(bf16[2,112,576]{2,1,0:T(8,128)(2,1)S(1)} %pad_maximum_fusion.4.pair), channel_id=1, source_target_pairs={{0,8},{4,12},{8,0},{12,4},{1,9},{5,13},{9,1},{13,5},{2,10},{6,14},... | collective-permute-start | bytes 774152 | tf_op jit(solution)/shard_map/ppermute | solution.py:36
  225.0 23.1 %collective-permute-start.65 = (bf16[2,96,768]{2,1,0:T(8,128)(2,1)S(1)}, bf16[2,96,768]{2,1,0:T(8,128)(2,1)S(1)}, u32[]{:S(2)}, u32[]{:S(2)}) collective-permute-start(bf16[2,96,768]{2,1,0:T(8,128)(2,1)S(1)} %pad_maximum_fusion.1.pair), channel_id=1, source_target_pairs={{0,4},{4,0},{8,12},{12,8},{1,5},{5,1},{9,13},{13,9},{2,6},{6,2},{1... | collective-permute-start | bytes 884744 | tf_op jit(solution)/shard_map/ppermute | solution.py:36
  232.3 13.7 %collective-permute-start.63 = (bf16[112,768]{1,0:T(8,128)(2,1)S(1)}, bf16[112,768]{1,0:T(8,128)(2,1)S(1)}, u32[]{:S(2)}, u32[]{:S(2)}) collective-permute-start(bf16[112,768]{1,0:T(8,128)(2,1)S(1)} %add_convert_fusion.8), channel_id=1, source_target_pairs={{0,8},{4,12},{8,0},{12,4},{1,9},{5,13},{9,1},{13,5},{2,10},{6,14},... | collective-permute-start | bytes 516104 | tf_op jit(solution)/shard_map/ppermute | solution.py:36
  (112 other events, 806.0 us)
